TPU v7x, 256 devices: a whole 4x4x8 slice. The times are simulated.
256 devices in a mesh: rows: 16 (over z_hi, y, core), cols: 16 (over z_lo, x).
Axes of the slice: x: 4, y: 4, z: 8 (z_hi: 2, z_lo: 4; z = z_hi * 4 + z_lo), core: 2. Of those that a mesh axis runs over, the one named last changes fastest.
Arguments:
- single: bfloat16 [2048, 1024], P('rows'), may hold values from -6 to 6
- pair: bfloat16 [2048, 2048, 128], P('rows', 'cols'), may hold values from -6 to 6
- residue_mask: int32 [2048], replicated, may hold values from 0 to 1, as said below
- w_bias: bfloat16 [128, 32], replicated, may hold values from -40 to 40
- w_project: bfloat16 [4, 1024, 1024], P(None, None, 'cols'), may hold values from -0.1875 to 0.1875
- w_out: bfloat16 [1024, 1024], replicated, may hold values from -0.1875 to 0.1875
- w_factors: bfloat16 [1024, 128], replicated, may hold values from -0.1875 to 0.1875
- w_pairout: bfloat16 [128, 128], replicated, may hold values from -0.5 to 0.5
- w_up: bfloat16 [128, 512], replicated, may hold values from -0.5 to 0.5
- w_down: bfloat16 [512, 128], replicated, may hold values from -0.25 to 0.25
Outputs:
- single_out: bfloat16 [2048, 1024], P('rows')
- pair_out: bfloat16 [2048, 2048, 128], P('rows', 'cols')
Inputs may be any that keep to these rules, and one draw needn't show every extreme that they name: residue_mask is 1 on a leading run of at least 1024 positions and 0 after it.
All inputs are finite; a program needn't handle non-finite values.
Results may differ from a plain program's by a relative error of at most 0.01.
The roundings to bfloat16 on the way count: a program that leaves them out, or rounds other values in their place, can miss the bound.
Values may be sent and summed in bfloat16 or wider, within the bound.
No kernel may reach another device: no remote copies, remote signals or barrier semaphores. Data moves between devices by JAX's collectives and lax.ppermute only.
A program may use at most 64 MiB of HBM per device.

v0:
```python
import math

import jax
import jax.numpy as jnp
from jax import lax
from jax.sharding import PartitionSpec as P

epsilon = 1e-05


def sent_together(arrays, axis, dim, along):
    both = jnp.concatenate(arrays, axis=along)
    filled, at, finished = (lax.all_gather(both, axis, axis=dim, tiled=True), 0, [])
    for a in arrays:
        finished.append(lax.slice_in_dim(filled, at, at + a.shape[along], axis=along))
        at += a.shape[along]
    return tuple(finished)


def copy_for_each(value, axis):
    count = lax.axis_size(axis)
    return lax.all_to_all(
        jnp.broadcast_to(value[None], (count, *value.shape)), axis, 0, 0, tiled=True
    )


def joined_along(pieces, dim):
    lengths = list(pieces.shape[1:])
    lengths[dim] *= pieces.shape[0]
    return jnp.moveaxis(pieces, 0, dim).reshape(lengths)


def gather_directly(value, axis, dim):
    pieces = copy_for_each(value, axis)
    return joined_along(pieces, dim)


def broadcast(value, axis, root):
    return lax.dynamic_index_in_dim(lax.all_gather(value, axis), root, 0, keepdims=False)


def layer_norm(values):
    values = values.astype(jnp.float32)
    centred = values - jnp.mean(values, -1, keepdims=True)
    return centred * lax.rsqrt(jnp.mean(centred * centred, -1, keepdims=True) + epsilon)


def per_device(
    single, pair, residue_mask, w_bias, w_project, w_out, w_factors, w_pairout, w_up, w_down
):
    tile_rows = pair.shape[0]
    tile_cols = pair.shape[1]
    normed_pair = layer_norm(pair).astype(jnp.bfloat16)
    bias_local = jnp.einsum(
        "rcp,ph->hrc", normed_pair, w_bias, preferred_element_type=jnp.float32
    ).astype(jnp.bfloat16)
    normed_single = layer_norm(single).astype(jnp.bfloat16)
    projected = jnp.einsum(
        "rs,fsc->frc", normed_single, w_project, preferred_element_type=jnp.float32
    )
    query_rows = projected[0].astype(jnp.bfloat16)
    key_local = projected[1].astype(jnp.bfloat16)
    value_local = projected[2].astype(jnp.bfloat16)
    gate_values = jax.nn.sigmoid(projected[3])
    first_residue = lax.axis_index("cols") * tile_cols
    owner_row = first_residue // tile_rows
    bias_heads = lax.all_to_all(bias_local, "cols", split_axis=0, concat_axis=2, tiled=True)
    key_rows, value_rows = sent_together((key_local, value_local), "rows", 0, 1)
    heads_here = bias_heads.shape[0]
    head_width = query_rows.shape[1] // heads_here
    residues = key_rows.shape[0]
    query_split = query_rows.reshape(tile_rows, heads_here, head_width)
    key_split = key_rows.reshape(residues, heads_here, head_width)
    value_split = value_rows.reshape(residues, heads_here, head_width)
    score_scale = 1.0 / math.sqrt(head_width)
    scores = jnp.einsum(
        "rhd,lhd->hrl", query_split, key_split, preferred_element_type=jnp.float32
    ) * score_scale + bias_heads.astype(jnp.float32)
    key_valid = (residue_mask > 0)[None, None, :]
    scores = jnp.where(key_valid, scores, -jnp.inf)
    weights = jax.nn.softmax(scores, axis=-1).astype(jnp.bfloat16)
    attended = jnp.einsum("hrl,lhd->rhd", weights, value_split, preferred_element_type=jnp.float32)
    attended = attended.reshape(tile_rows, heads_here * head_width)
    mixed = (attended * gate_values).astype(jnp.bfloat16)
    whole_heads = gather_directly(mixed, "cols", 1)
    head_total = jnp.dot(whole_heads, w_out, preferred_element_type=jnp.float32)
    single_out = (single.astype(jnp.float32) + head_total).astype(jnp.bfloat16)
    normed_out = layer_norm(single_out).astype(jnp.bfloat16)
    factors = jnp.dot(normed_out, w_factors, preferred_element_type=jnp.float32).astype(
        jnp.bfloat16
    )
    factor_width = factors.shape[1] // 2
    left_factor = factors[:, :factor_width]
    right_local = factors[:, factor_width:]
    right_cols = broadcast(right_local, "rows", owner_row)
    block_rows = math.gcd(tile_rows, max(1, 4096 // tile_cols))
    count_blocks = tile_rows // block_rows

    def update_block(operands):
        pair_block, left_block = operands
        left_wide = left_block.astype(jnp.float32)[:, None, :]
        right_wide = right_cols.astype(jnp.float32)[None, :, :]
        paired = jnp.concatenate([left_wide * right_wide, left_wide - right_wide], -1).astype(
            jnp.bfloat16
        )
        pair_mid = (
            pair_block.astype(jnp.float32)
            + jnp.einsum("rcq,qp->rcp", paired, w_pairout, preferred_element_type=jnp.float32)
        ).astype(jnp.bfloat16)
        normed_mid = layer_norm(pair_mid).astype(jnp.bfloat16)
        hidden = jax.nn.relu(
            jnp.einsum("rcp,pk->rck", normed_mid, w_up, preferred_element_type=jnp.float32)
        ).astype(jnp.bfloat16)
        return (
            pair_mid.astype(jnp.float32)
            + jnp.einsum("rck,kp->rcp", hidden, w_down, preferred_element_type=jnp.float32)
        ).astype(jnp.bfloat16)

    updated = lax.map(
        update_block,
        (
            pair.reshape(count_blocks, block_rows, tile_cols, pair.shape[2]),
            left_factor.reshape(count_blocks, block_rows, factor_width),
        ),
    )
    return (single_out, updated.reshape(pair.shape))


def solution(mesh):
    return jax.shard_map(
        per_device,
        mesh=mesh,
        in_specs=(
            P("rows", None),
            P("rows", "cols", None),
            P(),
            P(),
            P(None, None, "cols"),
            P(),
            P(),
            P(),
            P(),
            P(),
        ),
        out_specs=(P("rows", None), P("rows", "cols", None)),
        check_vma=False,
    )
```

profile of v0, /device:TPU:1, one launch (start us, length us, event | category | flops | bytes accessed | tf_op | source)
XLA Modules:
  0.0 169.1 jit_solution(11591808565831232262)
XLA Ops:
  0.6 0.0 copy-start
  0.6 0.0 copy-start.1
  0.7 3.5 %convert_reduce_fusion.1 = f32[128,128]{1,0:T(8,128)S(1)} fusion(bf16[128,128,128]{2,1,0:T(8,128)(2,1)} %param.13), kind=kLoop, calls=%fused_computation.33 | loop fusion | flops 4177920 | bytes 4259840 | tf_op jit(solution)/shard_map/reduce_sum | solution.py:44
  4.2 0.0 copy-done.1
  4.2 4.8 %fusion.29 = f32[128,128]{1,0:T(8,128)S(1)} fusion(bf16[128,128,128]{2,1,0:T(8,128)(2,1)S(1)} %copy-done.1, f32[128,128]{1,0:T(8,128)S(1)} %broadcast_multiply_fusion.1), kind=kLoop, calls=%fused_computation.36 | loop fusion | flops 8372224 | bytes 4325376 | tf_op jit(solution)/shard_map/reduce_sum | solution.py:45
  9.0 6.0 %fusion.42 = bf16[32,128,128]{2,0,1:T(8,128)(2,1)S(1)} fusion(bf16[128,128,128]{2,1,0:T(8,128)(2,1)S(1)} %copy-done.1, f32[128,128]{1,0:T(8,128)S(1)} %add_rsqrt_fusion.1, f32[128,128]{1,0:T(8,128)S(1)} %broadcast_multiply_fusion.1, bf16[128,32]{0,1:T(8,128)(2,1)S(1)} %copy-done.11), kind=kOutput, calls=%fused_computation.49 | convolution fusion | flops 143130624 | bytes 5382144 | tf_op jit(solution)/shard_map/rcp,ph->hrc/dot_general | solution.py:54
  15.0 0.0 copy-start.3
  15.0 1.4 copy.29
  16.4 9.0 %all-to-all-start = ((bf16[32,128,128]{2,1,0:T(8,128)(2,1)}), bf16[32,128,128]{2,1,0:T(8,128)(2,1)S(1)}, u32[]{:S(2)}, u32[]{:S(2)}) async-start(bf16[32,128,128]{2,1,0:T(8,128)(2,1)} %copy.29), calls=%async_computation | async-start | bytes 2097152 | tf_op jit(solution)/shard_map/all_to_all | solution.py:67
  25.4 0.1 convert_reduce_fusion.2
  25.6 0.2 fusion.51
  25.8 1.4 fusion.56
  27.3 1.3 broadcast_compare_fusion
  28.6 39.4 %all_gather.9 = bf16[2048,128]{0,1:T(8,128)(2,1)S(1)} all-gather(bf16[128,128]{0,1:T(8,128)(2,1)S(1)} %pad_maximum_fusion), channel_id=1, replica_groups=mesh['rows'=16,'cols'=16] {'rows'}, dimensions={0}, use_global_device_ids=true | all-gather | bytes 557056 | tf_op jit(solution)/shard_map/all_gather | solution.py:13
  68.0 0.8 fusion.69
  68.8 1.9 %copy.42 = f32[16,2,128,128]{3,0,2,1:T(8,128)} copy(bf16[16,2,128,128]{3,2,1,0:T(8,128)(2,1)S(1)} %bitcast.84) | data formatting | bytes 3145728 | tf_op jit(solution)/shard_map/convert_element_type | solution.py:78
  70.8 2.8 %reshape.107 = f32[2,128,2048]{2,1,0:T(8,128)} reshape(f32[2,128,16,128]{3,2,1,0:T(8,128)} %bitcast.83) | data formatting | bytes 4194304 | tf_op jit(solution)/shard_map/convert_element_type | solution.py:78
  73.5 2.1 %fusion.38 = f32[2,128,2048]{2,1,0:T(8,128)S(1)} fusion(f32[2,128,2048]{2,1,0:T(8,128)} %reshape.107, bf16[128,2,32]{0,2,1:T(8,128)(2,1)S(1)} %bitcast.94, bf16[2048,2,32]{0,2,1:T(8,128)(2,1)S(1)} %bitcast.87, pred[2048]{0:T(1024)(128)(4,1)S(1)} %copy-done.8), kind=kOutput, calls=%fused_computation.45 | convolution fusion | flops 35127296 | bytes 4474880 | tf_op jit(solution)/shard_map/rhd,lhd->hrl/dot_general | solution.py:76
  75.6 0.0 copy-start.2
  75.6 1.3 copy-done.2
  77.0 0.5 fusion.72
  77.4 0.5 copy-done.6
  77.9 3.0 %fusion.46 = f32[2,32,128]{2,1,0:T(8,128)S(1)} fusion(bf16[2048,2,32]{0,2,1:T(8,128)(2,1)S(1)} %bitcast.90, f32[2,128]{1,0:T(2,128)S(1)} %fusion.72, f32[2,128,2048]{2,1,0:T(8,128)} %copy-done.2), kind=kOutput, calls=%fused_computation.53 | convolution fusion | flops 35129600 | bytes 2393088 | tf_op jit(solution)/shard_map/hrl,lhd->rhd/dot_general | solution.py:82
  80.9 0.8 broadcast_in_dim.24
  81.7 7.3 %all-to-all-start.1 = ((bf16[16,128,64]{1,2,0:T(8,128)(2,1)}), bf16[16,128,64]{1,2,0:T(8,128)(2,1)S(1)}, u32[]{:S(2)}, u32[]{:S(2)}) async-start(bf16[16,128,64]{1,2,0:T(8,128)(2,1)} %broadcast_in_dim.24), calls=%async_computation.1 | async-start | bytes 524288 | tf_op jit(solution)/shard_map/all_to_all | solution.py:22
  89.0 0.0 copy-start.7
  89.0 6.4 %copy.31 = bf16[128,128,128]{1,2,0:T(8,128)(2,1)} copy(bf16[128,128,128]{2,1,0:T(8,128)(2,1)} %param.13) | data formatting | bytes 8388608 | tf_op args[1]
  95.4 0.1 copy.34
  95.5 3.5 %all-to-all-done.1 = bf16[16,128,64]{1,2,0:T(8,128)(2,1)S(1)} async-done(((bf16[16,128,64]{1,2,0:T(8,128)(2,1)}), bf16[16,128,64]{1,2,0:T(8,128)(2,1)S(1)}, u32[]{:S(2)}, u32[]{:S(2)}) %all-to-all-start.1) | async-done | bytes 262176 | tf_op jit(solution)/shard_map/all_to_all | solution.py:22
  99.0 0.5 convert_reduce_fusion.3
  99.6 0.2 fusion.53
  99.8 0.3 convolution_convert_fusion
  100.2 27.8 %all-gather = bf16[2048,64]{0,1:T(8,128)(2,1)S(1)} all-gather(bf16[128,64]{0,1:T(8,128)(2,1)S(1)} %get-tuple-element.94), channel_id=2, replica_groups=mesh['rows'=16,'cols'=16] {'rows'}, dimensions={0}, use_global_device_ids=true | all-gather | bytes 278528 | tf_op jit(solution)/shard_map/all_gather | solution.py:39
  128.1 0.1 copy.33
  128.2 0.1 copy.32
  128.3 40.7 %while.10 = (s32[]{:T(128)}, bf16[4,32,128,128]{3,2,1,0:T(8,128)(2,1)}, bf16[4,32,128,128]{2,3,1,0:T(8,128)(2,1)}, bf16[4,32,64]{2,1,0:T(8,128)(2,1)S(1)}, bf16[...) while((s32[]{:T(128)}, ...), condition=%wide.region_11.12_spmd, body=%wide.region_8.11_spmd.sunk | while | flops 1223702528 | bytes 12604033 | solution.py:119
  128.4 0.5 multiply_convert_fusion.2
  128.9 0.0 copy-start.10
  128.9 2.1 %convert_reduce_fusion.5 = (f32[32,128]{1,0:T(8,128)S(1)}, bf16[32,128,128]{1,2,0:T(8,128)(2,1)S(1)}) fusion(bf16[128,128]{0,1:T(8,128)(2,1)S(1)} %get-tuple-element.178, bf16[32,128,64]{2,1,0:T(8,128)(2,1)S(1)} %get-tuple-element.151, bf16[32,128,64]{2,1,0:T(8,128)(2,1)S(1)} %get-tuple-element.152, ...), kind=kOutput, calls=%fused_computation.6.clone.1 | convolution fusion | flops 138932224 | bytes 3194884 | tf_op jit(solution)/shard_map/while/body/eval_jaxpr/rcq,qp->rcp/dot_general | solution.py:108
  131.1 0.3 fusion.90
  131.4 4.5 %fusion.91 = bf16[1,32,128,128]{2,3,1,0:T(8,128)(2,1)} fusion(bf16[32,128,128]{1,2,0:T(8,128)(2,1)S(1)} %get-tuple-element.153, f32[32,128]{1,0:T(8,128)S(1)} %add_rsqrt_fusion.5, f32[32,128]{1,0:T(8,128)S(1)} %broadcast_multiply_fusion.5, bf16[512,128]{1,0:T(8,128)(2,1)} %get-tuple-element.180, bf16[128,512]{1,0:T(8,128)(2,1)S(1)} %copy-done.10), kind=kOutput, calls=%fused_computation.16.clone.1 | convolution fusion | flops 1081606144 | bytes 2392064 | tf_op jit(solution)/shard_map/while/body/eval_jaxpr/rck,kp->rcp/dot_general | solution.py:116
  135.9 1.6 copy.44
  137.5 1.0 constant_dynamic-update-slice_fusion.2
  138.6 0.5 multiply_convert_fusion.2
  139.1 0.0 copy-start.10
  139.1 2.1 %convert_reduce_fusion.5 = (f32[32,128]{1,0:T(8,128)S(1)}, bf16[32,128,128]{1,2,0:T(8,128)(2,1)S(1)}) fusion(bf16[128,128]{0,1:T(8,128)(2,1)S(1)} %get-tuple-element.178, bf16[32,128,64]{2,1,0:T(8,128)(2,1)S(1)} %get-tuple-element.151, bf16[32,128,64]{2,1,0:T(8,128)(2,1)S(1)} %get-tuple-element.152, ...), kind=kOutput, calls=%fused_computation.6.clone.1 | convolution fusion | flops 138932224 | bytes 3194884 | tf_op jit(solution)/shard_map/while/body/eval_jaxpr/rcq,qp->rcp/dot_general | solution.py:108
  141.2 0.3 fusion.90
  141.6 4.4 %fusion.91 = bf16[1,32,128,128]{2,3,1,0:T(8,128)(2,1)} fusion(bf16[32,128,128]{1,2,0:T(8,128)(2,1)S(1)} %get-tuple-element.153, f32[32,128]{1,0:T(8,128)S(1)} %add_rsqrt_fusion.5, f32[32,128]{1,0:T(8,128)S(1)} %broadcast_multiply_fusion.5, bf16[512,128]{1,0:T(8,128)(2,1)} %get-tuple-element.180, bf16[128,512]{1,0:T(8,128)(2,1)S(1)} %copy-done.10), kind=kOutput, calls=%fused_computation.16.clone.1 | convolution fusion | flops 1081606144 | bytes 2392064 | tf_op jit(solution)/shard_map/while/body/eval_jaxpr/rck,kp->rcp/dot_general | solution.py:116
  146.1 1.6 copy.44
  147.7 1.0 constant_dynamic-update-slice_fusion.2
  148.7 0.5 multiply_convert_fusion.2
  149.3 0.0 copy-start.10
  149.3 2.1 %convert_reduce_fusion.5 = (f32[32,128]{1,0:T(8,128)S(1)}, bf16[32,128,128]{1,2,0:T(8,128)(2,1)S(1)}) fusion(bf16[128,128]{0,1:T(8,128)(2,1)S(1)} %get-tuple-element.178, bf16[32,128,64]{2,1,0:T(8,128)(2,1)S(1)} %get-tuple-element.151, bf16[32,128,64]{2,1,0:T(8,128)(2,1)S(1)} %get-tuple-element.152, ...), kind=kOutput, calls=%fused_computation.6.clone.1 | convolution fusion | flops 138932224 | bytes 3194884 | tf_op jit(solution)/shard_map/while/body/eval_jaxpr/rcq,qp->rcp/dot_general | solution.py:108
  151.4 0.3 fusion.90
  151.8 4.4 %fusion.91 = bf16[1,32,128,128]{2,3,1,0:T(8,128)(2,1)} fusion(bf16[32,128,128]{1,2,0:T(8,128)(2,1)S(1)} %get-tuple-element.153, f32[32,128]{1,0:T(8,128)S(1)} %add_rsqrt_fusion.5, f32[32,128]{1,0:T(8,128)S(1)} %broadcast_multiply_fusion.5, bf16[512,128]{1,0:T(8,128)(2,1)} %get-tuple-element.180, bf16[128,512]{1,0:T(8,128)(2,1)S(1)} %copy-done.10), kind=kOutput, calls=%fused_computation.16.clone.1 | convolution fusion | flops 1081606144 | bytes 2392064 | tf_op jit(solution)/shard_map/while/body/eval_jaxpr/rck,kp->rcp/dot_general | solution.py:116
  156.2 1.6 copy.44
  157.8 1.0 constant_dynamic-update-slice_fusion.2
  158.9 0.5 multiply_convert_fusion.2
  159.4 0.0 copy-start.10
  159.4 2.1 %convert_reduce_fusion.5 = (f32[32,128]{1,0:T(8,128)S(1)}, bf16[32,128,128]{1,2,0:T(8,128)(2,1)S(1)}) fusion(bf16[128,128]{0,1:T(8,128)(2,1)S(1)} %get-tuple-element.178, bf16[32,128,64]{2,1,0:T(8,128)(2,1)S(1)} %get-tuple-element.151, bf16[32,128,64]{2,1,0:T(8,128)(2,1)S(1)} %get-tuple-element.152, ...), kind=kOutput, calls=%fused_computation.6.clone.1 | convolution fusion | flops 138932224 | bytes 3194884 | tf_op jit(solution)/shard_map/while/body/eval_jaxpr/rcq,qp->rcp/dot_general | solution.py:108
  161.6 0.3 fusion.90
  162.0 4.4 %fusion.91 = bf16[1,32,128,128]{2,3,1,0:T(8,128)(2,1)} fusion(bf16[32,128,128]{1,2,0:T(8,128)(2,1)S(1)} %get-tuple-element.153, f32[32,128]{1,0:T(8,128)S(1)} %add_rsqrt_fusion.5, f32[32,128]{1,0:T(8,128)S(1)} %broadcast_multiply_fusion.5, bf16[512,128]{1,0:T(8,128)(2,1)} %get-tuple-element.180, bf16[128,512]{1,0:T(8,128)(2,1)S(1)} %copy-done.10), kind=kOutput, calls=%fused_computation.16.clone.1 | convolution fusion | flops 1081606144 | bytes 2392064 | tf_op jit(solution)/shard_map/while/body/eval_jaxpr/rck,kp->rcp/dot_general | solution.py:116
  166.4 1.6 copy.44
  168.0 1.0 constant_dynamic-update-slice_fusion.2
  (49 shorter events, 0.3 us)
Async XLA Ops:
  0.6 98.4 %copy-start = (bf16[1024,1024]{1,0:T(8,128)(2,1)S(1)}, bf16[1024,1024]{1,0:T(8,128)(2,1)}, u32[]{:S(2)}) copy-start(bf16[1024,1024]{1,0:T(8,128)(2,1)} %param.17) | copy-start | bytes 6291460
  0.6 3.6 %copy-start.1 = (bf16[128,128,128]{2,1,0:T(8,128)(2,1)S(1)}, bf16[128,128,128]{2,1,0:T(8,128)(2,1)}, u32[]{:S(2)}) copy-start(bf16[128,128,128]{2,1,0:T(8,128)(2,1)} %param.13) | copy-start | bytes 12582916
  4.2 4.8 %copy-start.11 = (bf16[128,32]{0,1:T(8,128)(2,1)S(1)}, bf16[128,32]{0,1:T(8,128)(2,1)}, u32[]{:S(2)}) copy-start(bf16[128,32]{0,1:T(8,128)(2,1)} %param.15) | copy-start | bytes 24580
  15.0 10.4 %copy-start.3 = (bf16[128,1024]{1,0:T(8,128)(2,1)S(1)}, bf16[128,1024]{1,0:T(8,128)(2,1)}, u32[]{:S(2)}) copy-start(bf16[128,1024]{1,0:T(8,128)(2,1)} %param.12) | copy-start | bytes 786436
  16.4 52.4 %all-to-all-start = ((bf16[32,128,128]{2,1,0:T(8,128)(2,1)}), bf16[32,128,128]{2,1,0:T(8,128)(2,1)S(1)}, u32[]{:S(2)}, u32[]{:S(2)}) async-start(bf16[32,128,128]{2,1,0:T(8,128)(2,1)} %copy.29), calls=%async_computation | async-start | bytes 2097152 | tf_op jit(solution)/shard_map/all_to_all | solution.py:67
  70.8 2.8 %copy-start.5 = (bf16[2048,64]{0,1:T(8,128)(2,1)S(1)}, bf16[2048,64]{0,1:T(8,128)(2,1)}, u32[]{:S(2)}) copy-start(bf16[2048,64]{0,1:T(8,128)(2,1)} %get-tuple-element.89) | copy-start | bytes 786436
  70.8 2.8 %copy-start.8 = (pred[2048]{0:T(1024)(128)(4,1)S(1)}, pred[2048]{0:T(1024)(128)(4,1)}, u32[]{:S(2)}) copy-start(pred[2048]{0:T(1024)(128)(4,1)} %broadcast_compare_fusion) | copy-start | bytes 6148
  75.6 1.3 copy-start.2
  76.9 0.9 copy-start.6
  81.7 17.4 %all-to-all-start.1 = ((bf16[16,128,64]{1,2,0:T(8,128)(2,1)}), bf16[16,128,64]{1,2,0:T(8,128)(2,1)S(1)}, u32[]{:S(2)}, u32[]{:S(2)}) async-start(bf16[16,128,64]{1,2,0:T(8,128)(2,1)} %broadcast_in_dim.24), calls=%async_computation.1 | async-start | bytes 524288 | tf_op jit(solution)/shard_map/all_to_all | solution.py:22
  89.0 6.4 %copy-start.7 = (bf16[128,128]{1,0:T(8,128)(2,1)S(1)}, bf16[128,128]{1,0:T(8,128)(2,1)}, u32[]{:S(2)}) copy-start(bf16[128,128]{1,0:T(8,128)(2,1)} %param.19) | copy-start | bytes 98308
  95.4 4.5 %copy-start.9 = (bf16[1024,128]{1,0:T(8,128)(2,1)S(1)}, bf16[1024,128]{1,0:T(8,128)(2,1)}, u32[]{:S(2)}) copy-start(bf16[1024,128]{1,0:T(8,128)(2,1)} %param.18) | copy-start | bytes 786436
  99.6 28.4 %copy-start.4 = (bf16[128,1024]{1,0:T(8,128)(2,1)}, bf16[128,1024]{1,0:T(8,128)(2,1)S(1)}, u32[]{:S(2)}) copy-start(bf16[128,1024]{1,0:T(8,128)(2,1)S(1)} %get-tuple-element.97) | copy-start | bytes 786436
  128.9 2.5 %copy-start.10 = (bf16[128,512]{1,0:T(8,128)(2,1)S(1)}, bf16[128,512]{1,0:T(8,128)(2,1)}, u32[]{:S(2)}) copy-start(bf16[128,512]{1,0:T(8,128)(2,1)} %get-tuple-element.179) | copy-start | bytes 393220 | tf_op jit(solution)/shard_map/while
  139.1 2.5 %copy-start.10 = (bf16[128,512]{1,0:T(8,128)(2,1)S(1)}, bf16[128,512]{1,0:T(8,128)(2,1)}, u32[]{:S(2)}) copy-start(bf16[128,512]{1,0:T(8,128)(2,1)} %get-tuple-element.179) | copy-start | bytes 393220 | tf_op jit(solution)/shard_map/while
  149.3 2.5 %copy-start.10 = (bf16[128,512]{1,0:T(8,128)(2,1)S(1)}, bf16[128,512]{1,0:T(8,128)(2,1)}, u32[]{:S(2)}) copy-start(bf16[128,512]{1,0:T(8,128)(2,1)} %get-tuple-element.179) | copy-start | bytes 393220 | tf_op jit(solution)/shard_map/while
  159.4 2.5 %copy-start.10 = (bf16[128,512]{1,0:T(8,128)(2,1)S(1)}, bf16[128,512]{1,0:T(8,128)(2,1)}, u32[]{:S(2)}) copy-start(bf16[128,512]{1,0:T(8,128)(2,1)} %get-tuple-element.179) | copy-start | bytes 393220 | tf_op jit(solution)/shard_map/while
where the time goes:
time: 170 us; the launch traced here: 169 us
  blocking collectives  67.2 us (40%)
  matrix products  39.6 us (23%)
  local copies, waits for them, and re-layouts  27.1 us (16%)
  starting transfers between devices  16.3 us (10%)
  other arithmetic  14.2 us (8%)
  waiting for transfers between devices  3.54 us (2%)
    all_gather x1, blocking collectives, sent_together(): lax.all_gather(both, axis, axis=dim, tiled=True)  39.4 us
    all_gather x1, blocking collectives, broadcast(): lax.all_gather(value, axis)  27.8 us
    dot_general x4, matrix products, update_block(): jnp.einsum('rck,kp->rcp', hidden, w_down, preferred_element_type=jnp.floa...  17.8 us
    dynamic_update_slice x8, local copies, waits for them, and re-layouts, per_device(): lax.map(update_block, (pair.reshape(count_blocks, block_rows, tile_cols,...  10.6 us
    all_to_all x1, starting transfers between devices, per_device(): lax.all_to_all(bias_local, 'cols', split_axis=0, concat_axis=2, tiled=True)  9.01 us
    dot_general x4, matrix products, update_block(): jnp.einsum('rcq,qp->rcp', paired, w_pairout, preferred_element_type=jnp.f...  8.52 us
    unnamed x24, local copies, waits for them, and re-layouts  8.33 us
    all_to_all x1, starting transfers between devices, copy_for_each(): lax.all_to_all(jnp.broadcast_to(value[None], (count, *value.shape)), axis...  7.29 us
  transfers between devices with their start and end apart: 2, of which 1 were waited for; matrix products, arithmetic and copies ran while one was open for 6% of the time, Pallas kernels for 0%

commit v1 on v0

v1 whole, which is shorter than its diff:
```python
import functools
import math

import jax
import jax.numpy as jnp
from jax import lax
from jax.experimental import pallas as pl
from jax.experimental.pallas import tpu as pltpu
from jax.sharding import PartitionSpec as P

epsilon = 1e-05
f32 = jnp.float32
bf16 = jnp.bfloat16
lowest = -1e30


def normalize(values):
    centred = values - jnp.mean(values, -1, keepdims=True)
    return centred * lax.rsqrt(jnp.mean(centred * centred, -1, keepdims=True) + epsilon)


def nt_dot(a, b):
    return lax.dot_general(a, b, (((1,), (1,)), ((), ())), preferred_element_type=f32)


def project_kernel(single_ref, weight_ref, query_ref, kv_ref, gate_ref):
    normed = normalize(single_ref[...].astype(f32)).astype(bf16)
    projected = nt_dot(weight_ref[...], normed)
    width = query_ref.shape[0]
    query_ref[...] = projected[:width].astype(bf16)
    kv_ref[...] = projected[width : 3 * width].astype(bf16)
    gate_ref[...] = jax.nn.sigmoid(projected[3 * width :])


def bias_kernel(pair_ref, weight_ref, out_ref, held_ref):
    block_rows, tile_cols, width = pair_ref.shape
    weight = weight_ref[...]
    for i in range(0, block_rows, 2):
        values = pair_ref[i : i + 2].astype(f32).reshape(2 * tile_cols, width)
        both = nt_dot(weight, normalize(values).astype(bf16))
        held_ref[:, i, :] = both[:, :tile_cols]
        held_ref[:, i + 1, :] = both[:, tile_cols:]
    out_ref[...] = held_ref[...].astype(bf16)


def attend_kernel(swap_ref, query_ref, gate_ref, bias_ref, kv_ref, mask_ref, out_ref, score_ref):
    blocks, heads_here, tile_rows, tile_cols = bias_ref.shape
    width = query_ref.shape[0]
    head_width = width // heads_here
    score_scale = 1.0 / math.sqrt(head_width)
    half = kv_ref.shape[0]
    swap = swap_ref[0]
    query = jnp.transpose(query_ref[...].astype(f32)).astype(bf16)
    attended = []
    for h in range(heads_here):
        query_head = query[:, h * head_width : (h + 1) * head_width]
        key_rows = pl.ds(h * head_width, head_width)
        value_rows = pl.ds(width + h * head_width, head_width)
        top = None
        for b in range(blocks):
            key = kv_ref[b % half, (b // half) ^ swap, key_rows, :]
            scores = jnp.dot(query_head, key, preferred_element_type=f32) * score_scale
            scores = scores + bias_ref[b, h].astype(f32)
            scores = jnp.where(mask_ref[b : b + 1, :] > 0, scores, lowest)
            score_ref[b] = scores
            top = scores if top is None else jnp.maximum(top, scores)
        top = jnp.max(top, axis=-1, keepdims=True)
        total = mixed = None
        for b in range(blocks):
            value = kv_ref[b % half, (b // half) ^ swap, value_rows, :]
            weights = jnp.exp(score_ref[b] - top)
            part = nt_dot(weights.astype(bf16), value)
            total = weights if total is None else total + weights
            mixed = part if mixed is None else mixed + part
        attended.append(mixed / jnp.sum(total, axis=-1, keepdims=True))
    mixed = jnp.transpose(jnp.concatenate(attended, axis=1)) * gate_ref[...]
    mixed = mixed.astype(bf16)
    for d in range(out_ref.shape[0]):
        out_ref[d] = mixed


def factor_kernel(mixed_ref, w_out_ref, single_ref, w_factors_ref, out_ref, factors_ref):
    mixed = jnp.transpose(mixed_ref[...].astype(f32)).astype(bf16)
    head_total = jnp.dot(mixed, w_out_ref[...], preferred_element_type=f32)
    single_out = (single_ref[...].astype(f32) + head_total).astype(bf16)
    out_ref[...] = single_out
    normed = normalize(single_out.astype(f32)).astype(bf16)
    factors_ref[...] = jnp.dot(normed, w_factors_ref[...], preferred_element_type=f32).astype(bf16)


def update_kernel(pair_ref, left_ref, right_ref, w_pairout_ref, w_up_ref, w_down_ref, out_ref):
    block_rows, tile_cols, width = pair_ref.shape
    factor_width = width // 2
    right = right_ref[:, factor_width:].astype(f32)
    right = jnp.concatenate([right, right], axis=1)
    lane = lax.broadcasted_iota(jnp.int32, (1, width), 1)
    for i in range(block_rows):
        left = left_ref[i : i + 1, :factor_width].astype(f32)
        left = jnp.concatenate([left, left], axis=1)
        scale = jnp.where(lane < factor_width, left, -1.0)
        shift = jnp.where(lane < factor_width, 0.0, left)
        paired = (right * scale + shift).astype(bf16)
        moved = jnp.dot(paired, w_pairout_ref[...], preferred_element_type=f32)
        pair_mid = (pair_ref[i].astype(f32) + moved).astype(bf16).astype(f32)
        normed = normalize(pair_mid).astype(bf16)
        hidden = jnp.dot(normed, w_up_ref[...], preferred_element_type=f32)
        hidden = jnp.maximum(hidden, 0.0).astype(bf16)
        down = jnp.dot(hidden, w_down_ref[...], preferred_element_type=f32)
        out_ref[i] = (pair_mid + down).astype(bf16)


def whole(shape):
    return pl.BlockSpec(shape, lambda *_: (0,) * len(shape))


def params():
    return pltpu.CompilerParams(vmem_limit_bytes=16 * 1024 * 1024)


def gather_directly(value, axis, groups=None, count=None):
    count = count or lax.axis_size(axis)
    pieces = jnp.broadcast_to(value[None], (count, *value.shape))
    return lax.all_to_all(pieces, axis, 0, 0, axis_index_groups=groups, tiled=True)


def per_device(
    single, pair, residue_mask, w_bias, w_project, w_out, w_factors, w_pairout, w_up, w_down
):
    tile_rows, tile_cols, pair_width = pair.shape
    single_width = single.shape[1]
    width = w_project.shape[2]
    rows, cols = lax.axis_size("rows"), lax.axis_size("cols")
    heads = w_bias.shape[1]
    heads_here = heads // cols

    weight = jnp.transpose(w_project, (0, 2, 1)).reshape(4 * width, single_width)
    query, kv, gate_values = pl.pallas_call(
        project_kernel,
        out_shape=(
            jax.ShapeDtypeStruct((width, tile_rows), bf16),
            jax.ShapeDtypeStruct((2 * width, tile_rows), bf16),
            jax.ShapeDtypeStruct((width, tile_rows), f32),
        ),
        compiler_params=params(),
        name="project",
    )(single, weight)

    half = rows // 2
    kv_other = lax.ppermute(kv, "rows", [(r, r ^ half) for r in range(rows)])
    groups = [list(range(half)), list(range(half, rows))]
    kv_all = gather_directly(jnp.stack([kv, kv_other]), "rows", groups, half)

    block_rows = 16
    bias_local = pl.pallas_call(
        bias_kernel,
        grid=(tile_rows // block_rows,),
        in_specs=[
            pl.BlockSpec((block_rows, tile_cols, pair_width), lambda i: (i, 0, 0)),
            whole((heads, pair_width)),
        ],
        out_specs=pl.BlockSpec((heads, block_rows, tile_cols), lambda i: (0, i, 0)),
        out_shape=jax.ShapeDtypeStruct((heads, tile_rows, tile_cols), bf16),
        scratch_shapes=[pltpu.VMEM((heads, block_rows, tile_cols), f32)],
        compiler_params=params(),
        name="bias",
    )(pair, jnp.transpose(w_bias))
    bias_heads = lax.all_to_all(bias_local, "cols", 0, 0, tiled=True)

    swap = (lax.axis_index("rows") // half).astype(jnp.int32).reshape(1)
    mixed = pl.pallas_call(
        attend_kernel,
        in_specs=[pl.BlockSpec(memory_space=pltpu.SMEM)] + [pl.BlockSpec(memory_space=pltpu.VMEM)] * 5,
        out_shape=jax.ShapeDtypeStruct((cols, width, tile_rows), bf16),
        scratch_shapes=[pltpu.VMEM((cols, tile_rows, tile_cols), f32)],
        compiler_params=params(),
        name="attend",
    )(
        swap,
        query,
        gate_values,
        bias_heads.reshape(cols, heads_here, tile_rows, tile_cols),
        kv_all,
        residue_mask.reshape(cols, tile_cols),
    )
    mixed_all = lax.all_to_all(mixed, "cols", 0, 0, tiled=True).reshape(single_width, tile_rows)

    single_out, factors = pl.pallas_call(
        factor_kernel,
        out_shape=(
            jax.ShapeDtypeStruct(single.shape, bf16),
            jax.ShapeDtypeStruct((tile_rows, w_factors.shape[1]), bf16),
        ),
        compiler_params=params(),
        name="factor",
    )(mixed_all, w_out, single, w_factors)

    swapped = [(a * cols + b, b * cols + a) for a in range(rows) for b in range(cols)]
    right_factors = lax.ppermute(factors, ("rows", "cols"), swapped)

    block_rows = 16
    updated = pl.pallas_call(
        update_kernel,
        grid=(tile_rows // block_rows,),
        in_specs=[
            pl.BlockSpec((block_rows, tile_cols, pair_width), lambda i: (i, 0, 0)),
            pl.BlockSpec((block_rows, factors.shape[1]), lambda i: (i, 0)),
            whole(right_factors.shape),
            whole(w_pairout.shape),
            whole(w_up.shape),
            whole(w_down.shape),
        ],
        out_specs=pl.BlockSpec((block_rows, tile_cols, pair_width), lambda i: (i, 0, 0)),
        out_shape=jax.ShapeDtypeStruct(pair.shape, bf16),
        compiler_params=params(),
        name="update",
    )(pair, factors, right_factors, w_pairout, w_up, w_down)
    return (single_out, updated)


def solution(mesh):
    return jax.shard_map(
        per_device,
        mesh=mesh,
        in_specs=(
            P("rows", None),
            P("rows", "cols", None),
            P(),
            P(),
            P(None, None, "cols"),
            P(),
            P(),
            P(),
            P(),
            P(),
        ),
        out_specs=(P("rows", None), P("rows", "cols", None)),
        check_vma=False,
    )
```

time: 170 us -> 160 us (0.941)
  the two profiles are of different devices: /device:TPU:1 before, /device:TPU:88 now
where the time goes in v1:
time: 160 us
  Pallas kernels  73.5 us (46%)
  waiting for transfers between devices  34.7 us (22%)
  starting transfers between devices  25.2 us (16%)
  blocking collectives  13 us (8%)
  local copies, waits for them, and re-layouts  12.7 us (8%)
    pallas_call x1, Pallas kernels, per_device(): pl.pallas_call(update_kernel, grid=(tile_rows // block_rows,), in_specs=[...  61.2 us
    all_to_all x1, waiting for transfers between devices, per_device(): bias_heads = lax.all_to_all(bias_local, 'cols', 0, 0, tiled=True)  26.1 us
    all_to_all x1, blocking collectives, per_device(): lax.all_to_all(mixed, 'cols', 0, 0, tiled=True)  13 us
    unnamed x32, local copies, waits for them, and re-layouts  11.8 us
    pallas_call x1, Pallas kernels, per_device(): pl.pallas_call(bias_kernel, grid=(tile_rows // block_rows,), in_specs=[pl...  8.59 us
    all_to_all x1, starting transfers between devices, per_device(): bias_heads = lax.all_to_all(bias_local, 'cols', 0, 0, tiled=True)  7.93 us
    ppermute x1, starting transfers between devices, per_device(): right_factors = lax.ppermute(factors, ('rows', 'cols'), swapped)  7.23 us
    ppermute x1, waiting for transfers between devices, per_device(): right_factors = lax.ppermute(factors, ('rows', 'cols'), swapped)  6.08 us
  transfers between devices with their start and end apart: 4, of which 3 were waited for; matrix products, arithmetic and copies ran while one was open for 0% of the time, Pallas kernels for 5%

profile of v1, /device:TPU:88, one launch (start us, length us, event | category | flops | bytes accessed | tf_op | source)
XLA Modules:
  0.0 159.8 jit_solution(2869984868098267152)
XLA Ops:
  0.6 0.0 copy-start.5
  0.6 0.9 copy-done.5
  1.6 0.0 copy-start.7
  1.6 1.0 copy-done.7
  2.6 0.5 project.1
  3.1 0.0 copy-start.12
  3.2 0.6 copy-done.12
  3.8 5.4 %collective-permute-start = (bf16[128,128]{1,0:T(8,128)(2,1)S(1)}, bf16[128,128]{1,0:T(8,128)(2,1)S(1)}, u32[]{:S(2)}, u32[]{:S(2)}) collective-permute-start(bf16[128,128]{1,0:T(8,128)(2,1)S(1)} %get-tuple-element.9), channel_id=1, source_target_pairs={{0,128},{16,144},{32,160},{48,176},{64,192},{80,208},{96,224},{112... | collective-permute-start | bytes 98312 | tf_op jit(solution)/shard_map/ppermute | solution.py:149
  9.2 2.5 %collective-permute-done = bf16[128,128]{1,0:T(8,128)(2,1)S(1)} collective-permute-done((bf16[128,128]{1,0:T(8,128)(2,1)S(1)}, bf16[128,128]{1,0:T(8,128)(2,1)S(1)}, u32[]{:S(2)}, u32[]{:S(2)}) %collective-permute-start) | collective-permute-done | bytes 32800 | tf_op jit(solution)/shard_map/ppermute | solution.py:149
  11.7 0.9 broadcast_in_dim.2
  12.6 4.7 %all-to-all-start.1 = ((bf16[8,2,128,128]{3,2,1,0:T(8,128)(2,1)}), bf16[8,2,128,128]{3,2,1,0:T(8,128)(2,1)S(1)}, u32[]{:S(2)}, u32[]{:S(2)}) async-start(bf16[8,2,128,128]{3,2,1,0:T(8,128)(2,1)} %broadcast_in_dim.2), calls=%async_computation.1 | async-start | bytes 1048576 | tf_op jit(solution)/shard_map/all_to_all | solution.py:123
  17.3 0.0 copy-start
  17.3 2.2 %copy-done = bf16[128,128,128]{2,1,0:T(8,128)(2,1)S(1)} copy-done((bf16[128,128,128]{2,1,0:T(8,128)(2,1)S(1)}, bf16[128,128,128]{2,1,0:T(8,128)(2,1)}, u32[]{:S(2)}) %copy-start) | copy-done | bytes 4194328
  19.5 0.0 copy-start.14
  19.5 0.7 copy-done.14
  20.2 0.0 copy-start.2
  20.2 0.0 copy-start.6
  20.2 8.6 %bias.1 = bf16[32,128,128]{2,1,0:T(8,128)(2,1)} custom-call(bf16[128,128,128]{2,1,0:T(8,128)(2,1)S(1)} %copy-done, bf16[32,128]{1,0:T(8,128)(2,1)S(1)} %bitcast.14), custom_call_target="tpu_custom_call" | custom-call | tf_op jit(solution)/shard_map/bias/pallas_call | solution.py:154
  28.8 0.0 copy-start.9
  28.8 0.0 all-to-all-done.1.kv_ref
  28.8 0.0 copy-start.3
  28.8 0.8 copy-done.3
  29.6 7.9 %all-to-all-start = ((bf16[32,128,128]{2,1,0:T(8,128)(2,1)}), bf16[32,128,128]{2,1,0:T(8,128)(2,1)S(1)}, u32[]{:S(2)}, u32[]{:S(2)}) async-start(bf16[32,128,128]{2,1,0:T(8,128)(2,1)} %bias.1), calls=%async_computation | async-start | bytes 2097152 | tf_op jit(solution)/shard_map/all_to_all | solution.py:167
  37.5 26.1 %all-to-all-done = bf16[32,128,128]{2,1,0:T(8,128)(2,1)S(1)} async-done(((bf16[32,128,128]{2,1,0:T(8,128)(2,1)}), bf16[32,128,128]{2,1,0:T(8,128)(2,1)S(1)}, u32[]{:S(2)}, u32[]{:S(2)}) %all-to-all-start) | async-done | bytes 1048608 | tf_op jit(solution)/shard_map/all_to_all | solution.py:167
  63.6 0.0 copy-start.1
  63.6 0.0 copy-start.4
  63.6 1.2 copy-done.4
  64.8 0.0 copy-start.13
  64.8 1.0 copy-done.13
  65.8 0.0 copy-start.15
  65.8 0.7 copy-done.15
  66.5 1.8 %attend.1 = bf16[16,64,128]{2,1,0:T(8,128)(2,1)S(1)} custom-call(s32[1]{0:T(128)} %bitcast.swap_ref, bf16[64,128]{1,0:T(8,128)(2,1)S(1)} %get-tuple-element.7.query_ref, f32[64,128]{1,0:T(8,128)S(1)} %copy-done.13, bf16[16,2,128,128]{3,2,1,0:T(8,128)(2,1)S(1)} %bitcast.10, bf16[8,2,128,128]{3,2,1,0:T(8,128)(2,1)S(1)} %copy-done.4, s32[16,128]{1,0:T(8,128)S(1)} %bitcast.15), custom_call_target="tpu_custom_call" | custom-call | tf_op jit(solution)/shard_map/attend/pallas_call | solution.py:170
  68.3 13.0 %all_to_all.15 = bf16[16,64,128]{2,1,0:T(8,128)(2,1)S(1)} all-to-all(bf16[16,64,128]{2,1,0:T(8,128)(2,1)S(1)} %attend.1), channel_id=1, replica_groups=mesh['rows'=16,'cols'=16] {'cols'}, dimensions={0} | all-to-all | bytes 524288 | tf_op jit(solution)/shard_map/all_to_all | solution.py:185
  81.2 0.0 copy-done.2
  81.2 0.0 copy-done.6
  81.2 0.0 copy-start.8
  81.2 0.9 copy-done.8
  82.2 1.4 factor.1
  83.6 7.2 %collective-permute-start.1 = (bf16[128,128]{1,0:T(8,128)(2,1)S(1)}, bf16[128,128]{1,0:T(8,128)(2,1)S(1)}, u32[]{:S(2)}, u32[]{:S(2)}) collective-permute-start(bf16[128,128]{1,0:T(8,128)(2,1)S(1)} %get-tuple-element.11.left_ref), channel_id=1, source_target_pairs={{0,0},{1,16},{2,32},{3,48},{4,64},{5,80},{6,96},{7,112},{8,128},{9... | collective-permute-start | bytes 98312 | tf_op jit(solution)/shard_map/ppermute | solution.py:198
  90.8 6.1 %collective-permute-done.1.right_ref = bf16[128,128]{1,0:T(8,128)(2,1)S(1)} collective-permute-done((bf16[128,128]{1,0:T(8,128)(2,1)S(1)}, bf16[128,128]{1,0:T(8,128)(2,1)S(1)}, u32[]{:S(2)}, u32[]{:S(2)}) %collective-permute-start.1) | collective-permute-done | bytes 32800 | tf_op jit(solution)/shard_map/ppermute | solution.py:198
  96.9 0.0 copy-done.9
  96.9 0.0 copy-done.1
  96.9 0.0 copy-start.10
  96.9 0.9 copy-done.10
  97.8 0.0 copy-start.11
  97.8 0.8 copy-done.11
  98.6 61.2 %update.1 = bf16[128,128,128]{2,1,0:T(8,128)(2,1)} custom-call(bf16[128,128,128]{2,1,0:T(8,128)(2,1)S(1)} %copy-done.1, bf16[128,128]{1,0:T(8,128)(2,1)S(1)} %get-tuple-element.11.left_ref, bf16[128,128]{1,0:T(8,128)(2,1)S(1)} %collective-permute-done.1.right_ref, bf16[128,128]{1,0:T(8,128)(2,1)S(1)} %copy-done.11, bf16[128,512]{1,0:T(8,128)(2,1)S(1)} %copy-done.9, ...), custom_call_target="tpu_custom_call" | custom-call | tf_op jit(solution)/shard_map/update/pallas_call | solution.py:201
  (1 shorter events, 0.0 us)
Async XLA Ops:
  0.6 1.0 copy-start.5
  1.6 1.0 copy-start.7
  3.1 0.6 copy-start.12
  3.8 7.9 %collective-permute-start = (bf16[128,128]{1,0:T(8,128)(2,1)S(1)}, bf16[128,128]{1,0:T(8,128)(2,1)S(1)}, u32[]{:S(2)}, u32[]{:S(2)}) collective-permute-start(bf16[128,128]{1,0:T(8,128)(2,1)S(1)} %get-tuple-element.9), channel_id=1, source_target_pairs={{0,128},{16,144},{32,160},{48,176},{64,192},{80,208},{96,224},{112... | collective-permute-start | bytes 98312 | tf_op jit(solution)/shard_map/ppermute | solution.py:149
  12.6 16.2 %all-to-all-start.1 = ((bf16[8,2,128,128]{3,2,1,0:T(8,128)(2,1)}), bf16[8,2,128,128]{3,2,1,0:T(8,128)(2,1)S(1)}, u32[]{:S(2)}, u32[]{:S(2)}) async-start(bf16[8,2,128,128]{3,2,1,0:T(8,128)(2,1)} %broadcast_in_dim.2), calls=%async_computation.1 | async-start | bytes 1048576 | tf_op jit(solution)/shard_map/all_to_all | solution.py:123
  17.3 2.2 %copy-start = (bf16[128,128,128]{2,1,0:T(8,128)(2,1)S(1)}, bf16[128,128,128]{2,1,0:T(8,128)(2,1)}, u32[]{:S(2)}) copy-start(bf16[128,128,128]{2,1,0:T(8,128)(2,1)} %pair_ref.3) | copy-start | bytes 12582916
  19.5 0.7 copy-start.14
  20.2 61.1 %copy-start.2 = (bf16[1024,1024]{1,0:T(8,128)(2,1)S(1)}, bf16[1024,1024]{1,0:T(8,128)(2,1)}, u32[]{:S(2)}) copy-start(bf16[1024,1024]{1,0:T(8,128)(2,1)} %w_out_ref.1) | copy-start | bytes 6291460
  20.2 61.1 %copy-start.6 = (bf16[128,1024]{1,0:T(8,128)(2,1)S(1)}, bf16[128,1024]{1,0:T(8,128)(2,1)}, u32[]{:S(2)}) copy-start(bf16[128,1024]{1,0:T(8,128)(2,1)} %single_ref.3) | copy-start | bytes 786436
  28.8 68.1 %copy-start.9 = (bf16[128,512]{1,0:T(8,128)(2,1)S(1)}, bf16[128,512]{1,0:T(8,128)(2,1)}, u32[]{:S(2)}) copy-start(bf16[128,512]{1,0:T(8,128)(2,1)} %w_up_ref.1) | copy-start | bytes 393220
  28.8 0.8 copy-start.3
  29.6 34.0 %all-to-all-start = ((bf16[32,128,128]{2,1,0:T(8,128)(2,1)}), bf16[32,128,128]{2,1,0:T(8,128)(2,1)S(1)}, u32[]{:S(2)}, u32[]{:S(2)}) async-start(bf16[32,128,128]{2,1,0:T(8,128)(2,1)} %bias.1), calls=%async_computation | async-start | bytes 2097152 | tf_op jit(solution)/shard_map/all_to_all | solution.py:167
  63.6 33.3 %copy-start.1 = (bf16[128,128,128]{2,1,0:T(8,128)(2,1)S(1)}, bf16[128,128,128]{2,1,0:T(8,128)(2,1)}, u32[]{:S(2)}) copy-start(bf16[128,128,128]{2,1,0:T(8,128)(2,1)} %pair_ref.3) | copy-start | bytes 12582916
  63.6 1.2 copy-start.4
  64.8 1.0 copy-start.13
  65.8 0.7 copy-start.15
  81.2 1.0 copy-start.8
  83.6 13.3 %collective-permute-start.1 = (bf16[128,128]{1,0:T(8,128)(2,1)S(1)}, bf16[128,128]{1,0:T(8,128)(2,1)S(1)}, u32[]{:S(2)}, u32[]{:S(2)}) collective-permute-start(bf16[128,128]{1,0:T(8,128)(2,1)S(1)} %get-tuple-element.11.left_ref), channel_id=1, source_target_pairs={{0,0},{1,16},{2,32},{3,48},{4,64},{5,80},{6,96},{7,112},{8,128},{9... | collective-permute-start | bytes 98312 | tf_op jit(solution)/shard_map/ppermute | solution.py:198
  96.9 0.9 copy-start.10
  97.8 0.8 copy-start.11

commit v2 on v1

v2 whole, which is shorter than its diff:
```python
import functools
import math

import jax
import jax.numpy as jnp
from jax import lax
from jax.experimental import pallas as pl
from jax.experimental.pallas import tpu as pltpu
from jax.sharding import PartitionSpec as P

epsilon = 1e-05
f32 = jnp.float32
bf16 = jnp.bfloat16
lowest = -1e30


def normalize(values):
    centred = values - jnp.mean(values, -1, keepdims=True)
    return centred * lax.rsqrt(jnp.mean(centred * centred, -1, keepdims=True) + epsilon)


def nt_dot(a, b):
    return lax.dot_general(a, b, (((1,), (1,)), ((), ())), preferred_element_type=f32)


def project_kernel(single_ref, weight_ref, query_ref, kv_ref, gate_ref):
    normed = normalize(single_ref[...].astype(f32)).astype(bf16)
    projected = nt_dot(weight_ref[...], normed)
    width = query_ref.shape[0]
    query_ref[...] = projected[:width].astype(bf16)
    kv_ref[...] = projected[width : 3 * width].astype(bf16)
    gate_ref[...] = jax.nn.sigmoid(projected[3 * width :])


def normalize_rows(rounded):
    values = rounded.astype(f32)
    width = values.shape[-1]
    centred = values - jnp.dot(
        rounded, jnp.full((width, width), 1.0 / width, bf16), preferred_element_type=f32
    )
    square = jnp.mean(centred * centred, -1, keepdims=True)
    return (centred * lax.rsqrt(square + epsilon)).astype(bf16)


def bias_kernel(pair_ref, weight_ref, out_ref, held_ref):
    block_rows, tile_cols, width = pair_ref.shape
    normed = normalize_rows(pair_ref[...].reshape(block_rows * tile_cols, width))
    both = nt_dot(weight_ref[...], normed)
    for i in range(block_rows):
        held_ref[:, i, :] = both[:, i * tile_cols : (i + 1) * tile_cols]
    out_ref[...] = held_ref[...].astype(bf16)


def attend_kernel(
    place_ref, query_ref, gate_ref, bias_ref, near_ref, far_ref, mask_ref, out_ref, score_ref
):
    blocks, heads_here, tile_rows, tile_cols = bias_ref.shape
    width = query_ref.shape[0]
    head_width = width // heads_here
    score_scale = 1.0 / math.sqrt(head_width)
    shifts, halves = near_ref.shape[:2]
    half, turn, core = place_ref[0], place_ref[1], place_ref[2]
    order = []
    for c, kv_ref in enumerate((near_ref, far_ref)):
        for s in range(shifts):
            for z in range(halves):
                row = ((half ^ z) * shifts + ((turn + shifts - s) & (shifts - 1))) * 2 + (core ^ c)
                order.append((kv_ref, s, z, row))
    query = jnp.transpose(query_ref[...].astype(f32)).astype(bf16)
    attended = []
    for h in range(heads_here):
        query_head = query[:, h * head_width : (h + 1) * head_width]
        key_rows = pl.ds(h * head_width, head_width)
        value_rows = pl.ds(width + h * head_width, head_width)
        top = None
        for b, (kv_ref, s, z, row) in enumerate(order):
            key = kv_ref[s, z, key_rows, :]
            scores = jnp.dot(query_head, key, preferred_element_type=f32) * score_scale
            scores = scores + bias_ref[row, h].astype(f32)
            scores = jnp.where(mask_ref[row] > 0, scores, lowest)
            score_ref[b] = scores
            top = scores if top is None else jnp.maximum(top, scores)
        top = jnp.max(top, axis=-1, keepdims=True)
        total = mixed = None
        for b, (kv_ref, s, z, row) in enumerate(order):
            weights = jnp.exp(score_ref[b] - top)
            part = nt_dot(weights.astype(bf16), kv_ref[s, z, value_rows, :])
            total = weights if total is None else total + weights
            mixed = part if mixed is None else mixed + part
        attended.append(mixed / jnp.sum(total, axis=-1, keepdims=True))
    mixed = jnp.transpose(jnp.concatenate(attended, axis=1)) * gate_ref[...]
    mixed = mixed.astype(bf16)
    for d in range(out_ref.shape[0]):
        out_ref[d] = mixed


def factor_kernel(mixed_ref, w_out_ref, single_ref, w_factors_ref, out_ref, factors_ref):
    mixed = jnp.transpose(mixed_ref[...].astype(f32)).astype(bf16)
    head_total = jnp.dot(mixed, w_out_ref[...], preferred_element_type=f32)
    single_out = (single_ref[...].astype(f32) + head_total).astype(bf16)
    out_ref[...] = single_out
    normed = normalize(single_out.astype(f32)).astype(bf16)
    factors_ref[...] = jnp.dot(normed, w_factors_ref[...], preferred_element_type=f32).astype(bf16)


def update_kernel(
    pair_ref, left_ref, right_ref, w_pairout_ref, w_up_ref, w_down_ref, out_ref, scale_ref, shift_ref
):
    block_rows, tile_cols, width = pair_ref.shape
    factor_width = width // 2
    low = lax.broadcasted_iota(jnp.int32, (1, width), 1) < factor_width
    right = right_ref[:, factor_width:]
    right = jnp.concatenate([right, right], axis=1)
    left = left_ref[:, :factor_width].astype(f32)
    left = jnp.concatenate([left, left], axis=1)
    scale_ref[...] = jnp.where(low, left, -1.0).astype(bf16)[:, None, :]
    shift_ref[...] = jnp.where(low, 0.0, left).astype(bf16)[:, None, :]
    rows_here = block_rows * tile_cols
    paired = (right[None] * scale_ref[...] + shift_ref[...]).reshape(rows_here, width)
    moved = jnp.dot(paired, w_pairout_ref[...], preferred_element_type=f32)
    pair_mid = (pair_ref[...].reshape(rows_here, width).astype(f32) + moved).astype(bf16)
    normed = normalize_rows(pair_mid)
    hidden = jnp.dot(normed, w_up_ref[...], preferred_element_type=f32).astype(bf16)
    hidden = jnp.maximum(hidden, 0)
    down = jnp.dot(hidden, w_down_ref[...], preferred_element_type=f32)
    out_ref[...] = (pair_mid.astype(f32) + down).astype(bf16).reshape(pair_ref.shape)


def whole(shape):
    return pl.BlockSpec(shape, lambda *_: (0,) * len(shape))


def params(mib=8):
    return pltpu.CompilerParams(vmem_limit_bytes=mib * 1024 * 1024)


def per_device(
    single, pair, residue_mask, w_bias, w_project, w_out, w_factors, w_pairout, w_up, w_down
):
    tile_rows, tile_cols, pair_width = pair.shape
    single_width = single.shape[1]
    width = w_project.shape[2]
    rows, cols = lax.axis_size("rows"), lax.axis_size("cols")
    heads = w_bias.shape[1]
    heads_here = heads // cols

    block_rows = 64
    bias_local = pl.pallas_call(
        bias_kernel,
        grid=(tile_rows // block_rows,),
        in_specs=[
            pl.BlockSpec((block_rows, tile_cols, pair_width), lambda i: (i, 0, 0)),
            whole((heads, pair_width)),
        ],
        out_specs=pl.BlockSpec((heads, block_rows, tile_cols), lambda i: (0, i, 0)),
        out_shape=jax.ShapeDtypeStruct((heads, tile_rows, tile_cols), bf16),
        scratch_shapes=[pltpu.VMEM((heads, block_rows, tile_cols), f32)],
        compiler_params=params(20),
        name="bias",
    )(pair, jnp.transpose(w_bias))
    bias_local, single = lax.optimization_barrier((bias_local, single))
    bias_heads = lax.all_to_all(bias_local, "cols", 0, 0, tiled=True)

    weight = jnp.transpose(w_project, (0, 2, 1)).reshape(4 * width, single_width)
    query, kv, gate_values = pl.pallas_call(
        project_kernel,
        out_shape=(
            jax.ShapeDtypeStruct((width, tile_rows), bf16),
            jax.ShapeDtypeStruct((2 * width, tile_rows), bf16),
            jax.ShapeDtypeStruct((width, tile_rows), f32),
        ),
        compiler_params=params(),
        name="project",
    )(single, weight)

    shifts = rows // 4
    half = rows // 2

    def sent(value, target):
        return lax.ppermute(value, "rows", [(r, target(r)) for r in range(rows)])

    both = jnp.stack([kv, sent(kv, lambda r: r ^ half)])
    near = [both]
    for s in range(1, shifts):
        near.append(sent(both, lambda r: (r & half) | ((r + 2 * s) & (half - 1))))
    near = jnp.stack(near)
    far = sent(near, lambda r: r ^ 1)

    row = lax.axis_index("rows")
    place = jnp.stack([row // half, (row % half) // 2, row % 2]).astype(jnp.int32)
    mixed = pl.pallas_call(
        attend_kernel,
        in_specs=[pl.BlockSpec(memory_space=pltpu.SMEM)] + [pl.BlockSpec(memory_space=pltpu.VMEM)] * 6,
        out_shape=jax.ShapeDtypeStruct((cols, width, tile_rows), bf16),
        scratch_shapes=[pltpu.VMEM((cols, tile_rows, tile_cols), f32)],
        compiler_params=params(),
        name="attend",
    )(
        place,
        query,
        gate_values,
        bias_heads.reshape(cols, heads_here, tile_rows, tile_cols),
        near,
        far,
        residue_mask.reshape(cols, 1, tile_cols),
    )
    mixed_all = lax.all_to_all(mixed, "cols", 0, 0, tiled=True).reshape(single_width, tile_rows)

    single_out, factors = pl.pallas_call(
        factor_kernel,
        out_shape=(
            jax.ShapeDtypeStruct(single.shape, bf16),
            jax.ShapeDtypeStruct((tile_rows, w_factors.shape[1]), bf16),
        ),
        compiler_params=params(),
        name="factor",
    )(mixed_all, w_out, single, w_factors)

    swapped = [(a * cols + b, b * cols + a) for a in range(rows) for b in range(cols)]
    right_factors = lax.ppermute(factors, ("rows", "cols"), swapped)

    block_rows = 32
    updated = pl.pallas_call(
        update_kernel,
        grid=(tile_rows // block_rows,),
        in_specs=[
            pl.BlockSpec((block_rows, tile_cols, pair_width), lambda i: (i, 0, 0)),
            pl.BlockSpec((block_rows, factors.shape[1]), lambda i: (i, 0)),
            whole(right_factors.shape),
            whole(w_pairout.shape),
            whole(w_up.shape),
            whole(w_down.shape),
        ],
        out_specs=pl.BlockSpec((block_rows, tile_cols, pair_width), lambda i: (i, 0, 0)),
        out_shape=jax.ShapeDtypeStruct(pair.shape, bf16),
        scratch_shapes=[pltpu.VMEM((block_rows, 1, pair_width), bf16)] * 2,
        compiler_params=params(20),
        name="update",
    )(pair, factors, right_factors, w_pairout, w_up, w_down)
    return (single_out, updated)


def solution(mesh):
    return jax.shard_map(
        per_device,
        mesh=mesh,
        in_specs=(
            P("rows", None),
            P("rows", "cols", None),
            P(),
            P(),
            P(None, None, "cols"),
            P(),
            P(),
            P(),
            P(),
            P(),
        ),
        out_specs=(P("rows", None), P("rows", "cols", None)),
        check_vma=False,
    )
```

time: 160 us -> 105 us (0.66)
  Pallas kernels: 73.5 us -> 23.2 us
  blocking collectives: 13 us -> 23.3 us
  waiting for transfers between devices: 34.7 us -> 26.1 us
  starting transfers between devices: 25.2 us -> 19.6 us
  local copies, waits for them, and re-layouts: 12.7 us -> 10.5 us
    pallas_call x1, Pallas kernels: 61.2 us -> 13.6 us  [per_device(): pl.pallas_call(update_kernel, grid=(tile_rows // block_rows,), in_specs=[...]
    all_to_all x1, waiting for transfers between devices: 26.1 us -> 0.92 us  [per_device(): bias_heads = lax.all_to_all(bias_local, 'cols', 0, 0, tiled=True)]
    ppermute x1 -> x5, waiting for transfers between devices: 2.53 us -> 15.3 us  [sent(): return lax.ppermute(value, 'rows', [(r, target(r)) for r in range(rows)])]
    all_to_all x1, blocking collectives: 13 us -> 23.3 us  [per_device(): lax.all_to_all(mixed, 'cols', 0, 0, tiled=True)]
    all_to_all x1 -> x0, starting transfers between devices: 4.69 us -> none  [gather_directly(): lax.all_to_all(pieces, axis, 0, 0, axis_index_groups=groups, tiled=True)]
    ppermute x1, starting transfers between devices: 7.23 us -> 3.39 us  [per_device(): right_factors = lax.ppermute(factors, ('rows', 'cols'), swapped)]
    ppermute x1, waiting for transfers between devices: 6.08 us -> 9.92 us  [per_device(): right_factors = lax.ppermute(factors, ('rows', 'cols'), swapped)]
    pallas_call x1, Pallas kernels: 8.59 us -> 4.99 us  [per_device(): pl.pallas_call(bias_kernel, grid=(tile_rows // block_rows,), in_specs=[pl...]
  transfers between devices with their start and end apart: 4 -> 7, of which waited for: 3 -> 6; matrix products, arithmetic and copies ran while one was open for 0% -> 1% of each run, Pallas kernels for 5% -> 0%
where the time goes in v2:
time: 105 us; the launch traced here: 104 us
  waiting for transfers between devices  26.1 us (25%)
  blocking collectives  23.3 us (22%)
  Pallas kernels  23.2 us (22%)
  starting transfers between devices  19.6 us (19%)
  local copies, waits for them, and re-layouts  10.5 us (10%)
    all_to_all x1, blocking collectives, per_device(): lax.all_to_all(mixed, 'cols', 0, 0, tiled=True)  23.3 us
    ppermute x5, waiting for transfers between devices, sent(): return lax.ppermute(value, 'rows', [(r, target(r)) for r in range(rows)])  15.3 us
    pallas_call x1, Pallas kernels, per_device(): pl.pallas_call(update_kernel, grid=(tile_rows // block_rows,), in_specs=[...  13.6 us
    unnamed x30, local copies, waits for them, and re-layouts  10.5 us
    ppermute x1, waiting for transfers between devices, per_device(): right_factors = lax.ppermute(factors, ('rows', 'cols'), swapped)  9.92 us
    all_to_all x1, starting transfers between devices, per_device(): bias_heads = lax.all_to_all(bias_local, 'cols', 0, 0, tiled=True)  8.16 us
    ppermute x5, starting transfers between devices, sent(): return lax.ppermute(value, 'rows', [(r, target(r)) for r in range(rows)])  8.09 us
    pallas_call x1, Pallas kernels, per_device(): pl.pallas_call(bias_kernel, grid=(tile_rows // block_rows,), in_specs=[pl...  4.99 us
  transfers between devices with their start and end apart: 7, of which 6 were waited for; matrix products, arithmetic and copies ran while one was open for 1% of the time, Pallas kernels for 0%

profile of v2, /device:TPU:88, one launch (start us, length us, event | category | flops | bytes accessed | tf_op | source)
XLA Modules:
  0.0 104.2 jit_solution(5683834450455506164)
XLA Ops:
  0.6 0.0 copy-start
  0.6 2.2 %copy-done = bf16[128,128,128]{2,1,0:T(8,128)(2,1)S(1)} copy-done((bf16[128,128,128]{2,1,0:T(8,128)(2,1)S(1)}, bf16[128,128,128]{2,1,0:T(8,128)(2,1)}, u32[]{:S(2)}) %copy-start) | copy-done | bytes 4194328
  2.8 0.0 copy-start.12
  2.8 0.7 copy-done.12
  3.5 0.0 copy-start.3
  3.5 0.0 copy-start.7
  3.5 5.0 %bias.1 = bf16[32,128,128]{2,1,0:T(8,128)(2,1)} custom-call(bf16[128,128,128]{2,1,0:T(8,128)(2,1)S(1)} %copy-done, bf16[32,128]{1,0:T(8,128)(2,1)S(1)} %bitcast.21), custom_call_target="tpu_custom_call" | custom-call | tf_op jit(solution)/shard_map/bias/pallas_call | solution.py:148
  8.5 0.0 copy-start.2
  8.5 8.2 %all-to-all-start = ((bf16[32,128,128]{2,1,0:T(8,128)(2,1)}), bf16[32,128,128]{2,1,0:T(8,128)(2,1)S(1)}, u32[]{:S(2)}, u32[]{:S(2)}) async-start(bf16[32,128,128]{2,1,0:T(8,128)(2,1)} %bias.1), calls=%async_computation | async-start | bytes 2097152 | tf_op jit(solution)/shard_map/all_to_all | solution.py:162
  16.7 0.0 copy-done.3
  16.7 0.0 copy-start.5
  16.7 1.0 copy-done.5
  17.7 0.5 project.1
  18.2 0.0 copy-start.10
  18.3 0.6 copy-done.10
  18.9 4.5 %collective-permute-start = (bf16[128,128]{1,0:T(8,128)(2,1)S(1)}, bf16[128,128]{1,0:T(8,128)(2,1)S(1)}, u32[]{:S(2)}, u32[]{:S(2)}) collective-permute-start(bf16[128,128]{1,0:T(8,128)(2,1)S(1)} %get-tuple-element.13), channel_id=1, source_target_pairs={{0,128},{16,144},{32,160},{48,176},{64,192},{80,208},{96,224},{112... | collective-permute-start | bytes 98312 | tf_op jit(solution)/shard_map/ppermute | solution.py:180
  23.4 8.8 %collective-permute-done = bf16[128,128]{1,0:T(8,128)(2,1)S(1)} collective-permute-done((bf16[128,128]{1,0:T(8,128)(2,1)S(1)}, bf16[128,128]{1,0:T(8,128)(2,1)S(1)}, u32[]{:S(2)}, u32[]{:S(2)}) %collective-permute-start) | collective-permute-done | bytes 32800 | tf_op jit(solution)/shard_map/ppermute | solution.py:180
  32.1 1.3 %collective-permute-start.2 = (bf16[2,128,128]{2,1,0:T(8,128)(2,1)S(1)}, bf16[2,128,128]{2,1,0:T(8,128)(2,1)S(1)}, u32[]{:S(2)}, u32[]{:S(2)}) collective-permute-start(bf16[2,128,128]{2,1,0:T(8,128)(2,1)S(1)} %get-tuple-element.17), channel_id=1, source_target_pairs={{0,64},{16,80},{32,96},{48,112},{64,0},{80,16},{96,32},{112,48},{1... | collective-permute-start | bytes 196616 | tf_op jit(solution)/shard_map/ppermute | solution.py:180
  33.5 2.2 %collective-permute-start.1 = (bf16[2,128,128]{2,1,0:T(8,128)(2,1)S(1)}, bf16[2,128,128]{2,1,0:T(8,128)(2,1)S(1)}, u32[]{:S(2)}, u32[]{:S(2)}) collective-permute-start(bf16[2,128,128]{2,1,0:T(8,128)(2,1)S(1)} %get-tuple-element.17), channel_id=1, source_target_pairs={{0,32},{16,48},{32,64},{48,80},{64,96},{80,112},{96,0},{112,16},{1... | collective-permute-start | bytes 196616 | tf_op jit(solution)/shard_map/ppermute | solution.py:180
  35.6 0.0 collective-permute-start.3
  35.6 2.3 %collective-permute-done.2 = bf16[2,128,128]{2,1,0:T(8,128)(2,1)S(1)} collective-permute-done((bf16[2,128,128]{2,1,0:T(8,128)(2,1)S(1)}, bf16[2,128,128]{2,1,0:T(8,128)(2,1)S(1)}, u32[]{:S(2)}, u32[]{:S(2)}) %collective-permute-start.2) | collective-permute-done | bytes 65568 | tf_op jit(solution)/shard_map/ppermute | solution.py:180
  38.0 0.0 collective-permute-done.1
  38.0 3.1 %collective-permute-done.3 = bf16[2,128,128]{2,1,0:T(8,128)(2,1)S(1)} collective-permute-done((bf16[2,128,128]{2,1,0:T(8,128)(2,1)S(1)}, bf16[2,128,128]{2,1,0:T(8,128)(2,1)S(1)}, u32[]{:S(2)}, u32[]{:S(2)}) %collective-permute-start.3) | collective-permute-done | bytes 65568 | tf_op jit(solution)/shard_map/ppermute | solution.py:180
  41.2 0.1 collective-permute-start.4
  41.3 0.6 pad_add_fusion.place_ref
  41.9 1.0 collective-permute-done.4.far_ref
  42.9 0.9 all-to-all-done
  43.8 0.0 copy-start.1
  43.8 0.0 copy-start.11
  43.8 0.9 copy-done.11
  44.8 0.0 copy-start.13
  44.8 0.9 copy-done.13
  45.7 0.0 copy-start.14
  45.7 0.6 copy-done.14
  46.3 2.7 %attend.1 = bf16[16,64,128]{2,1,0:T(8,128)(2,1)S(1)} custom-call(s32[3]{0:T(128)S(1)} %copy-done.14, bf16[64,128]{1,0:T(8,128)(2,1)S(1)} %get-tuple-element.10.query_ref, f32[64,128]{1,0:T(8,128)S(1)} %copy-done.11, bf16[16,2,128,128]{3,2,1,0:T(8,128)(2,1)S(1)} %bitcast.17, bf16[4,2,128,128]{3,2,1,0:T(8,128)(2,1)S(1)} %pad_maximum_fusion.near_ref, ...), custom_call_target="tpu_custom_call" | custom-call | tf_op jit(solution)/shard_map/attend/pallas_call | solution.py:191
  49.0 23.3 %all_to_all.10 = bf16[16,64,128]{2,1,0:T(8,128)(2,1)S(1)} all-to-all(bf16[16,64,128]{2,1,0:T(8,128)(2,1)S(1)} %attend.1), channel_id=1, replica_groups=mesh['rows'=16,'cols'=16] {'cols'}, dimensions={0} | all-to-all | bytes 524288 | tf_op jit(solution)/shard_map/all_to_all | solution.py:207
  72.3 0.0 copy-done.2
  72.3 0.0 copy-start.4
  72.3 0.9 copy-done.4
  73.3 0.0 copy-start.6
  73.3 0.9 copy-done.6
  74.2 1.4 %factor.1 = (bf16[128,1024]{1,0:T(8,128)(2,1)}, bf16[128,128]{1,0:T(8,128)(2,1)S(1)}) custom-call(bf16[1024,128]{1,0:T(8,128)(2,1)S(1)} %bitcast.18, bf16[1024,1024]{1,0:T(8,128)(2,1)S(1)} %copy-done.2, bf16[128,1024]{1,0:T(8,128)(2,1)S(1)} %copy-done.4, bf16[1024,128]{1,0:T(8,128)(2,1)S(1)} %copy-done.6), custom_call_target="tpu_custom_call" | custom-call | tf_op jit(solution)/shard_map/factor/pallas_call | solution.py:209
  75.6 3.4 %collective-permute-start.5 = (bf16[128,128]{1,0:T(8,128)(2,1)S(1)}, bf16[128,128]{1,0:T(8,128)(2,1)S(1)}, u32[]{:S(2)}, u32[]{:S(2)}) collective-permute-start(bf16[128,128]{1,0:T(8,128)(2,1)S(1)} %get-tuple-element.15.left_ref), channel_id=1, source_target_pairs={{0,0},{1,16},{2,32},{3,48},{4,64},{5,80},{6,96},{7,112},{8,128},{9... | collective-permute-start | bytes 98312 | tf_op jit(solution)/shard_map/ppermute | solution.py:220
  79.0 9.9 %collective-permute-done.5.right_ref = bf16[128,128]{1,0:T(8,128)(2,1)S(1)} collective-permute-done((bf16[128,128]{1,0:T(8,128)(2,1)S(1)}, bf16[128,128]{1,0:T(8,128)(2,1)S(1)}, u32[]{:S(2)}, u32[]{:S(2)}) %collective-permute-start.5) | collective-permute-done | bytes 32800 | tf_op jit(solution)/shard_map/ppermute | solution.py:220
  88.9 0.0 copy-done.7
  88.9 0.0 copy-done.1
  89.0 0.0 copy-start.8
  89.0 0.9 copy-done.8
  89.9 0.0 copy-start.9
  89.9 0.8 copy-done.9
  90.6 13.6 %update.1 = bf16[128,128,128]{2,1,0:T(8,128)(2,1)} custom-call(bf16[128,128,128]{2,1,0:T(8,128)(2,1)S(1)} %copy-done.1, bf16[128,128]{1,0:T(8,128)(2,1)S(1)} %get-tuple-element.15.left_ref, bf16[128,128]{1,0:T(8,128)(2,1)S(1)} %collective-permute-done.5.right_ref, bf16[128,128]{1,0:T(8,128)(2,1)S(1)} %copy-done.9, bf16[128,512]{1,0:T(8,128)(2,1)S(1)} %copy-done.7, ...), custom_call_target="tpu_custom_call" | custom-call | tf_op jit(solution)/shard_map/update/pallas_call | solution.py:223
  (2 shorter events, 0.0 us)
Async XLA Ops:
  0.6 2.2 %copy-start = (bf16[128,128,128]{2,1,0:T(8,128)(2,1)S(1)}, bf16[128,128,128]{2,1,0:T(8,128)(2,1)}, u32[]{:S(2)}) copy-start(bf16[128,128,128]{2,1,0:T(8,128)(2,1)} %pair_ref.3) | copy-start | bytes 12582916
  2.8 0.7 copy-start.12
  3.5 13.2 %copy-start.3 = (bf16[128,1024]{1,0:T(8,128)(2,1)S(1)}, bf16[128,1024]{1,0:T(8,128)(2,1)}, u32[]{:S(2)}) copy-start(bf16[128,1024]{1,0:T(8,128)(2,1)} %single_ref.1) | copy-start | bytes 786436
  3.5 85.4 %copy-start.7 = (bf16[128,512]{1,0:T(8,128)(2,1)S(1)}, bf16[128,512]{1,0:T(8,128)(2,1)}, u32[]{:S(2)}) copy-start(bf16[128,512]{1,0:T(8,128)(2,1)} %w_up_ref.1) | copy-start | bytes 393220
  8.5 63.8 %copy-start.2 = (bf16[1024,1024]{1,0:T(8,128)(2,1)S(1)}, bf16[1024,1024]{1,0:T(8,128)(2,1)}, u32[]{:S(2)}) copy-start(bf16[1024,1024]{1,0:T(8,128)(2,1)} %w_out_ref.1) | copy-start | bytes 6291460
  8.5 35.3 %all-to-all-start = ((bf16[32,128,128]{2,1,0:T(8,128)(2,1)}), bf16[32,128,128]{2,1,0:T(8,128)(2,1)S(1)}, u32[]{:S(2)}, u32[]{:S(2)}) async-start(bf16[32,128,128]{2,1,0:T(8,128)(2,1)} %bias.1), calls=%async_computation | async-start | bytes 2097152 | tf_op jit(solution)/shard_map/all_to_all | solution.py:162
  16.7 1.0 %copy-start.5 = (bf16[4,1024,64]{1,2,0:T(8,128)(2,1)S(1)}, bf16[4,1024,64]{1,2,0:T(8,128)(2,1)}, u32[]{:S(2)}) copy-start(bf16[4,1024,64]{1,2,0:T(8,128)(2,1)} %param.14) | copy-start | bytes 1572868
  18.2 0.6 copy-start.10
  18.9 13.3 %collective-permute-start = (bf16[128,128]{1,0:T(8,128)(2,1)S(1)}, bf16[128,128]{1,0:T(8,128)(2,1)S(1)}, u32[]{:S(2)}, u32[]{:S(2)}) collective-permute-start(bf16[128,128]{1,0:T(8,128)(2,1)S(1)} %get-tuple-element.13), channel_id=1, source_target_pairs={{0,128},{16,144},{32,160},{48,176},{64,192},{80,208},{96,224},{112... | collective-permute-start | bytes 98312 | tf_op jit(solution)/shard_map/ppermute | solution.py:180
  32.1 5.9 %collective-permute-start.2 = (bf16[2,128,128]{2,1,0:T(8,128)(2,1)S(1)}, bf16[2,128,128]{2,1,0:T(8,128)(2,1)S(1)}, u32[]{:S(2)}, u32[]{:S(2)}) collective-permute-start(bf16[2,128,128]{2,1,0:T(8,128)(2,1)S(1)} %get-tuple-element.17), channel_id=1, source_target_pairs={{0,64},{16,80},{32,96},{48,112},{64,0},{80,16},{96,32},{112,48},{1... | collective-permute-start | bytes 196616 | tf_op jit(solution)/shard_map/ppermute | solution.py:180
  33.5 4.5 %collective-permute-start.1 = (bf16[2,128,128]{2,1,0:T(8,128)(2,1)S(1)}, bf16[2,128,128]{2,1,0:T(8,128)(2,1)S(1)}, u32[]{:S(2)}, u32[]{:S(2)}) collective-permute-start(bf16[2,128,128]{2,1,0:T(8,128)(2,1)S(1)} %get-tuple-element.17), channel_id=1, source_target_pairs={{0,32},{16,48},{32,64},{48,80},{64,96},{80,112},{96,0},{112,16},{1... | collective-permute-start | bytes 196616 | tf_op jit(solution)/shard_map/ppermute | solution.py:180
  35.6 5.5 %collective-permute-start.3 = (bf16[2,128,128]{2,1,0:T(8,128)(2,1)S(1)}, bf16[2,128,128]{2,1,0:T(8,128)(2,1)S(1)}, u32[]{:S(2)}, u32[]{:S(2)}) collective-permute-start(bf16[2,128,128]{2,1,0:T(8,128)(2,1)S(1)} %get-tuple-element.17), channel_id=1, source_target_pairs={{0,96},{16,112},{32,0},{48,16},{64,32},{80,48},{96,64},{112,80},{1... | collective-permute-start | bytes 196616 | tf_op jit(solution)/shard_map/ppermute | solution.py:180
  41.2 1.8 %collective-permute-start.4 = (bf16[4,2,128,128]{3,2,1,0:T(8,128)(2,1)S(1)}, bf16[4,2,128,128]{3,2,1,0:T(8,128)(2,1)}, u32[]{:S(2)}, u32[]{:S(2)}) collective-permute-start(bf16[4,2,128,128]{3,2,1,0:T(8,128)(2,1)S(1)} %pad_maximum_fusion.near_ref), channel_id=1, source_target_pairs={{0,16},{16,0},{32,48},{48,32},{64,80},{80,64},{96,112},{112,96},{1... | collective-permute-start | bytes 786440 | tf_op jit(solution)/shard_map/ppermute | solution.py:180
  43.8 45.1 %copy-start.1 = (bf16[128,128,128]{2,1,0:T(8,128)(2,1)S(1)}, bf16[128,128,128]{2,1,0:T(8,128)(2,1)}, u32[]{:S(2)}) copy-start(bf16[128,128,128]{2,1,0:T(8,128)(2,1)} %pair_ref.3) | copy-start | bytes 12582916
  43.8 0.9 copy-start.11
  44.8 0.9 copy-start.13
  45.7 0.6 copy-start.14
  72.3 1.0 copy-start.4
  73.3 0.9 copy-start.6
  75.6 13.3 %collective-permute-start.5 = (bf16[128,128]{1,0:T(8,128)(2,1)S(1)}, bf16[128,128]{1,0:T(8,128)(2,1)S(1)}, u32[]{:S(2)}, u32[]{:S(2)}) collective-permute-start(bf16[128,128]{1,0:T(8,128)(2,1)S(1)} %get-tuple-element.15.left_ref), channel_id=1, source_target_pairs={{0,0},{1,16},{2,32},{3,48},{4,64},{5,80},{6,96},{7,112},{8,128},{9... | collective-permute-start | bytes 98312 | tf_op jit(solution)/shard_map/ppermute | solution.py:220
  89.0 0.9 copy-start.8
  89.9 0.8 copy-start.9

commit v3 on v2

v3 whole, which is shorter than its diff:
```python
import functools
import math

import jax
import jax.numpy as jnp
from jax import lax
from jax.experimental import pallas as pl
from jax.experimental.pallas import tpu as pltpu
from jax.sharding import PartitionSpec as P

epsilon = 1e-05
f32 = jnp.float32
bf16 = jnp.bfloat16
lowest = -1e30


def normalize(values):
    centred = values - jnp.mean(values, -1, keepdims=True)
    return centred * lax.rsqrt(jnp.mean(centred * centred, -1, keepdims=True) + epsilon)


def nt_dot(a, b):
    return lax.dot_general(a, b, (((1,), (1,)), ((), ())), preferred_element_type=f32)


def start_copies(pairs, sems):
    copies = [pltpu.make_async_copy(a, b, sems.at[i]) for i, (a, b) in enumerate(pairs)]
    for copy in copies:
        copy.start()
    return copies


def project_kernel(
    single_hbm, weight_hbm, query_ref, kv_ref, gate_ref, single_ref, weight_ref, sems
):
    copies = start_copies(((single_hbm, single_ref), (weight_hbm, weight_ref)), sems)
    copies[0].wait()
    normed = normalize(single_ref[...].astype(f32)).astype(bf16)
    copies[1].wait()
    projected = nt_dot(weight_ref[...], normed)
    width = query_ref.shape[0]
    query_ref[...] = projected[:width].astype(bf16)
    kv_ref[...] = projected[width : 3 * width].astype(bf16)
    gate_ref[...] = jax.nn.sigmoid(projected[3 * width :])


def normalize_rows(rounded):
    values = rounded.astype(f32)
    width = values.shape[-1]
    centred = values - jnp.dot(
        rounded, jnp.full((width, width), 1.0 / width, bf16), preferred_element_type=f32
    )
    square = jnp.mean(centred * centred, -1, keepdims=True)
    return (centred * lax.rsqrt(square + epsilon)).astype(bf16)


def bias_kernel(
    pair_hbm, weight_hbm, mask_hbm, out_ref, pair_ref, weight_ref, mask_ref, held_ref, sems
):
    tile_rows, tile_cols, width = pair_ref.shape
    step = held_ref.shape[1]
    parts = [(weight_hbm, weight_ref), (mask_hbm.at[lax.axis_index("cols")], mask_ref)]
    for at in range(0, tile_rows, step):
        parts.append((pair_hbm.at[pl.ds(at, step)], pair_ref.at[pl.ds(at, step)]))
    copies = start_copies(parts, sems)
    copies[0].wait()
    copies[1].wait()
    included = mask_ref[...] > 0
    for at in range(0, tile_rows, step):
        copies[2 + at // step].wait()
        normed = normalize_rows(pair_ref[at : at + step].reshape(step * tile_cols, width))
        both = nt_dot(weight_ref[...], normed)
        for i in range(step):
            held_ref[:, i, :] = both[:, i * tile_cols : (i + 1) * tile_cols]
        held = jnp.where(included[None], held_ref[...], lowest)
        out_ref[:, at : at + step, :] = held.astype(bf16)


def attend_kernel(query_ref, gate_ref, bias_ref, kv_ref, out_ref, score_ref):
    blocks, heads_here, tile_rows, tile_cols = bias_ref.shape
    width = query_ref.shape[0]
    head_width = width // heads_here
    score_scale = 1.0 / math.sqrt(head_width)
    shifts = kv_ref.shape[1]
    me = lax.axis_index("rows")
    half, turn, core = me // (2 * shifts), (me // 2) % shifts, me % 2

    def block(b, part):
        sent = (turn + shifts - (b // 2) % shifts) % shifts
        return kv_ref[(b % 2) ^ core, sent, (b // (2 * shifts)) ^ half, part, :]

    query = jnp.transpose(query_ref[...].astype(f32)).astype(bf16)
    attended = []
    for h in range(heads_here):
        query_head = query[:, h * head_width : (h + 1) * head_width]
        key_rows = pl.ds(h * head_width, head_width)
        value_rows = pl.ds(width + h * head_width, head_width)
        top = None
        for b in range(blocks):
            scores = jnp.dot(query_head, block(b, key_rows), preferred_element_type=f32)
            scores = scores * score_scale + bias_ref[b, h].astype(f32)
            score_ref[b] = scores
            top = scores if top is None else jnp.maximum(top, scores)
        top = jnp.max(top, axis=-1, keepdims=True)
        total = mixed = None
        for b in range(blocks):
            weights = jnp.exp(score_ref[b] - top)
            part = nt_dot(weights.astype(bf16), block(b, value_rows))
            total = weights if total is None else total + weights
            mixed = part if mixed is None else mixed + part
        attended.append(mixed / jnp.sum(total, axis=-1, keepdims=True))
    mixed = jnp.transpose(jnp.concatenate(attended, axis=1)) * gate_ref[...]
    mixed = mixed.astype(bf16)
    for d in range(out_ref.shape[0]):
        out_ref[d] = mixed


def factor_kernel(
    mixed_ref,
    w_out_hbm,
    single_hbm,
    w_factors_hbm,
    out_ref,
    factors_ref,
    w_out_ref,
    single_ref,
    w_factors_ref,
    sems,
):
    depth = w_out_ref.shape[0]
    step = depth // 4
    parts = [(w_out_hbm.at[pl.ds(at, step)], w_out_ref.at[pl.ds(at, step)]) for at in range(0, depth, step)]
    parts += [(single_hbm, single_ref), (w_factors_hbm, w_factors_ref)]
    copies = start_copies(parts, sems)
    mixed = jnp.transpose(mixed_ref[...].astype(f32)).astype(bf16)
    head_total = None
    for at in range(0, depth, step):
        copies[at // step].wait()
        part = jnp.dot(
            mixed[:, at : at + step], w_out_ref[at : at + step, :], preferred_element_type=f32
        )
        head_total = part if head_total is None else head_total + part
    copies[4].wait()
    single_out = (single_ref[...].astype(f32) + head_total).astype(bf16)
    out_ref[...] = single_out
    normed = normalize(single_out.astype(f32)).astype(bf16)
    copies[5].wait()
    factors_ref[...] = jnp.dot(normed, w_factors_ref[...], preferred_element_type=f32).astype(bf16)


def update_kernel(
    pair_ref,
    left_ref,
    right_ref,
    w_pairout_hbm,
    w_up_hbm,
    w_down_hbm,
    out_ref,
    w_pairout_ref,
    w_up_ref,
    w_down_ref,
    scale_ref,
    shift_ref,
    sems,
):
    @pl.when(pl.program_id(0) == 0)
    def _():
        copies = start_copies(
            (
                (w_pairout_hbm, w_pairout_ref),
                (w_up_hbm, w_up_ref),
                (w_down_hbm, w_down_ref),
            ),
            sems,
        )
        for copy in copies:
            copy.wait()

    block_rows, tile_cols, width = pair_ref.shape
    factor_width = width // 2
    low = lax.broadcasted_iota(jnp.int32, (1, width), 1) < factor_width
    right = right_ref[:, factor_width:]
    right = jnp.concatenate([right, right], axis=1)
    left = left_ref[:, :factor_width].astype(f32)
    left = jnp.concatenate([left, left], axis=1)
    scale_ref[...] = jnp.where(low, left, -1.0).astype(bf16)[:, None, :]
    shift_ref[...] = jnp.where(low, 0.0, left).astype(bf16)[:, None, :]
    rows_here = block_rows * tile_cols
    paired = (right[None] * scale_ref[...] + shift_ref[...]).reshape(rows_here, width)
    moved = jnp.dot(paired, w_pairout_ref[...], preferred_element_type=f32)
    pair_mid = (pair_ref[...].reshape(rows_here, width).astype(f32) + moved).astype(bf16)
    normed = normalize_rows(pair_mid)
    hidden = jnp.dot(normed, w_up_ref[...], preferred_element_type=f32).astype(bf16)
    hidden = jnp.maximum(hidden, 0)
    down = jnp.dot(hidden, w_down_ref[...], preferred_element_type=f32)
    out_ref[...] = (pair_mid.astype(f32) + down).astype(bf16).reshape(pair_ref.shape)


def whole(shape):
    return pl.BlockSpec(shape, lambda *_: (0,) * len(shape))


def pinned(value):
    return pltpu.with_memory_space_constraint(value, pltpu.HBM)


def params(mib=8):
    return pltpu.CompilerParams(vmem_limit_bytes=mib * 1024 * 1024)


def per_device(
    single, pair, residue_mask, w_bias, w_project, w_out, w_factors, w_pairout, w_up, w_down
):
    tile_rows, tile_cols, pair_width = pair.shape
    single_width = single.shape[1]
    width = w_project.shape[2]
    rows, cols = lax.axis_size("rows"), lax.axis_size("cols")
    heads = w_bias.shape[1]
    heads_here = heads // cols
    in_place = pl.BlockSpec(memory_space=pl.ANY)
    in_hbm = pl.BlockSpec(memory_space=pltpu.HBM)

    weight = jnp.transpose(w_project, (0, 2, 1)).reshape(4 * width, single_width)
    query, kv, gate_values = pl.pallas_call(
        project_kernel,
        out_shape=(
            jax.ShapeDtypeStruct((width, tile_rows), bf16),
            jax.ShapeDtypeStruct((2 * width, tile_rows), bf16),
            jax.ShapeDtypeStruct((width, tile_rows), f32),
        ),
        in_specs=[in_hbm, in_hbm],
        scratch_shapes=[
            pltpu.VMEM(single.shape, bf16),
            pltpu.VMEM(weight.shape, bf16),
            pltpu.SemaphoreType.DMA((2,)),
        ],
        compiler_params=params(),
        name="project",
    )(pinned(single), pinned(weight))

    shifts = rows // 4
    half = rows // 2

    def sent(value, target):
        return lax.ppermute(value, "rows", [(r, target(r)) for r in range(rows)])

    kv_other = sent(kv, lambda r: r ^ half)
    kv, w_bias = lax.optimization_barrier((kv, w_bias))

    bias_local = pl.pallas_call(
        bias_kernel,
        out_shape=jax.ShapeDtypeStruct((heads, tile_rows, tile_cols), bf16),
        in_specs=[in_hbm, in_hbm, in_hbm],
        scratch_shapes=[
            pltpu.VMEM(pair.shape, bf16),
            pltpu.VMEM((heads, pair_width), bf16),
            pltpu.VMEM((1, tile_cols), jnp.int32),
            pltpu.VMEM((heads, tile_rows // 4, tile_cols), f32),
            pltpu.SemaphoreType.DMA((6,)),
        ],
        compiler_params=params(24),
        name="bias",
    )(pinned(pair), pinned(jnp.transpose(w_bias)), pinned(residue_mask.reshape(cols, 1, tile_cols)))
    bias_local, kv_other = lax.optimization_barrier((bias_local, kv_other))
    bias_heads = lax.all_to_all(bias_local, "cols", 0, 0, tiled=True)

    both = jnp.stack([kv, kv_other])
    near = [both]
    for s in range(1, shifts):
        near.append(sent(both, lambda r: (r & half) | ((r + 2 * s) & (half - 1))))
    near = jnp.stack(near)
    kv_all = jnp.stack([near, sent(near, lambda r: r ^ 1)])

    mixed = pl.pallas_call(
        attend_kernel,
        out_shape=jax.ShapeDtypeStruct((cols, width, tile_rows), bf16),
        scratch_shapes=[pltpu.VMEM((cols, tile_rows, tile_cols), f32)],
        compiler_params=params(),
        name="attend",
    )(
        query,
        gate_values,
        bias_heads.reshape(cols, heads_here, tile_rows, tile_cols),
        kv_all,
    )
    mixed_all = lax.all_to_all(mixed, "cols", 0, 0, tiled=True).reshape(single_width, tile_rows)

    single_out, factors = pl.pallas_call(
        factor_kernel,
        out_shape=(
            jax.ShapeDtypeStruct(single.shape, bf16),
            jax.ShapeDtypeStruct((tile_rows, w_factors.shape[1]), bf16),
        ),
        in_specs=[whole((single_width, tile_rows)), in_place, in_place, in_place],
        scratch_shapes=[
            pltpu.VMEM(w_out.shape, bf16),
            pltpu.VMEM(single.shape, bf16),
            pltpu.VMEM(w_factors.shape, bf16),
            pltpu.SemaphoreType.DMA((6,)),
        ],
        compiler_params=params(),
        name="factor",
    )(mixed_all, pinned(w_out), single, w_factors)

    swapped = [(a * cols + b, b * cols + a) for a in range(rows) for b in range(cols)]
    right_factors = lax.ppermute(factors, ("rows", "cols"), swapped)

    block_rows = 32
    updated = pl.pallas_call(
        update_kernel,
        grid=(tile_rows // block_rows,),
        in_specs=[
            pl.BlockSpec((block_rows, tile_cols, pair_width), lambda i: (i, 0, 0)),
            pl.BlockSpec((block_rows, factors.shape[1]), lambda i: (i, 0)),
            whole(right_factors.shape),
            in_place,
            in_place,
            in_place,
        ],
        out_specs=pl.BlockSpec((block_rows, tile_cols, pair_width), lambda i: (i, 0, 0)),
        out_shape=jax.ShapeDtypeStruct(pair.shape, bf16),
        scratch_shapes=[
            pltpu.VMEM(w_pairout.shape, bf16),
            pltpu.VMEM(w_up.shape, bf16),
            pltpu.VMEM(w_down.shape, bf16),
            pltpu.VMEM((block_rows, 1, pair_width), bf16),
            pltpu.VMEM((block_rows, 1, pair_width), bf16),
            pltpu.SemaphoreType.DMA((3,)),
        ],
        compiler_params=params(20),
        name="update",
    )(pair, factors, right_factors, w_pairout, w_up, w_down)
    return (single_out, updated)


def solution(mesh):
    return jax.shard_map(
        per_device,
        mesh=mesh,
        in_specs=(
            P("rows", None),
            P("rows", "cols", None),
            P(),
            P(),
            P(None, None, "cols"),
            P(),
            P(),
            P(),
            P(),
            P(),
        ),
        out_specs=(P("rows", None), P("rows", "cols", None)),
        check_vma=False,
    )
```

time: 105 us -> 92.6 us (0.88)
  blocking collectives: 23.3 us -> 12.8 us
  local copies, waits for them, and re-layouts: 10.5 us -> 0.03 us
  waiting for transfers between devices: 26.1 us -> 31.3 us
  Pallas kernels: 23.2 us -> 27.1 us
    all_to_all x1, waiting for transfers between devices: 0.92 us -> 14.7 us  [per_device(): bias_heads = lax.all_to_all(bias_local, 'cols', 0, 0, tiled=True)]
    all_to_all x1, blocking collectives: 23.3 us -> 12.8 us  [per_device(): lax.all_to_all(mixed, 'cols', 0, 0, tiled=True)]
    unnamed x30 -> x12, local copies, waits for them, and re-layouts: 10.5 us -> 0.03 us
    ppermute x5, waiting for transfers between devices: 15.3 us -> 7 us  [sent(): return lax.ppermute(value, 'rows', [(r, target(r)) for r in range(rows)])]
    pallas_call x1, Pallas kernels: 1.39 us -> 2.77 us  [per_device(): pl.pallas_call(factor_kernel, out_shape=(jax.ShapeDtypeStruct(single.shap...]
  transfers between devices with their start and end apart: 7 -> 7, of which waited for: 6 -> 5; matrix products, arithmetic and copies ran while one was open for 1% -> 0% of each run, Pallas kernels for 0% -> 8%
where the time goes in v3:
time: 92.6 us; the launch traced here: 92.3 us
  waiting for transfers between devices  31.3 us (34%)
  Pallas kernels  27.1 us (29%)
  starting transfers between devices  20.1 us (22%)
  blocking collectives  12.8 us (14%)
    all_to_all x1, waiting for transfers between devices, per_device(): bias_heads = lax.all_to_all(bias_local, 'cols', 0, 0, tiled=True)  14.7 us
    pallas_call x1, Pallas kernels, per_device(): pl.pallas_call(update_kernel, grid=(tile_rows // block_rows,), in_specs=[...  14.1 us
    all_to_all x1, blocking collectives, per_device(): lax.all_to_all(mixed, 'cols', 0, 0, tiled=True)  12.8 us
    ppermute x1, waiting for transfers between devices, per_device(): right_factors = lax.ppermute(factors, ('rows', 'cols'), swapped)  9.53 us
    ppermute x5, starting transfers between devices, sent(): return lax.ppermute(value, 'rows', [(r, target(r)) for r in range(rows)])  9.08 us
    all_to_all x1, starting transfers between devices, per_device(): bias_heads = lax.all_to_all(bias_local, 'cols', 0, 0, tiled=True)  7.27 us
    ppermute x5, waiting for transfers between devices, sent(): return lax.ppermute(value, 'rows', [(r, target(r)) for r in range(rows)])  7 us
    pallas_call x1, Pallas kernels, per_device(): pl.pallas_call(bias_kernel, out_shape=jax.ShapeDtypeStruct((heads, tile_r...  6.99 us
  transfers between devices with their start and end apart: 7, of which 5 were waited for; matrix products, arithmetic and copies ran while one was open for 0% of the time, Pallas kernels for 8%

profile of v3, /device:TPU:88, one launch (start us, length us, event | category | flops | bytes accessed | tf_op | source)
XLA Modules:
  0.0 92.3 jit_solution(11359642953428966934)
XLA Ops:
  0.6 1.5 %project.1 = (bf16[64,128]{1,0:T(8,128)(2,1)S(1)}, bf16[128,128]{1,0:T(8,128)(2,1)S(1)}, f32[64,128]{1,0:T(8,128)S(1)}) custom-call(bf16[128,1024]{1,0:T(8,128)(2,1)} %single_hbm.3, bf16[256,1024]{1,0:T(8,128)(2,1)} %bitcast.20), custom_call_target="tpu_custom_call" | custom-call | tf_op jit(solution)/shard_map/project/pallas_call | solution.py:224
  2.2 5.5 %collective-permute-start = (bf16[128,128]{1,0:T(8,128)(2,1)S(1)}, bf16[128,128]{1,0:T(8,128)(2,1)S(1)}, u32[]{:S(2)}, u32[]{:S(2)}) collective-permute-start(bf16[128,128]{1,0:T(8,128)(2,1)S(1)} %get-tuple-element.16), channel_id=1, source_target_pairs={{0,128},{16,144},{32,160},{48,176},{64,192},{80,208},{96,224},{112... | collective-permute-start | bytes 98312 | tf_op jit(solution)/shard_map/ppermute | solution.py:245
  7.6 7.0 %bias.1 = bf16[32,128,128]{2,1,0:T(8,128)(2,1)} custom-call(bf16[128,128,128]{2,1,0:T(8,128)(2,1)} %pair_ref.1, bf16[32,128]{1,0:T(8,128)(2,1)} %bitcast.26, s32[16,1,128]{2,1,0:T(1,128)} %bitcast.27), custom_call_target="tpu_custom_call" | custom-call | tf_op jit(solution)/shard_map/bias/pallas_call | solution.py:250
  14.6 0.0 copy-start.1
  14.6 0.0 copy-start.2
  14.7 0.0 collective-permute-done
  14.7 7.3 %all-to-all-start = ((bf16[32,128,128]{2,1,0:T(8,128)(2,1)}), bf16[32,128,128]{2,1,0:T(8,128)(2,1)S(1)}, u32[]{:S(2)}, u32[]{:S(2)}) async-start(bf16[32,128,128]{2,1,0:T(8,128)(2,1)} %bias.1), calls=%async_computation | async-start | bytes 2097152 | tf_op jit(solution)/shard_map/all_to_all | solution.py:265
  21.9 0.0 copy-start.3
  21.9 0.0 copy-start.4
  22.0 0.0 copy-start.5
  22.0 1.3 %collective-permute-start.2 = (bf16[2,128,128]{2,1,0:T(8,128)(2,1)S(1)}, bf16[2,128,128]{2,1,0:T(8,128)(2,1)S(1)}, u32[]{:S(2)}, u32[]{:S(2)}) collective-permute-start(bf16[2,128,128]{2,1,0:T(8,128)(2,1)S(1)} %get-tuple-element.23), channel_id=1, source_target_pairs={{0,64},{16,80},{32,96},{48,112},{64,0},{80,16},{96,32},{112,48},{1... | collective-permute-start | bytes 196616 | tf_op jit(solution)/shard_map/ppermute | solution.py:245
  23.3 2.2 %collective-permute-start.1 = (bf16[2,128,128]{2,1,0:T(8,128)(2,1)S(1)}, bf16[2,128,128]{2,1,0:T(8,128)(2,1)S(1)}, u32[]{:S(2)}, u32[]{:S(2)}) collective-permute-start(bf16[2,128,128]{2,1,0:T(8,128)(2,1)S(1)} %get-tuple-element.23), channel_id=1, source_target_pairs={{0,32},{16,48},{32,64},{48,80},{64,96},{80,112},{96,0},{112,16},{1... | collective-permute-start | bytes 196616 | tf_op jit(solution)/shard_map/ppermute | solution.py:245
  25.5 0.0 collective-permute-start.3
  25.5 2.6 %collective-permute-done.2 = bf16[2,128,128]{2,1,0:T(8,128)(2,1)S(1)} collective-permute-done((bf16[2,128,128]{2,1,0:T(8,128)(2,1)S(1)}, bf16[2,128,128]{2,1,0:T(8,128)(2,1)S(1)}, u32[]{:S(2)}, u32[]{:S(2)}) %collective-permute-start.2) | collective-permute-done | bytes 65568 | tf_op jit(solution)/shard_map/ppermute | solution.py:245
  28.1 0.0 collective-permute-done.1
  28.1 2.9 %collective-permute-done.3 = bf16[2,128,128]{2,1,0:T(8,128)(2,1)S(1)} collective-permute-done((bf16[2,128,128]{2,1,0:T(8,128)(2,1)S(1)}, bf16[2,128,128]{2,1,0:T(8,128)(2,1)S(1)}, u32[]{:S(2)}, u32[]{:S(2)}) %collective-permute-start.3) | collective-permute-done | bytes 65568 | tf_op jit(solution)/shard_map/ppermute | solution.py:245
  31.0 0.1 collective-permute-start.4
  31.1 1.5 %collective-permute-done.4 = bf16[4,2,128,128]{3,2,1,0:T(8,128)(2,1)S(1)} collective-permute-done((bf16[4,2,128,128]{3,2,1,0:T(8,128)(2,1)S(1)}, bf16[4,2,128,128]{3,2,1,0:T(8,128)(2,1)S(1)}, u32[]{:S(2)}, u32[]{:S(2)}) %collective-permute-start.4) | collective-permute-done | bytes 262176 | tf_op jit(solution)/shard_map/ppermute | solution.py:245
  32.6 0.1 pad_maximum_fusion.kv_ref
  32.7 14.7 %all-to-all-done = bf16[32,128,128]{2,1,0:T(8,128)(2,1)S(1)} async-done(((bf16[32,128,128]{2,1,0:T(8,128)(2,1)}), bf16[32,128,128]{2,1,0:T(8,128)(2,1)S(1)}, u32[]{:S(2)}, u32[]{:S(2)}) %all-to-all-start) | async-done | bytes 1048608 | tf_op jit(solution)/shard_map/all_to_all | solution.py:265
  47.4 0.0 copy-start
  47.4 1.8 %attend.1 = bf16[16,64,128]{2,1,0:T(8,128)(2,1)S(1)} custom-call(bf16[64,128]{1,0:T(8,128)(2,1)S(1)} %get-tuple-element.11.query_ref, f32[64,128]{1,0:T(8,128)S(1)} %get-tuple-element.12.gate_ref, bf16[16,2,128,128]{3,2,1,0:T(8,128)(2,1)S(1)} %bitcast.17, bf16[2,4,2,128,128]{4,3,2,1,0:T(8,128)(2,1)S(1)} %pad_maximum_fusion.kv_ref), custom_call_target="tpu_custom_call" | custom-call | tf_op jit(solution)/shard_map/attend/pallas_call | solution.py:274
  49.2 12.8 %all_to_all.10 = bf16[16,64,128]{2,1,0:T(8,128)(2,1)S(1)} all-to-all(bf16[16,64,128]{2,1,0:T(8,128)(2,1)S(1)} %attend.1), channel_id=1, replica_groups=mesh['rows'=16,'cols'=16] {'cols'}, dimensions={0} | all-to-all | bytes 524288 | tf_op jit(solution)/shard_map/all_to_all | solution.py:286
  62.0 0.0 copy-done.1
  62.0 0.0 copy-done.2
  62.0 2.8 %factor.1 = (bf16[128,1024]{1,0:T(8,128)(2,1)}, bf16[128,128]{1,0:T(8,128)(2,1)S(1)}) custom-call(bf16[1024,128]{1,0:T(8,128)(2,1)S(1)} %bitcast.18, bf16[1024,1024]{1,0:T(8,128)(2,1)} %w_out_hbm.1, bf16[128,1024]{1,0:T(8,128)(2,1)S(1)} %copy-done.1, bf16[1024,128]{1,0:T(8,128)(2,1)S(1)} %copy-done.2), custom_call_target="tpu_custom_call" | custom-call | tf_op jit(solution)/shard_map/factor/pallas_call | solution.py:288
  64.8 3.8 %collective-permute-start.5 = (bf16[128,128]{1,0:T(8,128)(2,1)S(1)}, bf16[128,128]{1,0:T(8,128)(2,1)S(1)}, u32[]{:S(2)}, u32[]{:S(2)}) collective-permute-start(bf16[128,128]{1,0:T(8,128)(2,1)S(1)} %get-tuple-element.19.left_ref), channel_id=1, source_target_pairs={{0,0},{1,16},{2,32},{3,48},{4,64},{5,80},{6,96},{7,112},{8,128},{9... | collective-permute-start | bytes 98312 | tf_op jit(solution)/shard_map/ppermute | solution.py:306
  68.6 9.5 %collective-permute-done.5.right_ref = bf16[128,128]{1,0:T(8,128)(2,1)S(1)} collective-permute-done((bf16[128,128]{1,0:T(8,128)(2,1)S(1)}, bf16[128,128]{1,0:T(8,128)(2,1)S(1)}, u32[]{:S(2)}, u32[]{:S(2)}) %collective-permute-start.5) | collective-permute-done | bytes 32800 | tf_op jit(solution)/shard_map/ppermute | solution.py:306
  78.1 0.0 copy-done.3
  78.1 0.0 copy-done.4
  78.1 0.0 copy-done.5
  78.1 0.0 copy-done
  78.1 14.1 %update.1 = bf16[128,128,128]{2,1,0:T(8,128)(2,1)} custom-call(bf16[128,128,128]{2,1,0:T(8,128)(2,1)S(1)} %copy-done, bf16[128,128]{1,0:T(8,128)(2,1)S(1)} %get-tuple-element.19.left_ref, bf16[128,128]{1,0:T(8,128)(2,1)S(1)} %collective-permute-done.5.right_ref, bf16[128,128]{1,0:T(8,128)(2,1)S(1)} %copy-done.5, bf16[128,512]{1,0:T(8,128)(2,1)S(1)} %copy-done.3, ...), custom_call_target="tpu_custom_call" | custom-call | tf_op jit(solution)/shard_map/update/pallas_call | solution.py:309
  (2 shorter events, 0.1 us)
Async XLA Ops:
  2.2 12.5 %collective-permute-start = (bf16[128,128]{1,0:T(8,128)(2,1)S(1)}, bf16[128,128]{1,0:T(8,128)(2,1)S(1)}, u32[]{:S(2)}, u32[]{:S(2)}) collective-permute-start(bf16[128,128]{1,0:T(8,128)(2,1)S(1)} %get-tuple-element.16), channel_id=1, source_target_pairs={{0,128},{16,144},{32,160},{48,176},{64,192},{80,208},{96,224},{112... | collective-permute-start | bytes 98312 | tf_op jit(solution)/shard_map/ppermute | solution.py:245
  14.6 47.3 %copy-start.1 = (bf16[128,1024]{1,0:T(8,128)(2,1)S(1)}, bf16[128,1024]{1,0:T(8,128)(2,1)}, u32[]{:S(2)}) copy-start(bf16[128,1024]{1,0:T(8,128)(2,1)} %single_hbm.3) | copy-start | bytes 786436
  14.6 47.3 %copy-start.2 = (bf16[1024,128]{1,0:T(8,128)(2,1)S(1)}, bf16[1024,128]{1,0:T(8,128)(2,1)}, u32[]{:S(2)}) copy-start(bf16[1024,128]{1,0:T(8,128)(2,1)} %w_factors_hbm.1) | copy-start | bytes 786436
  14.7 32.8 %all-to-all-start = ((bf16[32,128,128]{2,1,0:T(8,128)(2,1)}), bf16[32,128,128]{2,1,0:T(8,128)(2,1)S(1)}, u32[]{:S(2)}, u32[]{:S(2)}) async-start(bf16[32,128,128]{2,1,0:T(8,128)(2,1)} %bias.1), calls=%async_computation | async-start | bytes 2097152 | tf_op jit(solution)/shard_map/all_to_all | solution.py:265
  21.9 56.1 %copy-start.3 = (bf16[128,512]{1,0:T(8,128)(2,1)S(1)}, bf16[128,512]{1,0:T(8,128)(2,1)}, u32[]{:S(2)}) copy-start(bf16[128,512]{1,0:T(8,128)(2,1)} %w_up_hbm.1) | copy-start | bytes 393220
  21.9 56.1 %copy-start.4 = (bf16[512,128]{1,0:T(8,128)(2,1)S(1)}, bf16[512,128]{1,0:T(8,128)(2,1)}, u32[]{:S(2)}) copy-start(bf16[512,128]{1,0:T(8,128)(2,1)} %w_down_hbm.1) | copy-start | bytes 393220
  22.0 56.1 %copy-start.5 = (bf16[128,128]{1,0:T(8,128)(2,1)S(1)}, bf16[128,128]{1,0:T(8,128)(2,1)}, u32[]{:S(2)}) copy-start(bf16[128,128]{1,0:T(8,128)(2,1)} %w_pairout_hbm.1) | copy-start | bytes 98308
  22.0 6.1 %collective-permute-start.2 = (bf16[2,128,128]{2,1,0:T(8,128)(2,1)S(1)}, bf16[2,128,128]{2,1,0:T(8,128)(2,1)S(1)}, u32[]{:S(2)}, u32[]{:S(2)}) collective-permute-start(bf16[2,128,128]{2,1,0:T(8,128)(2,1)S(1)} %get-tuple-element.23), channel_id=1, source_target_pairs={{0,64},{16,80},{32,96},{48,112},{64,0},{80,16},{96,32},{112,48},{1... | collective-permute-start | bytes 196616 | tf_op jit(solution)/shard_map/ppermute | solution.py:245
  23.3 4.8 %collective-permute-start.1 = (bf16[2,128,128]{2,1,0:T(8,128)(2,1)S(1)}, bf16[2,128,128]{2,1,0:T(8,128)(2,1)S(1)}, u32[]{:S(2)}, u32[]{:S(2)}) collective-permute-start(bf16[2,128,128]{2,1,0:T(8,128)(2,1)S(1)} %get-tuple-element.23), channel_id=1, source_target_pairs={{0,32},{16,48},{32,64},{48,80},{64,96},{80,112},{96,0},{112,16},{1... | collective-permute-start | bytes 196616 | tf_op jit(solution)/shard_map/ppermute | solution.py:245
  25.5 5.5 %collective-permute-start.3 = (bf16[2,128,128]{2,1,0:T(8,128)(2,1)S(1)}, bf16[2,128,128]{2,1,0:T(8,128)(2,1)S(1)}, u32[]{:S(2)}, u32[]{:S(2)}) collective-permute-start(bf16[2,128,128]{2,1,0:T(8,128)(2,1)S(1)} %get-tuple-element.23), channel_id=1, source_target_pairs={{0,96},{16,112},{32,0},{48,16},{64,32},{80,48},{96,64},{112,80},{1... | collective-permute-start | bytes 196616 | tf_op jit(solution)/shard_map/ppermute | solution.py:245
  31.0 1.6 %collective-permute-start.4 = (bf16[4,2,128,128]{3,2,1,0:T(8,128)(2,1)S(1)}, bf16[4,2,128,128]{3,2,1,0:T(8,128)(2,1)S(1)}, u32[]{:S(2)}, u32[]{:S(2)}) collective-permute-start(bf16[4,2,128,128]{3,2,1,0:T(8,128)(2,1)S(1)} %get-tuple-element.21), channel_id=1, source_target_pairs={{0,16},{16,0},{32,48},{48,32},{64,80},{80,64},{96,112},{112,96},{1... | collective-permute-start | bytes 786440 | tf_op jit(solution)/shard_map/ppermute | solution.py:245
  47.4 30.7 %copy-start = (bf16[128,128,128]{2,1,0:T(8,128)(2,1)S(1)}, bf16[128,128,128]{2,1,0:T(8,128)(2,1)}, u32[]{:S(2)}) copy-start(bf16[128,128,128]{2,1,0:T(8,128)(2,1)} %pair_ref.1) | copy-start | bytes 12582916
  64.8 13.3 %collective-permute-start.5 = (bf16[128,128]{1,0:T(8,128)(2,1)S(1)}, bf16[128,128]{1,0:T(8,128)(2,1)S(1)}, u32[]{:S(2)}, u32[]{:S(2)}) collective-permute-start(bf16[128,128]{1,0:T(8,128)(2,1)S(1)} %get-tuple-element.19.left_ref), channel_id=1, source_target_pairs={{0,0},{1,16},{2,32},{3,48},{4,64},{5,80},{6,96},{7,112},{8,128},{9... | collective-permute-start | bytes 98312 | tf_op jit(solution)/shard_map/ppermute | solution.py:306

commit v4 on v3

v4 whole, which is shorter than its diff:
```python
import functools
import math

import jax
import jax.numpy as jnp
from jax import lax
from jax.experimental import pallas as pl
from jax.experimental.pallas import tpu as pltpu
from jax.sharding import PartitionSpec as P

epsilon = 1e-05
f32 = jnp.float32
bf16 = jnp.bfloat16
lowest = -1e30


def normalize(values):
    centred = values - jnp.mean(values, -1, keepdims=True)
    return centred * lax.rsqrt(jnp.mean(centred * centred, -1, keepdims=True) + epsilon)


def nt_dot(a, b):
    return lax.dot_general(a, b, (((1,), (1,)), ((), ())), preferred_element_type=f32)


def start_copies(pairs, sems):
    copies = [pltpu.make_async_copy(a, b, sems.at[i]) for i, (a, b) in enumerate(pairs)]
    for copy in copies:
        copy.start()
    return copies


def project_kernel(
    single_hbm, weight_hbm, query_ref, kv_ref, single_ref, weight_ref, sems
):
    copies = start_copies(((single_hbm, single_ref), (weight_hbm, weight_ref)), sems)
    copies[0].wait()
    normed = normalize(single_ref[...].astype(f32)).astype(bf16)
    copies[1].wait()
    projected = nt_dot(weight_ref[...], normed)
    width = query_ref.shape[0] // 2
    query_ref[:width] = projected[:width].astype(bf16).astype(f32)
    query_ref[width:] = jax.nn.sigmoid(projected[3 * width :])
    kv_ref[...] = projected[width : 3 * width].astype(bf16)


def normalize_rows(rounded):
    values = rounded.astype(f32)
    width = values.shape[-1]
    centred = values - jnp.dot(
        rounded, jnp.full((width, width), 1.0 / width, bf16), preferred_element_type=f32
    )
    square = jnp.mean(centred * centred, -1, keepdims=True)
    return (centred * lax.rsqrt(square + epsilon)).astype(bf16)


def bias_kernel(
    pair_hbm,
    weight_hbm,
    mask_hbm,
    out_hbm,
    pair_ref,
    weight_ref,
    mask_ref,
    held_ref,
    staged_ref,
    sems,
    out_sems,
):
    tile_rows, tile_cols, width = pair_ref.shape
    targets, heads_there = staged_ref.shape[:2]
    pairs = heads_there // 2
    ends = [tile_rows // 4, 3 * tile_rows // 4, tile_rows]
    parts = [(weight_hbm, weight_ref), (mask_hbm.at[lax.axis_index("cols")], mask_ref)]
    at = 0
    for end in ends:
        rows_here = pl.ds(at, end - at)
        parts.append((pair_hbm.at[rows_here], pair_ref.at[rows_here]))
        at = end
    copies = start_copies(parts, sems)
    copies[0].wait()
    copies[1].wait()
    included = mask_ref[...] > 0
    at = 0
    outs = []
    for chunk, end in enumerate(ends):
        copies[2 + chunk].wait()
        step = end - at
        normed = normalize_rows(pair_ref[at:end].reshape(step * tile_cols, width))
        both = nt_dot(weight_ref[...], normed)
        for i in range(step):
            held_ref[:, i, :] = both[:, i * tile_cols : (i + 1) * tile_cols]
        held = jnp.where(included[None], held_ref[:, :step, :], lowest).astype(bf16)
        for d in range(targets):
            for p in range(heads_there // pairs):
                first = p * targets * pairs + d * pairs
                staged_ref[d, p * pairs : (p + 1) * pairs, at:end] = held[first : first + pairs]
        rows_here = pl.ds(at, step)
        out = pltpu.make_async_copy(
            staged_ref.at[:, :, rows_here], out_hbm.at[:, :, rows_here], out_sems.at[chunk]
        )
        out.start()
        outs.append(out)
        at = end
    for out in outs:
        out.wait()


def attend_kernel(own_ref, other_ref, bias_ref, near_ref, far_ref, out_ref, score_ref):
    blocks, heads_there, tile_rows, tile_cols = bias_ref.shape
    width = own_ref.shape[0] // 2
    pairs = heads_there // 2
    head_width = width // pairs
    score_scale = 1.0 / math.sqrt(head_width)
    shifts = near_ref.shape[0]
    row, col = lax.axis_index("rows"), lax.axis_index("cols")
    half, turn, core = row // (2 * shifts), (row // 2) % shifts, row % 2
    second = col // blocks

    def block(b, z, part):
        sent = (turn + shifts - b // 2) % shifts
        near, far = near_ref[sent, half ^ z, part, :], far_ref[sent, half ^ z, part, :]
        return jnp.where(core == b % 2, near, far)

    own, other = own_ref[...], other_ref[...]
    attended, gates, sums = [], [], []
    for z in range(2):
        here = jnp.where(second == z, own, other)
        query = jnp.transpose(here[:width]).astype(bf16)
        gates.append(here[width:])
        for h in range(pairs):
            query_head = query[:, h * head_width : (h + 1) * head_width]
            key_rows = pl.ds(h * head_width, head_width)
            value_rows = pl.ds(width + h * head_width, head_width)
            top = None
            for b in range(blocks):
                scores = jnp.dot(query_head, block(b, z, key_rows), preferred_element_type=f32)
                scores = scores * score_scale + bias_ref[b, z * pairs + h].astype(f32)
                score_ref[b] = scores
                top = scores if top is None else jnp.maximum(top, scores)
            top = jnp.max(top, axis=-1, keepdims=True)
            total = mixed = None
            for b in range(blocks):
                weights = jnp.exp(score_ref[b] - top)
                part = nt_dot(weights.astype(bf16), block(b, z, value_rows))
                total = weights if total is None else total + weights
                mixed = part if mixed is None else mixed + part
            total = jnp.sum(total, axis=-1, keepdims=True)
            attended.append(mixed / total)
            sums.append(top + jnp.log(total))
    gated = jnp.transpose(jnp.concatenate(attended, axis=1)) * jnp.concatenate(gates, axis=0)
    lane = lax.broadcasted_iota(jnp.int32, (tile_rows, 128), 1)
    coded = jnp.zeros((tile_rows, 128), f32)
    for h, value in enumerate(sums):
        for p in range(3):
            part = value.astype(bf16).astype(f32)
            value = value - part
            coded = jnp.where(lane == p * heads_there + h, part, coded)
    coded = jnp.transpose(coded)[: out_ref.shape[1] - 2 * width]
    gated, coded = gated.astype(bf16), coded.astype(bf16)
    for d in range(out_ref.shape[0]):
        out_ref[d, : 2 * width] = gated
        out_ref[d, 2 * width :] = coded


def factor_kernel(
    sent_ref,
    w_out_ref,
    single_hbm,
    w_factors_hbm,
    out_ref,
    factors_ref,
    mixed_ref,
    single_ref,
    w_factors_ref,
    sems,
):
    copies = start_copies(((single_hbm, single_ref), (w_factors_hbm, w_factors_ref)), sems)
    targets = sent_ref.shape[0] // 2
    width = mixed_ref.shape[0] // sent_ref.shape[0]
    heads_there = 4
    head_width = 2 * width // heads_there

    def log_sum(d):
        coded = sent_ref[d, 2 * width :].astype(f32)
        parts = [coded[p * heads_there : (p + 1) * heads_there] for p in range(3)]
        return parts[0] + parts[1] + parts[2]

    for d in range(targets):
        first, last = log_sum(d), log_sum(d + targets)
        top = jnp.maximum(first, last)
        first, last = jnp.exp(first - top), jnp.exp(last - top)
        inverse = 1.0 / (first + last)
        first, last = first * inverse, last * inverse
        for h in range(heads_there):
            rows_here = pl.ds(h * head_width, head_width)
            joined = (
                sent_ref[d, rows_here].astype(f32) * first[h : h + 1]
                + sent_ref[d + targets, rows_here].astype(f32) * last[h : h + 1]
            )
            owner = (h * head_width // width) * targets + d
            place = owner * width + h * head_width % width
            mixed_ref[place : place + head_width] = joined.astype(bf16)
    mixed = jnp.transpose(mixed_ref[...].astype(f32)).astype(bf16)
    head_total = jnp.dot(mixed, w_out_ref[...], preferred_element_type=f32)
    copies[0].wait()
    single_out = (single_ref[...].astype(f32) + head_total).astype(bf16)
    out_ref[...] = single_out
    normed = normalize(single_out.astype(f32)).astype(bf16)
    copies[1].wait()
    factors_ref[...] = jnp.dot(normed, w_factors_ref[...], preferred_element_type=f32).astype(bf16)


def update_kernel(
    pair_ref,
    left_ref,
    right_ref,
    w_pairout_hbm,
    w_up_hbm,
    w_down_hbm,
    out_ref,
    w_pairout_ref,
    w_up_ref,
    w_down_ref,
    scale_ref,
    shift_ref,
    sems,
):
    copies = [
        pltpu.make_async_copy(w_pairout_hbm, w_pairout_ref, sems.at[0]),
        pltpu.make_async_copy(w_up_hbm, w_up_ref, sems.at[1]),
        pltpu.make_async_copy(w_down_hbm, w_down_ref, sems.at[2]),
    ]

    @pl.when(pl.program_id(0) == 0)
    def _():
        for copy in copies:
            copy.start()

    block_rows, tile_cols, width = pair_ref.shape
    factor_width = width // 2
    low = lax.broadcasted_iota(jnp.int32, (1, width), 1) < factor_width
    right = right_ref[:, factor_width:]
    right = jnp.concatenate([right, right], axis=1)
    left = left_ref[:, :factor_width].astype(f32)
    left = jnp.concatenate([left, left], axis=1)
    scale_ref[...] = jnp.where(low, left, -1.0).astype(bf16)[:, None, :]
    shift_ref[...] = jnp.where(low, 0.0, left).astype(bf16)[:, None, :]
    rows_here = block_rows * tile_cols
    paired = (right[None] * scale_ref[...] + shift_ref[...]).reshape(rows_here, width)

    @pl.when(pl.program_id(0) == 0)
    def _():
        for copy in copies:
            copy.wait()

    moved = jnp.dot(paired, w_pairout_ref[...], preferred_element_type=f32)
    pair_mid = (pair_ref[...].reshape(rows_here, width).astype(f32) + moved).astype(bf16)
    normed = normalize_rows(pair_mid)
    hidden = jnp.dot(normed, w_up_ref[...], preferred_element_type=f32).astype(bf16)
    hidden = jnp.maximum(hidden, 0)
    down = jnp.dot(hidden, w_down_ref[...], preferred_element_type=f32)
    out_ref[...] = (pair_mid.astype(f32) + down).astype(bf16).reshape(pair_ref.shape)


def whole(shape):
    return pl.BlockSpec(shape, lambda *_: (0,) * len(shape))


def pinned(value):
    return pltpu.with_memory_space_constraint(value, pltpu.HBM)


def params(mib=8):
    return pltpu.CompilerParams(vmem_limit_bytes=mib * 1024 * 1024)


def per_device(
    single, pair, residue_mask, w_bias, w_project, w_out, w_factors, w_pairout, w_up, w_down
):
    tile_rows, tile_cols, pair_width = pair.shape
    single_width = single.shape[1]
    width = w_project.shape[2]
    rows, cols = lax.axis_size("rows"), lax.axis_size("cols")
    heads = w_bias.shape[1]
    in_place = pl.BlockSpec(memory_space=pl.ANY)
    in_hbm = pl.BlockSpec(memory_space=pltpu.HBM)

    shifts = rows // 4
    half_rows, half_cols = rows // 2, cols // 2
    both_axes = ("rows", "cols")

    def sent(value, axes, target):
        if axes == "rows":
            routes = [(r, target(r)) for r in range(rows)]
        elif axes == "cols":
            routes = [(c, target(c)) for c in range(cols)]
        else:
            routes = []
            for r in range(rows):
                for c in range(cols):
                    to_row, to_col = target(r, c)
                    routes.append((r * cols + c, to_row * cols + to_col))
        return lax.ppermute(value, axes, routes)

    def rerouted(flip):
        def target(r, c):
            z_row, z_col = r // half_rows, c // half_cols
            return (z_col ^ flip) * half_rows + r % half_rows, z_row * half_cols + c % half_cols

        return target

    weight = jnp.transpose(w_project, (0, 2, 1)).reshape(4 * width, single_width)
    query, kv = pl.pallas_call(
        project_kernel,
        out_shape=(
            jax.ShapeDtypeStruct((2 * width, tile_rows), f32),
            jax.ShapeDtypeStruct((2 * width, tile_rows), bf16),
        ),
        in_specs=[in_hbm, in_hbm],
        scratch_shapes=[
            pltpu.VMEM(single.shape, bf16),
            pltpu.VMEM(weight.shape, bf16),
            pltpu.SemaphoreType.DMA((2,)),
        ],
        compiler_params=params(),
        name="project",
    )(pinned(single), pinned(weight))

    kv_first = sent(kv, both_axes, rerouted(0))
    kv_last = sent(kv, both_axes, rerouted(1))
    kv, w_bias = lax.optimization_barrier((kv, w_bias))

    heads_there = 2 * heads // cols
    sent_shape = (half_cols, heads_there, tile_rows, tile_cols)
    bias_local = pl.pallas_call(
        bias_kernel,
        out_shape=jax.ShapeDtypeStruct(sent_shape, bf16),
        in_specs=[in_hbm, in_hbm, in_hbm],
        out_specs=in_place,
        scratch_shapes=[
            pltpu.VMEM(pair.shape, bf16),
            pltpu.VMEM((heads, pair_width), bf16),
            pltpu.VMEM((1, tile_cols), jnp.int32),
            pltpu.VMEM((heads, tile_rows // 2, tile_cols), f32),
            pltpu.VMEM(sent_shape, bf16),
            pltpu.SemaphoreType.DMA((5,)),
            pltpu.SemaphoreType.DMA((3,)),
        ],
        compiler_params=params(28),
        name="bias",
    )(pinned(pair), pinned(jnp.transpose(w_bias)), pinned(residue_mask.reshape(cols, 1, tile_cols)))
    bias_local, kv_first, kv_last = lax.optimization_barrier((bias_local, kv_first, kv_last))
    groups = [list(range(half_cols)), list(range(half_cols, cols))]
    bias_heads = lax.all_to_all(bias_local, "cols", 0, 0, axis_index_groups=groups, tiled=True)

    both = jnp.stack([kv_first, kv_last])
    near = [both]
    for s in range(1, shifts):
        around = lambda r: (r & half_rows) | ((r + 2 * s) & (half_rows - 1))
        near.append(sent(both, "rows", around))
    near = jnp.stack(near)
    query, near = lax.optimization_barrier((query, near))
    far = sent(near, "rows", lambda r: r ^ 1)
    query_other = sent(query, "cols", lambda c: c ^ half_cols)

    mixed = pl.pallas_call(
        attend_kernel,
        out_shape=jax.ShapeDtypeStruct((cols, 2 * width + 16, tile_rows), bf16),
        scratch_shapes=[pltpu.VMEM((half_cols, tile_rows, tile_cols), f32)],
        compiler_params=params(),
        name="attend",
    )(query, query_other, bias_heads, near, far)
    mixed_all = lax.all_to_all(mixed, "cols", 0, 0, tiled=True)

    single_out, factors = pl.pallas_call(
        factor_kernel,
        out_shape=(
            jax.ShapeDtypeStruct(single.shape, bf16),
            jax.ShapeDtypeStruct((tile_rows, w_factors.shape[1]), bf16),
        ),
        in_specs=[whole(mixed_all.shape), whole(w_out.shape), in_hbm, in_hbm],
        scratch_shapes=[
            pltpu.VMEM((single_width, tile_rows), bf16),
            pltpu.VMEM(single.shape, bf16),
            pltpu.VMEM(w_factors.shape, bf16),
            pltpu.SemaphoreType.DMA((2,)),
        ],
        compiler_params=params(),
        name="factor",
    )(mixed_all, w_out, pinned(single), pinned(w_factors))

    swapped = [(a * cols + b, b * cols + a) for a in range(rows) for b in range(cols)]
    right_factors = lax.ppermute(factors, ("rows", "cols"), swapped)

    block_rows = 32
    updated = pl.pallas_call(
        update_kernel,
        grid=(tile_rows // block_rows,),
        in_specs=[
            pl.BlockSpec((block_rows, tile_cols, pair_width), lambda i: (i, 0, 0)),
            pl.BlockSpec((block_rows, factors.shape[1]), lambda i: (i, 0)),
            whole(right_factors.shape),
            in_place,
            in_place,
            in_place,
        ],
        out_specs=pl.BlockSpec((block_rows, tile_cols, pair_width), lambda i: (i, 0, 0)),
        out_shape=jax.ShapeDtypeStruct(pair.shape, bf16),
        scratch_shapes=[
            pltpu.VMEM(w_pairout.shape, bf16),
            pltpu.VMEM(w_up.shape, bf16),
            pltpu.VMEM(w_down.shape, bf16),
            pltpu.VMEM((block_rows, 1, pair_width), bf16),
            pltpu.VMEM((block_rows, 1, pair_width), bf16),
            pltpu.SemaphoreType.DMA((3,)),
        ],
        compiler_params=params(20),
        name="update",
    )(pair, factors, right_factors, pinned(w_pairout), pinned(w_up), pinned(w_down))
    return (single_out, updated)


def solution(mesh):
    return jax.shard_map(
        per_device,
        mesh=mesh,
        in_specs=(
            P("rows", None),
            P("rows", "cols", None),
            P(),
            P(),
            P(None, None, "cols"),
            P(),
            P(),
            P(),
            P(),
            P(),
        ),
        out_specs=(P("rows", None), P("rows", "cols", None)),
        check_vma=False,
    )
```

time: 92.6 us -> 96.1 us (1.038)
  blocking collectives: 12.8 us -> 25.3 us
  waiting for transfers between devices: 31.3 us -> 22.1 us
  local copies, waits for them, and re-layouts: 0.03 us -> 1.66 us
  starting transfers between devices: 20.1 us -> 18.6 us
    all_to_all x1, waiting for transfers between devices: 14.7 us -> 0.01 us  [per_device(): lax.all_to_all(bias_local, 'cols', 0, 0, axis_index_groups=groups, tiled=...]
    all_to_all x1, blocking collectives: 12.8 us -> 25.3 us  [per_device(): mixed_all = lax.all_to_all(mixed, 'cols', 0, 0, tiled=True)]
    ppermute x5 -> x7, waiting for transfers between devices: 7 us -> 10.9 us  [sent(): return lax.ppermute(value, axes, routes)]
    ppermute x5 -> x7, starting transfers between devices: 9.08 us -> 11.6 us  [sent(): return lax.ppermute(value, axes, routes)]
    all_to_all x1, starting transfers between devices: 7.27 us -> 4.9 us  [per_device(): lax.all_to_all(bias_local, 'cols', 0, 0, axis_index_groups=groups, tiled=...]
    ppermute x1, starting transfers between devices: 3.79 us -> 2.1 us  [per_device(): right_factors = lax.ppermute(factors, ('rows', 'cols'), swapped)]
    ppermute x1, waiting for transfers between devices: 9.53 us -> 11.2 us  [per_device(): right_factors = lax.ppermute(factors, ('rows', 'cols'), swapped)]
    unnamed x12 -> x8, local copies, waits for them, and re-layouts: 0.03 us -> 1.66 us
  transfers between devices with their start and end apart: 7 -> 9, of which waited for: 5 -> 4; matrix products, arithmetic and copies ran while one was open for 0% -> 0% of each run, Pallas kernels for 8% -> 7%
where the time goes in v4:
time: 96.1 us; the launch traced here: 95.8 us
  Pallas kernels  27.1 us (28%)
  blocking collectives  25.3 us (26%)
  waiting for transfers between devices  22.1 us (23%)
  starting transfers between devices  18.6 us (19%)
  local copies, waits for them, and re-layouts  1.66 us (2%)
    all_to_all x1, blocking collectives, per_device(): mixed_all = lax.all_to_all(mixed, 'cols', 0, 0, tiled=True)  25.3 us
    pallas_call x1, Pallas kernels, per_device(): pl.pallas_call(update_kernel, grid=(tile_rows // block_rows,), in_specs=[...  15 us
    ppermute x7, starting transfers between devices, sent(): return lax.ppermute(value, axes, routes)  11.6 us
    ppermute x1, waiting for transfers between devices, per_device(): right_factors = lax.ppermute(factors, ('rows', 'cols'), swapped)  11.2 us
    ppermute x7, waiting for transfers between devices, sent(): return lax.ppermute(value, axes, routes)  10.9 us
    pallas_call x1, Pallas kernels, per_device(): pl.pallas_call(bias_kernel, out_shape=jax.ShapeDtypeStruct(sent_shape, bf...  6.62 us
    all_to_all x1, starting transfers between devices, per_device(): lax.all_to_all(bias_local, 'cols', 0, 0, axis_index_groups=groups, tiled=...  4.9 us
    pallas_call x1, Pallas kernels, per_device(): pl.pallas_call(factor_kernel, out_shape=(jax.ShapeDtypeStruct(single.shap...  2.32 us
  transfers between devices with their start and end apart: 9, of which 4 were waited for; matrix products, arithmetic and copies ran while one was open for 0% of the time, Pallas kernels for 7%

profile of v4, /device:TPU:88, one launch (start us, length us, event | category | flops | bytes accessed | tf_op | source)
XLA Modules:
  0.0 95.8 jit_solution(17146082140190667794)
XLA Ops:
  0.6 1.5 %project.1 = (f32[128,128]{1,0:T(8,128)S(1)}, bf16[128,128]{1,0:T(8,128)(2,1)S(1)}) custom-call(bf16[128,1024]{1,0:T(8,128)(2,1)} %single_hbm.3, bf16[256,1024]{1,0:T(8,128)(2,1)} %bitcast.12), custom_call_target="tpu_custom_call" | custom-call | tf_op jit(solution)/shard_map/project/pallas_call | solution.py:314
  2.2 0.1 collective-permute-start.1
  2.2 7.8 %collective-permute-start = (bf16[128,128]{1,0:T(8,128)(2,1)S(1)}, bf16[128,128]{1,0:T(8,128)(2,1)S(1)}, u32[]{:S(2)}, u32[]{:S(2)}) collective-permute-start(bf16[128,128]{1,0:T(8,128)(2,1)S(1)} %get-tuple-element.13), channel_id=1, source_target_pairs={{0,0},{1,1},{2,2},{3,3},{4,4},{5,5},{6,6},{7,7},{8,128},{9,129},{1... | collective-permute-start | bytes 98312 | tf_op jit(solution)/shard_map/ppermute | solution.py:304
  10.1 6.6 %bias.1 = bf16[8,4,128,128]{3,2,1,0:T(8,128)(2,1)} custom-call(bf16[128,128,128]{2,1,0:T(8,128)(2,1)} %pair_ref.1, bf16[32,128]{1,0:T(8,128)(2,1)} %bitcast.18, s32[16,1,128]{2,1,0:T(1,128)} %bitcast.19), custom_call_target="tpu_custom_call" | custom-call | tf_op jit(solution)/shard_map/bias/pallas_call | solution.py:336
  16.7 0.0 copy-start.1
  16.7 0.0 collective-permute-done.1
  16.7 0.0 collective-permute-done
  16.8 4.9 %all-to-all-start = ((bf16[8,4,128,128]{3,2,1,0:T(8,128)(2,1)}), bf16[8,4,128,128]{3,2,1,0:T(8,128)(2,1)S(1)}, u32[]{:S(2)}, u32[]{:S(2)}) async-start(bf16[8,4,128,128]{3,2,1,0:T(8,128)(2,1)} %bias.1), calls=%async_computation | async-start | bytes 2097152 | tf_op jit(solution)/shard_map/all_to_all | solution.py:355
  21.7 1.3 %collective-permute-start.3 = (bf16[2,128,128]{2,1,0:T(8,128)(2,1)S(1)}, bf16[2,128,128]{2,1,0:T(8,128)(2,1)S(1)}, u32[]{:S(2)}, u32[]{:S(2)}) collective-permute-start(bf16[2,128,128]{2,1,0:T(8,128)(2,1)S(1)} %get-tuple-element.23), channel_id=1, source_target_pairs={{0,64},{16,80},{32,96},{48,112},{64,0},{80,16},{96,32},{112,48},{1... | collective-permute-start | bytes 196616 | tf_op jit(solution)/shard_map/ppermute | solution.py:304
  23.0 2.2 %collective-permute-start.2 = (bf16[2,128,128]{2,1,0:T(8,128)(2,1)S(1)}, bf16[2,128,128]{2,1,0:T(8,128)(2,1)S(1)}, u32[]{:S(2)}, u32[]{:S(2)}) collective-permute-start(bf16[2,128,128]{2,1,0:T(8,128)(2,1)S(1)} %get-tuple-element.23), channel_id=1, source_target_pairs={{0,32},{16,48},{32,64},{48,80},{64,96},{80,112},{96,0},{112,16},{1... | collective-permute-start | bytes 196616 | tf_op jit(solution)/shard_map/ppermute | solution.py:304
  25.2 0.0 collective-permute-start.4
  25.2 2.6 %collective-permute-done.3 = bf16[2,128,128]{2,1,0:T(8,128)(2,1)S(1)} collective-permute-done((bf16[2,128,128]{2,1,0:T(8,128)(2,1)S(1)}, bf16[2,128,128]{2,1,0:T(8,128)(2,1)S(1)}, u32[]{:S(2)}, u32[]{:S(2)}) %collective-permute-start.3) | collective-permute-done | bytes 65568 | tf_op jit(solution)/shard_map/ppermute | solution.py:304
  27.8 0.0 collective-permute-done.2
  27.8 2.9 %collective-permute-done.4 = bf16[2,128,128]{2,1,0:T(8,128)(2,1)S(1)} collective-permute-done((bf16[2,128,128]{2,1,0:T(8,128)(2,1)S(1)}, bf16[2,128,128]{2,1,0:T(8,128)(2,1)S(1)}, u32[]{:S(2)}, u32[]{:S(2)}) %collective-permute-start.4) | collective-permute-done | bytes 65568 | tf_op jit(solution)/shard_map/ppermute | solution.py:304
  30.7 0.1 collective-permute-start.6
  30.8 0.1 collective-permute-start.5
  30.9 5.4 %collective-permute-done.5.other_ref = f32[128,128]{1,0:T(8,128)S(1)} collective-permute-done((f32[128,128]{1,0:T(8,128)S(1)}, f32[128,128]{1,0:T(8,128)S(1)}, u32[]{:S(2)}, u32[]{:S(2)}) %collective-permute-start.5) | collective-permute-done | bytes 65568 | tf_op jit(solution)/shard_map/ppermute | solution.py:304
  36.3 0.0 collective-permute-done.6.far_ref
  36.3 0.0 copy-start.2
  36.3 0.7 copy-done.2
  37.0 0.0 all-to-all-done.bias_ref
  37.0 0.0 copy-start.3
  37.0 0.9 copy-done.3
  38.0 0.0 copy-start
  38.0 1.7 %attend.1 = bf16[16,144,128]{2,1,0:T(8,128)(2,1)S(1)} custom-call(f32[128,128]{1,0:T(8,128)S(1)} %get-tuple-element.17.own_ref, f32[128,128]{1,0:T(8,128)S(1)} %collective-permute-done.5.other_ref, bf16[8,4,128,128]{3,2,1,0:T(8,128)(2,1)S(1)} %all-to-all-done.bias_ref, bf16[4,2,128,128]{3,2,1,0:T(8,128)(2,1)S(1)} %pad_maximum_fusion.near_ref, ...), custom_call_target="tpu_custom_call" | custom-call | tf_op jit(solution)/shard_map/attend/pallas_call | solution.py:367
  39.6 25.3 %all_to_all.10.sent_ref = bf16[16,144,128]{2,1,0:T(8,128)(2,1)S(1)} all-to-all(bf16[16,144,128]{2,1,0:T(8,128)(2,1)S(1)} %attend.1), channel_id=1, replica_groups=mesh['rows'=16,'cols'=16] {'cols'}, dimensions={0} | all-to-all | bytes 1179648 | tf_op jit(solution)/shard_map/all_to_all | solution.py:374
  65.0 0.0 copy-done.1
  65.0 2.3 %factor.1 = (bf16[128,1024]{1,0:T(8,128)(2,1)}, bf16[128,128]{1,0:T(8,128)(2,1)S(1)}) custom-call(bf16[16,144,128]{2,1,0:T(8,128)(2,1)S(1)} %all_to_all.10.sent_ref, bf16[1024,1024]{1,0:T(8,128)(2,1)S(1)} %copy-done.1, bf16[128,1024]{1,0:T(8,128)(2,1)} %single_hbm.3, bf16[1024,128]{1,0:T(8,128)(2,1)} %w_factors_hbm.1), custom_call_target="tpu_custom_call" | custom-call | tf_op jit(solution)/shard_map/factor/pallas_call | solution.py:376
  67.3 2.1 %collective-permute-start.7 = (bf16[128,128]{1,0:T(8,128)(2,1)S(1)}, bf16[128,128]{1,0:T(8,128)(2,1)S(1)}, u32[]{:S(2)}, u32[]{:S(2)}) collective-permute-start(bf16[128,128]{1,0:T(8,128)(2,1)S(1)} %get-tuple-element.21.left_ref), channel_id=1, source_target_pairs={{0,0},{1,16},{2,32},{3,48},{4,64},{5,80},{6,96},{7,112},{8,128},{9... | collective-permute-start | bytes 98312 | tf_op jit(solution)/shard_map/ppermute | solution.py:394
  69.4 11.2 %collective-permute-done.7.right_ref = bf16[128,128]{1,0:T(8,128)(2,1)S(1)} collective-permute-done((bf16[128,128]{1,0:T(8,128)(2,1)S(1)}, bf16[128,128]{1,0:T(8,128)(2,1)S(1)}, u32[]{:S(2)}, u32[]{:S(2)}) %collective-permute-start.7) | collective-permute-done | bytes 32800 | tf_op jit(solution)/shard_map/ppermute | solution.py:394
  80.7 0.0 copy-done
  80.7 15.0 %update.1 = bf16[128,128,128]{2,1,0:T(8,128)(2,1)} custom-call(bf16[128,128,128]{2,1,0:T(8,128)(2,1)S(1)} %copy-done, bf16[128,128]{1,0:T(8,128)(2,1)S(1)} %get-tuple-element.21.left_ref, bf16[128,128]{1,0:T(8,128)(2,1)S(1)} %collective-permute-done.7.right_ref, bf16[128,128]{1,0:T(8,128)(2,1)} %w_pairout_hbm.1, bf16[128,512]{1,0:T(8,128)(2,1)} %w_up_hbm.1, ...), custom_call_target="tpu_custom_call" | custom-call | tf_op jit(solution)/shard_map/update/pallas_call | solution.py:397
  (2 shorter events, 0.0 us)
Async XLA Ops:
  2.2 14.6 %collective-permute-start.1 = (bf16[128,128]{1,0:T(8,128)(2,1)S(1)}, bf16[128,128]{1,0:T(8,128)(2,1)S(1)}, u32[]{:S(2)}, u32[]{:S(2)}) collective-permute-start(bf16[128,128]{1,0:T(8,128)(2,1)S(1)} %get-tuple-element.13), channel_id=1, source_target_pairs={{0,128},{1,129},{2,130},{3,131},{4,132},{5,133},{6,134},{7,135},{8... | collective-permute-start | bytes 98312 | tf_op jit(solution)/shard_map/ppermute | solution.py:304
  2.2 14.5 %collective-permute-start = (bf16[128,128]{1,0:T(8,128)(2,1)S(1)}, bf16[128,128]{1,0:T(8,128)(2,1)S(1)}, u32[]{:S(2)}, u32[]{:S(2)}) collective-permute-start(bf16[128,128]{1,0:T(8,128)(2,1)S(1)} %get-tuple-element.13), channel_id=1, source_target_pairs={{0,0},{1,1},{2,2},{3,3},{4,4},{5,5},{6,6},{7,7},{8,128},{9,129},{1... | collective-permute-start | bytes 98312 | tf_op jit(solution)/shard_map/ppermute | solution.py:304
  16.7 48.3 %copy-start.1 = (bf16[1024,1024]{1,0:T(8,128)(2,1)S(1)}, bf16[1024,1024]{1,0:T(8,128)(2,1)}, u32[]{:S(2)}) copy-start(bf16[1024,1024]{1,0:T(8,128)(2,1)} %w_out_ref.1) | copy-start | bytes 6291460
  16.8 20.2 %all-to-all-start = ((bf16[8,4,128,128]{3,2,1,0:T(8,128)(2,1)}), bf16[8,4,128,128]{3,2,1,0:T(8,128)(2,1)S(1)}, u32[]{:S(2)}, u32[]{:S(2)}) async-start(bf16[8,4,128,128]{3,2,1,0:T(8,128)(2,1)} %bias.1), calls=%async_computation | async-start | bytes 2097152 | tf_op jit(solution)/shard_map/all_to_all | solution.py:355
  21.7 6.1 %collective-permute-start.3 = (bf16[2,128,128]{2,1,0:T(8,128)(2,1)S(1)}, bf16[2,128,128]{2,1,0:T(8,128)(2,1)S(1)}, u32[]{:S(2)}, u32[]{:S(2)}) collective-permute-start(bf16[2,128,128]{2,1,0:T(8,128)(2,1)S(1)} %get-tuple-element.23), channel_id=1, source_target_pairs={{0,64},{16,80},{32,96},{48,112},{64,0},{80,16},{96,32},{112,48},{1... | collective-permute-start | bytes 196616 | tf_op jit(solution)/shard_map/ppermute | solution.py:304
  23.0 4.8 %collective-permute-start.2 = (bf16[2,128,128]{2,1,0:T(8,128)(2,1)S(1)}, bf16[2,128,128]{2,1,0:T(8,128)(2,1)S(1)}, u32[]{:S(2)}, u32[]{:S(2)}) collective-permute-start(bf16[2,128,128]{2,1,0:T(8,128)(2,1)S(1)} %get-tuple-element.23), channel_id=1, source_target_pairs={{0,32},{16,48},{32,64},{48,80},{64,96},{80,112},{96,0},{112,16},{1... | collective-permute-start | bytes 196616 | tf_op jit(solution)/shard_map/ppermute | solution.py:304
  25.2 5.5 %collective-permute-start.4 = (bf16[2,128,128]{2,1,0:T(8,128)(2,1)S(1)}, bf16[2,128,128]{2,1,0:T(8,128)(2,1)S(1)}, u32[]{:S(2)}, u32[]{:S(2)}) collective-permute-start(bf16[2,128,128]{2,1,0:T(8,128)(2,1)S(1)} %get-tuple-element.23), channel_id=1, source_target_pairs={{0,96},{16,112},{32,0},{48,16},{64,32},{80,48},{96,64},{112,80},{1... | collective-permute-start | bytes 196616 | tf_op jit(solution)/shard_map/ppermute | solution.py:304
  30.7 5.6 %collective-permute-start.6 = (bf16[4,2,128,128]{3,2,1,0:T(8,128)(2,1)S(1)}, bf16[4,2,128,128]{3,2,1,0:T(8,128)(2,1)S(1)}, u32[]{:S(2)}, u32[]{:S(2)}) collective-permute-start(bf16[4,2,128,128]{3,2,1,0:T(8,128)(2,1)S(1)} %pad_maximum_fusion.near_ref), channel_id=1, source_target_pairs={{0,16},{16,0},{32,48},{48,32},{64,80},{80,64},{96,112},{112,96},{1... | collective-permute-start | bytes 786440 | tf_op jit(solution)/shard_map/ppermute | solution.py:304
  30.8 5.5 %collective-permute-start.5 = (f32[128,128]{1,0:T(8,128)S(1)}, f32[128,128]{1,0:T(8,128)S(1)}, u32[]{:S(2)}, u32[]{:S(2)}) collective-permute-start(f32[128,128]{1,0:T(8,128)S(1)} %get-tuple-element.17.own_ref), channel_id=1, source_target_pairs={{0,8},{1,9},{2,10},{3,11},{4,12},{5,13},{6,14},{7,15},{8,0},{9,1},... | collective-permute-start | bytes 196616 | tf_op jit(solution)/shard_map/ppermute | solution.py:304
  36.3 0.7 copy-start.2
  37.0 1.0 copy-start.3
  38.0 42.7 %copy-start = (bf16[128,128,128]{2,1,0:T(8,128)(2,1)S(1)}, bf16[128,128,128]{2,1,0:T(8,128)(2,1)}, u32[]{:S(2)}) copy-start(bf16[128,128,128]{2,1,0:T(8,128)(2,1)} %pair_ref.1) | copy-start | bytes 12582916
  67.3 13.3 %collective-permute-start.7 = (bf16[128,128]{1,0:T(8,128)(2,1)S(1)}, bf16[128,128]{1,0:T(8,128)(2,1)S(1)}, u32[]{:S(2)}, u32[]{:S(2)}) collective-permute-start(bf16[128,128]{1,0:T(8,128)(2,1)S(1)} %get-tuple-element.21.left_ref), channel_id=1, source_target_pairs={{0,0},{1,16},{2,32},{3,48},{4,64},{5,80},{6,96},{7,112},{8,128},{9... | collective-permute-start | bytes 98312 | tf_op jit(solution)/shard_map/ppermute | solution.py:394

commit v5 on v4

--- a/solution.py
+++ b/solution.py
@@ -106,7 +106,10 @@
         out.wait()
 
 
-def attend_kernel(own_ref, other_ref, bias_ref, near_ref, far_ref, out_ref, score_ref):
+def attend_kernel(
+    own_ref, other_ref, bias_ref, near_ref, far_hbm, out_ref, score_ref, far_ref, sems
+):
+    copies = start_copies(((far_hbm, far_ref),), sems)
     blocks, heads_there, tile_rows, tile_cols = bias_ref.shape
     width = own_ref.shape[0] // 2
     pairs = heads_there // 2
@@ -123,6 +126,7 @@
         return jnp.where(core == b % 2, near, far)
 
     own, other = own_ref[...], other_ref[...]
+    copies[0].wait()
     attended, gates, sums = [], [], []
     for z in range(2):
         here = jnp.where(second == z, own, other)
@@ -148,19 +152,29 @@
             total = jnp.sum(total, axis=-1, keepdims=True)
             attended.append(mixed / total)
             sums.append(top + jnp.log(total))
+    def for_half(z, first, last):
+        low = lax.broadcasted_iota(jnp.int32, first.shape, 1) < tile_rows // 2
+        if z == 0:
+            return jnp.where(low, first, pltpu.roll(last, tile_rows // 2, 1)).astype(bf16)
+        return jnp.where(low, pltpu.roll(first, tile_rows // 2, 1), last).astype(bf16)
+
     gated = jnp.transpose(jnp.concatenate(attended, axis=1)) * jnp.concatenate(gates, axis=0)
     lane = lax.broadcasted_iota(jnp.int32, (tile_rows, 128), 1)
+    coded_rows = out_ref.shape[1] - width
     coded = jnp.zeros((tile_rows, 128), f32)
     for h, value in enumerate(sums):
         for p in range(3):
             part = value.astype(bf16).astype(f32)
             value = value - part
-            coded = jnp.where(lane == p * heads_there + h, part, coded)
-    coded = jnp.transpose(coded)[: out_ref.shape[1] - 2 * width]
-    gated, coded = gated.astype(bf16), coded.astype(bf16)
-    for d in range(out_ref.shape[0]):
-        out_ref[d, : 2 * width] = gated
-        out_ref[d, 2 * width :] = coded
+            place = (h // pairs) * coded_rows + p * pairs + h % pairs
+            coded = jnp.where(lane == place, part, coded)
+    coded = jnp.transpose(coded)
+    for z in range(2):
+        values = for_half(z, gated[:width], gated[width:])
+        codes = for_half(z, coded[:coded_rows], coded[coded_rows : 2 * coded_rows])
+        for d in range(blocks):
+            out_ref[z * blocks + d, :width] = values
+            out_ref[z * blocks + d, width:] = codes
 
 
 def factor_kernel(
@@ -170,39 +184,48 @@
     w_factors_hbm,
     out_ref,
     factors_ref,
-    mixed_ref,
+    joined_ref,
     single_ref,
     w_factors_ref,
     sems,
 ):
-    copies = start_copies(((single_hbm, single_ref), (w_factors_hbm, w_factors_ref)), sems)
-    targets = sent_ref.shape[0] // 2
-    width = mixed_ref.shape[0] // sent_ref.shape[0]
-    heads_there = 4
-    head_width = 2 * width // heads_there
+    blocks = sent_ref.shape[0] // 2
+    width = joined_ref.shape[0] // blocks
+    rows_here = out_ref.shape[0]
+    mine = lax.axis_index("cols") // blocks
+    copies = start_copies(
+        (
+            (single_hbm.at[pl.ds(mine * rows_here, rows_here)], single_ref),
+            (w_factors_hbm, w_factors_ref),
+        ),
+        sems,
+    )
+    pairs = 2
+    head_width = width // pairs
 
     def log_sum(d):
-        coded = sent_ref[d, 2 * width :].astype(f32)
-        parts = [coded[p * heads_there : (p + 1) * heads_there] for p in range(3)]
+        coded = sent_ref[d, width:].astype(f32)
+        parts = [coded[p * pairs : (p + 1) * pairs] for p in range(3)]
         return parts[0] + parts[1] + parts[2]
 
-    for d in range(targets):
-        first, last = log_sum(d), log_sum(d + targets)
+    for d in range(blocks):
+        first, last = log_sum(d), log_sum(d + blocks)
         top = jnp.maximum(first, last)
         first, last = jnp.exp(first - top), jnp.exp(last - top)
         inverse = 1.0 / (first + last)
         first, last = first * inverse, last * inverse
-        for h in range(heads_there):
-            rows_here = pl.ds(h * head_width, head_width)
+        for h in range(pairs):
+            here = pl.ds(h * head_width, head_width)
             joined = (
-                sent_ref[d, rows_here].astype(f32) * first[h : h + 1]
-                + sent_ref[d + targets, rows_here].astype(f32) * last[h : h + 1]
+                sent_ref[d, here].astype(f32) * first[h : h + 1]
+                + sent_ref[d + blocks, here].astype(f32) * last[h : h + 1]
             )
-            owner = (h * head_width // width) * targets + d
-            place = owner * width + h * head_width % width
-            mixed_ref[place : place + head_width] = joined.astype(bf16)
-    mixed = jnp.transpose(mixed_ref[...].astype(f32)).astype(bf16)
-    head_total = jnp.dot(mixed, w_out_ref[...], preferred_element_type=f32)
+            place = d * width + h * head_width
+            joined_ref[place : place + head_width] = joined.astype(bf16)
+    mixed = jnp.transpose(joined_ref[...].astype(f32)).astype(bf16)
+    depth = blocks * width
+    head_total = jnp.dot(mixed[:rows_here], w_out_ref[:depth], preferred_element_type=f32)
+    head_total += jnp.dot(mixed[rows_here:], w_out_ref[depth:], preferred_element_type=f32)
     copies[0].wait()
     single_out = (single_ref[...].astype(f32) + head_total).astype(bf16)
     out_ref[...] = single_out
@@ -213,47 +236,66 @@
 
 def update_kernel(
     pair_ref,
-    left_ref,
-    right_ref,
+    left_own_ref,
+    left_other_ref,
+    right_one_ref,
+    right_two_ref,
+    single_own_hbm,
+    single_other_hbm,
     w_pairout_hbm,
     w_up_hbm,
     w_down_hbm,
     out_ref,
+    single_hbm,
     w_pairout_ref,
     w_up_ref,
     w_down_ref,
     scale_ref,
     shift_ref,
+    right_ref,
     sems,
 ):
+    block_rows, tile_cols, width = pair_ref.shape
+    factor_width = width // 2
+    half = left_own_ref.shape[0]
+    at = pl.program_id(0)
+    col_half = lax.axis_index("cols") // (lax.axis_size("cols") // 2)
+    row_half = lax.axis_index("rows") // (lax.axis_size("rows") // 2)
     copies = [
         pltpu.make_async_copy(w_pairout_hbm, w_pairout_ref, sems.at[0]),
         pltpu.make_async_copy(w_up_hbm, w_up_ref, sems.at[1]),
         pltpu.make_async_copy(w_down_hbm, w_down_ref, sems.at[2]),
     ]
-
-    @pl.when(pl.program_id(0) == 0)
+    singles = [
+        pltpu.make_async_copy(
+            single_own_hbm, single_hbm.at[pl.ds(col_half * half, half)], sems.at[3]
+        ),
+        pltpu.make_async_copy(
+            single_other_hbm, single_hbm.at[pl.ds((1 - col_half) * half, half)], sems.at[4]
+        ),
+    ]
+
+    def in_order(first_is, one, two):
+        top = jnp.where(first_is == 0, one, two)
+        return jnp.concatenate([top, jnp.where(first_is == 0, two, one)], axis=0)
+
+    @pl.when(at == 0)
     def _():
-        for copy in copies:
+        for copy in copies + singles:
             copy.start()
-
-    block_rows, tile_cols, width = pair_ref.shape
-    factor_width = width // 2
-    low = lax.broadcasted_iota(jnp.int32, (1, width), 1) < factor_width
-    right = right_ref[:, factor_width:]
-    right = jnp.concatenate([right, right], axis=1)
-    left = left_ref[:, :factor_width].astype(f32)
-    left = jnp.concatenate([left, left], axis=1)
-    scale_ref[...] = jnp.where(low, left, -1.0).astype(bf16)[:, None, :]
-    shift_ref[...] = jnp.where(low, 0.0, left).astype(bf16)[:, None, :]
-    rows_here = block_rows * tile_cols
-    paired = (right[None] * scale_ref[...] + shift_ref[...]).reshape(rows_here, width)
-
-    @pl.when(pl.program_id(0) == 0)
-    def _():
+        right = in_order(row_half, right_one_ref[...], right_two_ref[...])[:, factor_width:]
+        right_ref[...] = jnp.concatenate([right, right], axis=1)
+        left = in_order(col_half, left_own_ref[...], left_other_ref[...])[:, :factor_width]
+        left = jnp.concatenate([left, left], axis=1).astype(f32)
+        low = lax.broadcasted_iota(jnp.int32, (1, width), 1) < factor_width
+        scale_ref[...] = jnp.where(low, left, -1.0).astype(bf16)[:, None, :]
+        shift_ref[...] = jnp.where(low, 0.0, left).astype(bf16)[:, None, :]
         for copy in copies:
             copy.wait()
 
+    rows_here = block_rows * tile_cols
+    here = pl.ds(at * block_rows, block_rows)
+    paired = (right_ref[...][None] * scale_ref[here] + shift_ref[here]).reshape(rows_here, width)
     moved = jnp.dot(paired, w_pairout_ref[...], preferred_element_type=f32)
     pair_mid = (pair_ref[...].reshape(rows_here, width).astype(f32) + moved).astype(bf16)
     normed = normalize_rows(pair_mid)
@@ -261,6 +303,11 @@
     hidden = jnp.maximum(hidden, 0)
     down = jnp.dot(hidden, w_down_ref[...], preferred_element_type=f32)
     out_ref[...] = (pair_mid.astype(f32) + down).astype(bf16).reshape(pair_ref.shape)
+
+    @pl.when(at == pl.num_programs(0) - 1)
+    def _():
+        for copy in singles:
+            copy.wait()
 
 
 def whole(shape):
@@ -285,6 +332,7 @@
     heads = w_bias.shape[1]
     in_place = pl.BlockSpec(memory_space=pl.ANY)
     in_hbm = pl.BlockSpec(memory_space=pltpu.HBM)
+    in_vmem = pl.BlockSpec(memory_space=pltpu.VMEM)
 
     shifts = rows // 4
     half_rows, half_cols = rows // 2, cols // 2
@@ -354,35 +402,40 @@
     groups = [list(range(half_cols)), list(range(half_cols, cols))]
     bias_heads = lax.all_to_all(bias_local, "cols", 0, 0, axis_index_groups=groups, tiled=True)
 
+    query_other = sent(query, "cols", lambda c: c ^ half_cols)
     both = jnp.stack([kv_first, kv_last])
     near = [both]
     for s in range(1, shifts):
         around = lambda r: (r & half_rows) | ((r + 2 * s) & (half_rows - 1))
         near.append(sent(both, "rows", around))
     near = jnp.stack(near)
-    query, near = lax.optimization_barrier((query, near))
     far = sent(near, "rows", lambda r: r ^ 1)
-    query_other = sent(query, "cols", lambda c: c ^ half_cols)
 
     mixed = pl.pallas_call(
         attend_kernel,
-        out_shape=jax.ShapeDtypeStruct((cols, 2 * width + 16, tile_rows), bf16),
-        scratch_shapes=[pltpu.VMEM((half_cols, tile_rows, tile_cols), f32)],
+        out_shape=jax.ShapeDtypeStruct((cols, width + 16, tile_rows), bf16),
+        in_specs=[in_vmem] * 4 + [in_hbm],
+        scratch_shapes=[
+            pltpu.VMEM((half_cols, tile_rows, tile_cols), f32),
+            pltpu.VMEM(near.shape, bf16),
+            pltpu.SemaphoreType.DMA((1,)),
+        ],
         compiler_params=params(),
         name="attend",
-    )(query, query_other, bias_heads, near, far)
+    )(query, query_other, bias_heads, near, pinned(far))
     mixed_all = lax.all_to_all(mixed, "cols", 0, 0, tiled=True)
 
-    single_out, factors = pl.pallas_call(
+    factor_shape = (tile_rows // 2, w_factors.shape[1])
+    single_half, factors = pl.pallas_call(
         factor_kernel,
         out_shape=(
-            jax.ShapeDtypeStruct(single.shape, bf16),
-            jax.ShapeDtypeStruct((tile_rows, w_factors.shape[1]), bf16),
+            jax.ShapeDtypeStruct((tile_rows // 2, single_width), bf16),
+            jax.ShapeDtypeStruct(factor_shape, bf16),
         ),
         in_specs=[whole(mixed_all.shape), whole(w_out.shape), in_hbm, in_hbm],
         scratch_shapes=[
-            pltpu.VMEM((single_width, tile_rows), bf16),
-            pltpu.VMEM(single.shape, bf16),
+            pltpu.VMEM((single_width // 2, tile_rows), bf16),
+            pltpu.VMEM((tile_rows // 2, single_width), bf16),
             pltpu.VMEM(w_factors.shape, bf16),
             pltpu.SemaphoreType.DMA((2,)),
         ],
@@ -390,34 +443,45 @@
         name="factor",
     )(mixed_all, w_out, pinned(single), pinned(w_factors))
 
-    swapped = [(a * cols + b, b * cols + a) for a in range(rows) for b in range(cols)]
-    right_factors = lax.ppermute(factors, ("rows", "cols"), swapped)
+    right_one = sent(factors, both_axes, lambda r, c: (c, r))
+    right_two = sent(factors, both_axes, lambda r, c: (c ^ half_rows, r))
+    left_other = sent(factors, "cols", lambda c: c ^ half_cols)
+    single_other = sent(single_half, "cols", lambda c: c ^ half_cols)
 
     block_rows = 32
-    updated = pl.pallas_call(
+    pair_block = pl.BlockSpec((block_rows, tile_cols, pair_width), lambda i: (i, 0, 0))
+    updated, single_out = pl.pallas_call(
         update_kernel,
         grid=(tile_rows // block_rows,),
-        in_specs=[
-            pl.BlockSpec((block_rows, tile_cols, pair_width), lambda i: (i, 0, 0)),
-            pl.BlockSpec((block_rows, factors.shape[1]), lambda i: (i, 0)),
-            whole(right_factors.shape),
-            in_place,
-            in_place,
-            in_place,
-        ],
-        out_specs=pl.BlockSpec((block_rows, tile_cols, pair_width), lambda i: (i, 0, 0)),
-        out_shape=jax.ShapeDtypeStruct(pair.shape, bf16),
+        in_specs=[pair_block] + [whole(factor_shape)] * 4 + [in_place] * 2 + [in_hbm] * 3,
+        out_specs=(pair_block, in_place),
+        out_shape=(
+            jax.ShapeDtypeStruct(pair.shape, bf16),
+            jax.ShapeDtypeStruct(single.shape, bf16),
+        ),
         scratch_shapes=[
             pltpu.VMEM(w_pairout.shape, bf16),
             pltpu.VMEM(w_up.shape, bf16),
             pltpu.VMEM(w_down.shape, bf16),
-            pltpu.VMEM((block_rows, 1, pair_width), bf16),
-            pltpu.VMEM((block_rows, 1, pair_width), bf16),
-            pltpu.SemaphoreType.DMA((3,)),
+            pltpu.VMEM((tile_rows, 1, pair_width), bf16),
+            pltpu.VMEM((tile_rows, 1, pair_width), bf16),
+            pltpu.VMEM((tile_cols, pair_width), bf16),
+            pltpu.SemaphoreType.DMA((5,)),
         ],
         compiler_params=params(20),
         name="update",
-    )(pair, factors, right_factors, pinned(w_pairout), pinned(w_up), pinned(w_down))
+    )(
+        pair,
+        factors,
+        left_other,
+        right_one,
+        right_two,
+        single_half,
+        single_other,
+        pinned(w_pairout),
+        pinned(w_up),
+        pinned(w_down),
+    )
     return (single_out, updated)
 
 

time: 96.1 us -> 92.3 us (0.960)
  starting transfers between devices: 18.6 us -> 25.9 us
  blocking collectives: 25.3 us -> 19.7 us
  waiting for transfers between devices: 22.1 us -> 17.3 us
  local copies, waits for them, and re-layouts: 1.66 us -> 0.01 us
    ppermute x1 -> x0, waiting for transfers between devices: 11.2 us -> none  [per_device(): right_factors = lax.ppermute(factors, ('rows', 'cols'), swapped)]
    ppermute x7 -> x11, starting transfers between devices: 11.6 us -> 21.2 us  [sent(): return lax.ppermute(value, axes, routes)]
    ppermute x7 -> x11, waiting for transfers between devices: 10.9 us -> 17.3 us  [sent(): return lax.ppermute(value, axes, routes)]
    all_to_all x1, blocking collectives: 25.3 us -> 19.7 us  [per_device(): mixed_all = lax.all_to_all(mixed, 'cols', 0, 0, tiled=True)]
    ppermute x1 -> x0, starting transfers between devices: 2.1 us -> none  [per_device(): right_factors = lax.ppermute(factors, ('rows', 'cols'), swapped)]
    unnamed x8 -> x4, local copies, waits for them, and re-layouts: 1.66 us -> 0.01 us
  transfers between devices with their start and end apart: 9 -> 12, of which waited for: 4 -> 5; matrix products, arithmetic and copies ran while one was open for 0% -> 0% of each run, Pallas kernels for 7% -> 7%
where the time goes in v5:
time: 92.3 us; the launch traced here: 91.7 us
  Pallas kernels  27.8 us (30%)
  starting transfers between devices  25.9 us (28%)
  blocking collectives  19.7 us (21%)
  waiting for transfers between devices  17.3 us (19%)
    ppermute x11, starting transfers between devices, sent(): return lax.ppermute(value, axes, routes)  21.2 us
    all_to_all x1, blocking collectives, per_device(): mixed_all = lax.all_to_all(mixed, 'cols', 0, 0, tiled=True)  19.7 us
    ppermute x11, waiting for transfers between devices, sent(): return lax.ppermute(value, axes, routes)  17.3 us
    pallas_call x1, Pallas kernels, per_device(): pl.pallas_call(update_kernel, grid=(tile_rows // block_rows,), in_specs=[...  14.8 us
    pallas_call x1, Pallas kernels, per_device(): pl.pallas_call(bias_kernel, out_shape=jax.ShapeDtypeStruct(sent_shape, bf...  6.77 us
    all_to_all x1, starting transfers between devices, per_device(): lax.all_to_all(bias_local, 'cols', 0, 0, axis_index_groups=groups, tiled=...  4.76 us
    pallas_call x1, Pallas kernels, per_device(): pl.pallas_call(attend_kernel, out_shape=jax.ShapeDtypeStruct((cols, width...  2.86 us
  transfers between devices with their start and end apart: 12, of which 5 were waited for; matrix products, arithmetic and copies ran while one was open for 0% of the time, Pallas kernels for 7%

profile of v5, /device:TPU:88, one launch (start us, length us, event | category | flops | bytes accessed | tf_op | source)
XLA Modules:
  0.0 91.7 jit_solution(7115800998370208233)
XLA Ops:
  0.6 1.5 %project.1 = (f32[128,128]{1,0:T(8,128)S(1)}, bf16[128,128]{1,0:T(8,128)(2,1)S(1)}) custom-call(bf16[128,1024]{1,0:T(8,128)(2,1)} %single_hbm.3, bf16[256,1024]{1,0:T(8,128)(2,1)} %bitcast.12), custom_call_target="tpu_custom_call" | custom-call | tf_op jit(solution)/shard_map/project/pallas_call | solution.py:362
  2.2 0.1 collective-permute-start.2
  2.2 7.8 %collective-permute-start.1 = (bf16[128,128]{1,0:T(8,128)(2,1)S(1)}, bf16[128,128]{1,0:T(8,128)(2,1)S(1)}, u32[]{:S(2)}, u32[]{:S(2)}) collective-permute-start(bf16[128,128]{1,0:T(8,128)(2,1)S(1)} %get-tuple-element.13), channel_id=1, source_target_pairs={{0,0},{1,1},{2,2},{3,3},{4,4},{5,5},{6,6},{7,7},{8,128},{9,129},{1... | collective-permute-start | bytes 98312 | tf_op jit(solution)/shard_map/ppermute | solution.py:352
  10.1 0.0 copy-start.1
  10.1 6.8 %bias.1 = bf16[8,4,128,128]{3,2,1,0:T(8,128)(2,1)} custom-call(bf16[128,128,128]{2,1,0:T(8,128)(2,1)} %pair_ref.1, bf16[32,128]{1,0:T(8,128)(2,1)} %bitcast.18, s32[16,1,128]{2,1,0:T(1,128)} %bitcast.19), custom_call_target="tpu_custom_call" | custom-call | tf_op jit(solution)/shard_map/bias/pallas_call | solution.py:384
  16.9 0.0 collective-permute-done.2
  16.9 0.0 collective-permute-done.1
  16.9 4.8 %all-to-all-start = ((bf16[8,4,128,128]{3,2,1,0:T(8,128)(2,1)}), bf16[8,4,128,128]{3,2,1,0:T(8,128)(2,1)S(1)}, u32[]{:S(2)}, u32[]{:S(2)}) async-start(bf16[8,4,128,128]{3,2,1,0:T(8,128)(2,1)} %bias.1), calls=%async_computation | async-start | bytes 2097152 | tf_op jit(solution)/shard_map/all_to_all | solution.py:403
  21.7 1.3 %collective-permute-start.4 = (bf16[2,128,128]{2,1,0:T(8,128)(2,1)S(1)}, bf16[2,128,128]{2,1,0:T(8,128)(2,1)S(1)}, u32[]{:S(2)}, u32[]{:S(2)}) collective-permute-start(bf16[2,128,128]{2,1,0:T(8,128)(2,1)S(1)} %get-tuple-element.23), channel_id=1, source_target_pairs={{0,64},{16,80},{32,96},{48,112},{64,0},{80,16},{96,32},{112,48},{1... | collective-permute-start | bytes 196616 | tf_op jit(solution)/shard_map/ppermute | solution.py:352
  23.0 2.2 %collective-permute-start.3 = (bf16[2,128,128]{2,1,0:T(8,128)(2,1)S(1)}, bf16[2,128,128]{2,1,0:T(8,128)(2,1)S(1)}, u32[]{:S(2)}, u32[]{:S(2)}) collective-permute-start(bf16[2,128,128]{2,1,0:T(8,128)(2,1)S(1)} %get-tuple-element.23), channel_id=1, source_target_pairs={{0,32},{16,48},{32,64},{48,80},{64,96},{80,112},{96,0},{112,16},{1... | collective-permute-start | bytes 196616 | tf_op jit(solution)/shard_map/ppermute | solution.py:352
  25.2 0.0 collective-permute-start.5
  25.2 2.6 %collective-permute-done.4 = bf16[2,128,128]{2,1,0:T(8,128)(2,1)S(1)} collective-permute-done((bf16[2,128,128]{2,1,0:T(8,128)(2,1)S(1)}, bf16[2,128,128]{2,1,0:T(8,128)(2,1)S(1)}, u32[]{:S(2)}, u32[]{:S(2)}) %collective-permute-start.4) | collective-permute-done | bytes 65568 | tf_op jit(solution)/shard_map/ppermute | solution.py:352
  27.8 0.0 collective-permute-done.3
  27.8 2.9 %collective-permute-done.5 = bf16[2,128,128]{2,1,0:T(8,128)(2,1)S(1)} collective-permute-done((bf16[2,128,128]{2,1,0:T(8,128)(2,1)S(1)}, bf16[2,128,128]{2,1,0:T(8,128)(2,1)S(1)}, u32[]{:S(2)}, u32[]{:S(2)}) %collective-permute-start.5) | collective-permute-done | bytes 65568 | tf_op jit(solution)/shard_map/ppermute | solution.py:352
  30.7 0.1 collective-permute-start.6
  30.8 0.1 collective-permute-start
  30.9 5.4 %collective-permute-done.other_ref = f32[128,128]{1,0:T(8,128)S(1)} collective-permute-done((f32[128,128]{1,0:T(8,128)S(1)}, f32[128,128]{1,0:T(8,128)S(1)}, u32[]{:S(2)}, u32[]{:S(2)}) %collective-permute-start) | collective-permute-done | bytes 65568 | tf_op jit(solution)/shard_map/ppermute | solution.py:352
  36.3 0.0 collective-permute-done.6.far_hbm
  36.3 0.0 all-to-all-done.bias_ref
  36.3 0.0 copy-start
  36.3 2.9 %attend.1 = bf16[16,80,128]{2,1,0:T(8,128)(2,1)S(1)} custom-call(f32[128,128]{1,0:T(8,128)S(1)} %get-tuple-element.12.own_ref, f32[128,128]{1,0:T(8,128)S(1)} %collective-permute-done.other_ref, bf16[8,4,128,128]{3,2,1,0:T(8,128)(2,1)S(1)} %all-to-all-done.bias_ref, bf16[4,2,128,128]{3,2,1,0:T(8,128)(2,1)S(1)} %pad_maximum_fusion.near_ref, ...), custom_call_target="tpu_custom_call" | custom-call | tf_op jit(solution)/shard_map/attend/pallas_call | solution.py:414
  39.2 19.7 %all_to_all.10.sent_ref = bf16[16,80,128]{2,1,0:T(8,128)(2,1)S(1)} all-to-all(bf16[16,80,128]{2,1,0:T(8,128)(2,1)S(1)} %attend.1), channel_id=1, replica_groups=mesh['rows'=16,'cols'=16] {'cols'}, dimensions={0} | all-to-all | bytes 655360 | tf_op jit(solution)/shard_map/all_to_all | solution.py:426
  58.9 0.0 copy-done.1
  58.9 1.8 %factor.1 = (bf16[64,1024]{1,0:T(8,128)(2,1)S(1)}, bf16[64,128]{1,0:T(8,128)(2,1)S(1)}) custom-call(bf16[16,80,128]{2,1,0:T(8,128)(2,1)S(1)} %all_to_all.10.sent_ref, bf16[1024,1024]{1,0:T(8,128)(2,1)S(1)} %copy-done.1, bf16[128,1024]{1,0:T(8,128)(2,1)} %single_hbm.3, bf16[1024,128]{1,0:T(8,128)(2,1)} %w_factors_hbm.1), custom_call_target="tpu_custom_call" | custom-call | tf_op jit(solution)/shard_map/factor/pallas_call | solution.py:429
  60.7 1.7 %collective-permute-start.10 = (bf16[64,1024]{1,0:T(8,128)(2,1)S(1)}, bf16[64,1024]{1,0:T(8,128)(2,1)S(1)}, u32[]{:S(2)}, u32[]{:S(2)}) collective-permute-start(bf16[64,1024]{1,0:T(8,128)(2,1)S(1)} %get-tuple-element.19.single_own_hbm), channel_id=1, source_target_pairs={{0,8},{1,9},{2,10},{3,11},{4,12},{5,13},{6,14},{7,15},{8,0},{9,1},... | collective-permute-start | bytes 393224 | tf_op jit(solution)/shard_map/ppermute | solution.py:352
  62.4 1.1 %collective-permute-start.9 = (bf16[64,128]{1,0:T(8,128)(2,1)S(1)}, bf16[64,128]{1,0:T(8,128)(2,1)S(1)}, u32[]{:S(2)}, u32[]{:S(2)}) collective-permute-start(bf16[64,128]{1,0:T(8,128)(2,1)S(1)} %get-tuple-element.18.left_own_ref), channel_id=1, source_target_pairs={{0,128},{1,144},{2,160},{3,176},{4,192},{5,208},{6,224},{7,240},{8... | collective-permute-start | bytes 49160 | tf_op jit(solution)/shard_map/ppermute | solution.py:352
  63.5 5.4 %collective-permute-start.8 = (bf16[64,128]{1,0:T(8,128)(2,1)S(1)}, bf16[64,128]{1,0:T(8,128)(2,1)S(1)}, u32[]{:S(2)}, u32[]{:S(2)}) collective-permute-start(bf16[64,128]{1,0:T(8,128)(2,1)S(1)} %get-tuple-element.18.left_own_ref), channel_id=1, source_target_pairs={{0,0},{1,16},{2,32},{3,48},{4,64},{5,80},{6,96},{7,112},{8,128},{9... | collective-permute-start | bytes 49160 | tf_op jit(solution)/shard_map/ppermute | solution.py:352
  68.9 1.4 %collective-permute-start.7 = (bf16[64,128]{1,0:T(8,128)(2,1)S(1)}, bf16[64,128]{1,0:T(8,128)(2,1)S(1)}, u32[]{:S(2)}, u32[]{:S(2)}) collective-permute-start(bf16[64,128]{1,0:T(8,128)(2,1)S(1)} %get-tuple-element.18.left_own_ref), channel_id=1, source_target_pairs={{0,8},{1,9},{2,10},{3,11},{4,12},{5,13},{6,14},{7,15},{8,0},{9,1},... | collective-permute-start | bytes 49160 | tf_op jit(solution)/shard_map/ppermute | solution.py:352
  70.3 3.4 %collective-permute-done.9.right_two_ref = bf16[64,128]{1,0:T(8,128)(2,1)S(1)} collective-permute-done((bf16[64,128]{1,0:T(8,128)(2,1)S(1)}, bf16[64,128]{1,0:T(8,128)(2,1)S(1)}, u32[]{:S(2)}, u32[]{:S(2)}) %collective-permute-start.9) | collective-permute-done | bytes 16416 | tf_op jit(solution)/shard_map/ppermute | solution.py:352
  73.7 3.0 %collective-permute-done.8.right_one_ref = bf16[64,128]{1,0:T(8,128)(2,1)S(1)} collective-permute-done((bf16[64,128]{1,0:T(8,128)(2,1)S(1)}, bf16[64,128]{1,0:T(8,128)(2,1)S(1)}, u32[]{:S(2)}, u32[]{:S(2)}) %collective-permute-start.8) | collective-permute-done | bytes 16416 | tf_op jit(solution)/shard_map/ppermute | solution.py:352
  76.7 0.0 collective-permute-done.7.left_other_ref
  76.7 0.0 collective-permute-done.10.single_other_hbm
  76.7 0.0 copy-done
  76.7 14.8 %update.1 = (bf16[128,128,128]{2,1,0:T(8,128)(2,1)}, bf16[128,1024]{1,0:T(8,128)(2,1)}) custom-call(bf16[128,128,128]{2,1,0:T(8,128)(2,1)S(1)} %copy-done, bf16[64,128]{1,0:T(8,128)(2,1)S(1)} %get-tuple-element.18.left_own_ref, bf16[64,128]{1,0:T(8,128)(2,1)S(1)} %collective-permute-done.7.left_other_ref, ...), custom_call_target="tpu_custom_call" | custom-call | tf_op jit(solution)/shard_map/update/pallas_call | solution.py:453
  (2 shorter events, 0.0 us)
Async XLA Ops:
  2.2 14.7 %collective-permute-start.2 = (bf16[128,128]{1,0:T(8,128)(2,1)S(1)}, bf16[128,128]{1,0:T(8,128)(2,1)S(1)}, u32[]{:S(2)}, u32[]{:S(2)}) collective-permute-start(bf16[128,128]{1,0:T(8,128)(2,1)S(1)} %get-tuple-element.13), channel_id=1, source_target_pairs={{0,128},{1,129},{2,130},{3,131},{4,132},{5,133},{6,134},{7,135},{8... | collective-permute-start | bytes 98312 | tf_op jit(solution)/shard_map/ppermute | solution.py:352
  2.2 14.7 %collective-permute-start.1 = (bf16[128,128]{1,0:T(8,128)(2,1)S(1)}, bf16[128,128]{1,0:T(8,128)(2,1)S(1)}, u32[]{:S(2)}, u32[]{:S(2)}) collective-permute-start(bf16[128,128]{1,0:T(8,128)(2,1)S(1)} %get-tuple-element.13), channel_id=1, source_target_pairs={{0,0},{1,1},{2,2},{3,3},{4,4},{5,5},{6,6},{7,7},{8,128},{9,129},{1... | collective-permute-start | bytes 98312 | tf_op jit(solution)/shard_map/ppermute | solution.py:352
  10.1 48.8 %copy-start.1 = (bf16[1024,1024]{1,0:T(8,128)(2,1)S(1)}, bf16[1024,1024]{1,0:T(8,128)(2,1)}, u32[]{:S(2)}) copy-start(bf16[1024,1024]{1,0:T(8,128)(2,1)} %w_out_ref.1) | copy-start | bytes 6291460
  16.9 19.4 %all-to-all-start = ((bf16[8,4,128,128]{3,2,1,0:T(8,128)(2,1)}), bf16[8,4,128,128]{3,2,1,0:T(8,128)(2,1)S(1)}, u32[]{:S(2)}, u32[]{:S(2)}) async-start(bf16[8,4,128,128]{3,2,1,0:T(8,128)(2,1)} %bias.1), calls=%async_computation | async-start | bytes 2097152 | tf_op jit(solution)/shard_map/all_to_all | solution.py:403
  21.7 6.1 %collective-permute-start.4 = (bf16[2,128,128]{2,1,0:T(8,128)(2,1)S(1)}, bf16[2,128,128]{2,1,0:T(8,128)(2,1)S(1)}, u32[]{:S(2)}, u32[]{:S(2)}) collective-permute-start(bf16[2,128,128]{2,1,0:T(8,128)(2,1)S(1)} %get-tuple-element.23), channel_id=1, source_target_pairs={{0,64},{16,80},{32,96},{48,112},{64,0},{80,16},{96,32},{112,48},{1... | collective-permute-start | bytes 196616 | tf_op jit(solution)/shard_map/ppermute | solution.py:352
  23.0 4.8 %collective-permute-start.3 = (bf16[2,128,128]{2,1,0:T(8,128)(2,1)S(1)}, bf16[2,128,128]{2,1,0:T(8,128)(2,1)S(1)}, u32[]{:S(2)}, u32[]{:S(2)}) collective-permute-start(bf16[2,128,128]{2,1,0:T(8,128)(2,1)S(1)} %get-tuple-element.23), channel_id=1, source_target_pairs={{0,32},{16,48},{32,64},{48,80},{64,96},{80,112},{96,0},{112,16},{1... | collective-permute-start | bytes 196616 | tf_op jit(solution)/shard_map/ppermute | solution.py:352
  25.2 5.5 %collective-permute-start.5 = (bf16[2,128,128]{2,1,0:T(8,128)(2,1)S(1)}, bf16[2,128,128]{2,1,0:T(8,128)(2,1)S(1)}, u32[]{:S(2)}, u32[]{:S(2)}) collective-permute-start(bf16[2,128,128]{2,1,0:T(8,128)(2,1)S(1)} %get-tuple-element.23), channel_id=1, source_target_pairs={{0,96},{16,112},{32,0},{48,16},{64,32},{80,48},{96,64},{112,80},{1... | collective-permute-start | bytes 196616 | tf_op jit(solution)/shard_map/ppermute | solution.py:352
  30.7 5.6 %collective-permute-start.6 = (bf16[4,2,128,128]{3,2,1,0:T(8,128)(2,1)S(1)}, bf16[4,2,128,128]{3,2,1,0:T(8,128)(2,1)}, u32[]{:S(2)}, u32[]{:S(2)}) collective-permute-start(bf16[4,2,128,128]{3,2,1,0:T(8,128)(2,1)S(1)} %pad_maximum_fusion.near_ref), channel_id=1, source_target_pairs={{0,16},{16,0},{32,48},{48,32},{64,80},{80,64},{96,112},{112,96},{1... | collective-permute-start | bytes 786440 | tf_op jit(solution)/shard_map/ppermute | solution.py:352
  30.8 5.5 %collective-permute-start = (f32[128,128]{1,0:T(8,128)S(1)}, f32[128,128]{1,0:T(8,128)S(1)}, u32[]{:S(2)}, u32[]{:S(2)}) collective-permute-start(f32[128,128]{1,0:T(8,128)S(1)} %get-tuple-element.12.own_ref), channel_id=1, source_target_pairs={{0,8},{1,9},{2,10},{3,11},{4,12},{5,13},{6,14},{7,15},{8,0},{9,1},... | collective-permute-start | bytes 196616 | tf_op jit(solution)/shard_map/ppermute | solution.py:352
  36.3 40.4 %copy-start = (bf16[128,128,128]{2,1,0:T(8,128)(2,1)S(1)}, bf16[128,128,128]{2,1,0:T(8,128)(2,1)}, u32[]{:S(2)}) copy-start(bf16[128,128,128]{2,1,0:T(8,128)(2,1)} %pair_ref.1) | copy-start | bytes 12582916
  60.7 16.0 %collective-permute-start.10 = (bf16[64,1024]{1,0:T(8,128)(2,1)S(1)}, bf16[64,1024]{1,0:T(8,128)(2,1)S(1)}, u32[]{:S(2)}, u32[]{:S(2)}) collective-permute-start(bf16[64,1024]{1,0:T(8,128)(2,1)S(1)} %get-tuple-element.19.single_own_hbm), channel_id=1, source_target_pairs={{0,8},{1,9},{2,10},{3,11},{4,12},{5,13},{6,14},{7,15},{8,0},{9,1},... | collective-permute-start | bytes 393224 | tf_op jit(solution)/shard_map/ppermute | solution.py:352
  62.4 11.3 %collective-permute-start.9 = (bf16[64,128]{1,0:T(8,128)(2,1)S(1)}, bf16[64,128]{1,0:T(8,128)(2,1)S(1)}, u32[]{:S(2)}, u32[]{:S(2)}) collective-permute-start(bf16[64,128]{1,0:T(8,128)(2,1)S(1)} %get-tuple-element.18.left_own_ref), channel_id=1, source_target_pairs={{0,128},{1,144},{2,160},{3,176},{4,192},{5,208},{6,224},{7,240},{8... | collective-permute-start | bytes 49160 | tf_op jit(solution)/shard_map/ppermute | solution.py:352
  63.5 13.2 %collective-permute-start.8 = (bf16[64,128]{1,0:T(8,128)(2,1)S(1)}, bf16[64,128]{1,0:T(8,128)(2,1)S(1)}, u32[]{:S(2)}, u32[]{:S(2)}) collective-permute-start(bf16[64,128]{1,0:T(8,128)(2,1)S(1)} %get-tuple-element.18.left_own_ref), channel_id=1, source_target_pairs={{0,0},{1,16},{2,32},{3,48},{4,64},{5,80},{6,96},{7,112},{8,128},{9... | collective-permute-start | bytes 49160 | tf_op jit(solution)/shard_map/ppermute | solution.py:352
  68.9 7.8 %collective-permute-start.7 = (bf16[64,128]{1,0:T(8,128)(2,1)S(1)}, bf16[64,128]{1,0:T(8,128)(2,1)S(1)}, u32[]{:S(2)}, u32[]{:S(2)}) collective-permute-start(bf16[64,128]{1,0:T(8,128)(2,1)S(1)} %get-tuple-element.18.left_own_ref), channel_id=1, source_target_pairs={{0,8},{1,9},{2,10},{3,11},{4,12},{5,13},{6,14},{7,15},{8,0},{9,1},... | collective-permute-start | bytes 49160 | tf_op jit(solution)/shard_map/ppermute | solution.py:352

commit v6 on v4

--- a/solution.py
+++ b/solution.py
@@ -106,7 +106,23 @@
         out.wait()
 
 
-def attend_kernel(own_ref, other_ref, bias_ref, near_ref, far_ref, out_ref, score_ref):
+def attend_kernel(
+    own_hbm,
+    other_hbm,
+    bias_ref,
+    near_ref,
+    far_hbm,
+    kept_ref,
+    sent_ref,
+    score_ref,
+    own_ref,
+    other_ref,
+    far_ref,
+    sems,
+):
+    copies = start_copies(
+        ((own_hbm, own_ref), (other_hbm, other_ref), (far_hbm, far_ref)), sems
+    )
     blocks, heads_there, tile_rows, tile_cols = bias_ref.shape
     width = own_ref.shape[0] // 2
     pairs = heads_there // 2
@@ -122,12 +138,13 @@
         near, far = near_ref[sent, half ^ z, part, :], far_ref[sent, half ^ z, part, :]
         return jnp.where(core == b % 2, near, far)
 
-    own, other = own_ref[...], other_ref[...]
-    attended, gates, sums = [], [], []
-    for z in range(2):
-        here = jnp.where(second == z, own, other)
-        query = jnp.transpose(here[:width]).astype(bf16)
-        gates.append(here[width:])
+    for copy in copies:
+        copy.wait()
+    lane = lax.broadcasted_iota(jnp.int32, (tile_rows, 128), 1)
+    for slot, query_ref in enumerate((own_ref, other_ref)):
+        z = second ^ slot
+        query = jnp.transpose(query_ref[:width]).astype(bf16)
+        attended, sums = [], []
         for h in range(pairs):
             query_head = query[:, h * head_width : (h + 1) * head_width]
             key_rows = pl.ds(h * head_width, head_width)
@@ -148,59 +165,52 @@
             total = jnp.sum(total, axis=-1, keepdims=True)
             attended.append(mixed / total)
             sums.append(top + jnp.log(total))
-    gated = jnp.transpose(jnp.concatenate(attended, axis=1)) * jnp.concatenate(gates, axis=0)
-    lane = lax.broadcasted_iota(jnp.int32, (tile_rows, 128), 1)
-    coded = jnp.zeros((tile_rows, 128), f32)
-    for h, value in enumerate(sums):
-        for p in range(3):
-            part = value.astype(bf16).astype(f32)
-            value = value - part
-            coded = jnp.where(lane == p * heads_there + h, part, coded)
-    coded = jnp.transpose(coded)[: out_ref.shape[1] - 2 * width]
-    gated, coded = gated.astype(bf16), coded.astype(bf16)
-    for d in range(out_ref.shape[0]):
-        out_ref[d, : 2 * width] = gated
-        out_ref[d, 2 * width :] = coded
+        gated = jnp.transpose(jnp.concatenate(attended, axis=1)) * query_ref[width:]
+        coded = jnp.zeros((tile_rows, 128), f32)
+        for h, value in enumerate(sums):
+            if slot == 0:
+                coded = jnp.where(lane == h, value, coded)
+                continue
+            for p in range(3):
+                part = value.astype(bf16).astype(f32)
+                value = value - part
+                coded = jnp.where(lane == p * pairs + h, part, coded)
+        out_ref = sent_ref if slot else kept_ref
+        out_ref[:width] = gated.astype(out_ref.dtype)
+        out_ref[width:] = jnp.transpose(coded)[: out_ref.shape[0] - width].astype(out_ref.dtype)
+
+
+def join_kernel(kept_ref, received_ref, out_ref):
+    width = out_ref.shape[1]
+    pairs = 2
+    head_width = width // pairs
+    first = kept_ref[width : width + pairs]
+    coded = received_ref[width:].astype(f32)
+    last = coded[:pairs] + coded[pairs : 2 * pairs] + coded[2 * pairs : 3 * pairs]
+    top = jnp.maximum(first, last)
+    first, last = jnp.exp(first - top), jnp.exp(last - top)
+    inverse = 1.0 / (first + last)
+    first, last = first * inverse, last * inverse
+    for h in range(pairs):
+        here = pl.ds(h * head_width, head_width)
+        joined = kept_ref[here] * first[h : h + 1]
+        joined += received_ref[here].astype(f32) * last[h : h + 1]
+        for d in range(out_ref.shape[0]):
+            out_ref[d, here] = joined.astype(bf16)
 
 
 def factor_kernel(
-    sent_ref,
+    mixed_ref,
     w_out_ref,
     single_hbm,
     w_factors_hbm,
     out_ref,
     factors_ref,
-    mixed_ref,
     single_ref,
     w_factors_ref,
     sems,
 ):
     copies = start_copies(((single_hbm, single_ref), (w_factors_hbm, w_factors_ref)), sems)
-    targets = sent_ref.shape[0] // 2
-    width = mixed_ref.shape[0] // sent_ref.shape[0]
-    heads_there = 4
-    head_width = 2 * width // heads_there
-
-    def log_sum(d):
-        coded = sent_ref[d, 2 * width :].astype(f32)
-        parts = [coded[p * heads_there : (p + 1) * heads_there] for p in range(3)]
-        return parts[0] + parts[1] + parts[2]
-
-    for d in range(targets):
-        first, last = log_sum(d), log_sum(d + targets)
-        top = jnp.maximum(first, last)
-        first, last = jnp.exp(first - top), jnp.exp(last - top)
-        inverse = 1.0 / (first + last)
-        first, last = first * inverse, last * inverse
-        for h in range(heads_there):
-            rows_here = pl.ds(h * head_width, head_width)
-            joined = (
-                sent_ref[d, rows_here].astype(f32) * first[h : h + 1]
-                + sent_ref[d + targets, rows_here].astype(f32) * last[h : h + 1]
-            )
-            owner = (h * head_width // width) * targets + d
-            place = owner * width + h * head_width % width
-            mixed_ref[place : place + head_width] = joined.astype(bf16)
     mixed = jnp.transpose(mixed_ref[...].astype(f32)).astype(bf16)
     head_total = jnp.dot(mixed, w_out_ref[...], preferred_element_type=f32)
     copies[0].wait()
@@ -214,7 +224,7 @@
 def update_kernel(
     pair_ref,
     left_ref,
-    right_ref,
+    right_factors_ref,
     w_pairout_hbm,
     w_up_hbm,
     w_down_hbm,
@@ -224,36 +234,36 @@
     w_down_ref,
     scale_ref,
     shift_ref,
+    right_ref,
     sems,
 ):
-    copies = [
-        pltpu.make_async_copy(w_pairout_hbm, w_pairout_ref, sems.at[0]),
-        pltpu.make_async_copy(w_up_hbm, w_up_ref, sems.at[1]),
-        pltpu.make_async_copy(w_down_hbm, w_down_ref, sems.at[2]),
-    ]
-
-    @pl.when(pl.program_id(0) == 0)
-    def _():
-        for copy in copies:
-            copy.start()
-
     block_rows, tile_cols, width = pair_ref.shape
     factor_width = width // 2
-    low = lax.broadcasted_iota(jnp.int32, (1, width), 1) < factor_width
-    right = right_ref[:, factor_width:]
-    right = jnp.concatenate([right, right], axis=1)
-    left = left_ref[:, :factor_width].astype(f32)
-    left = jnp.concatenate([left, left], axis=1)
-    scale_ref[...] = jnp.where(low, left, -1.0).astype(bf16)[:, None, :]
-    shift_ref[...] = jnp.where(low, 0.0, left).astype(bf16)[:, None, :]
-    rows_here = block_rows * tile_cols
-    paired = (right[None] * scale_ref[...] + shift_ref[...]).reshape(rows_here, width)
-
-    @pl.when(pl.program_id(0) == 0)
+    at = pl.program_id(0)
+
+    @pl.when(at == 0)
     def _():
+        copies = start_copies(
+            (
+                (w_pairout_hbm, w_pairout_ref),
+                (w_up_hbm, w_up_ref),
+                (w_down_hbm, w_down_ref),
+            ),
+            sems,
+        )
+        right = right_factors_ref[:, factor_width:]
+        right_ref[...] = jnp.concatenate([right, right], axis=1)
+        left = left_ref[:, :factor_width].astype(f32)
+        left = jnp.concatenate([left, left], axis=1)
+        low = lax.broadcasted_iota(jnp.int32, (1, width), 1) < factor_width
+        scale_ref[...] = jnp.where(low, left, -1.0).astype(bf16)[:, None, :]
+        shift_ref[...] = jnp.where(low, 0.0, left).astype(bf16)[:, None, :]
         for copy in copies:
             copy.wait()
 
+    rows_here = block_rows * tile_cols
+    here = pl.ds(at * block_rows, block_rows)
+    paired = (right_ref[...][None] * scale_ref[here] + shift_ref[here]).reshape(rows_here, width)
     moved = jnp.dot(paired, w_pairout_ref[...], preferred_element_type=f32)
     pair_mid = (pair_ref[...].reshape(rows_here, width).astype(f32) + moved).astype(bf16)
     normed = normalize_rows(pair_mid)
@@ -285,6 +295,7 @@
     heads = w_bias.shape[1]
     in_place = pl.BlockSpec(memory_space=pl.ANY)
     in_hbm = pl.BlockSpec(memory_space=pltpu.HBM)
+    in_vmem = pl.BlockSpec(memory_space=pltpu.VMEM)
 
     shifts = rows // 4
     half_rows, half_cols = rows // 2, cols // 2
@@ -350,7 +361,10 @@
         compiler_params=params(28),
         name="bias",
     )(pinned(pair), pinned(jnp.transpose(w_bias)), pinned(residue_mask.reshape(cols, 1, tile_cols)))
-    bias_local, kv_first, kv_last = lax.optimization_barrier((bias_local, kv_first, kv_last))
+    query_other = sent(query, "cols", lambda c: c ^ half_cols)
+    bias_local, kv_first, kv_last, query_other = lax.optimization_barrier(
+        (bias_local, kv_first, kv_last, query_other)
+    )
     groups = [list(range(half_cols)), list(range(half_cols, cols))]
     bias_heads = lax.all_to_all(bias_local, "cols", 0, 0, axis_index_groups=groups, tiled=True)
 
@@ -360,18 +374,33 @@
         around = lambda r: (r & half_rows) | ((r + 2 * s) & (half_rows - 1))
         near.append(sent(both, "rows", around))
     near = jnp.stack(near)
-    query, near = lax.optimization_barrier((query, near))
     far = sent(near, "rows", lambda r: r ^ 1)
-    query_other = sent(query, "cols", lambda c: c ^ half_cols)
-
-    mixed = pl.pallas_call(
+
+    kept, partial = pl.pallas_call(
         attend_kernel,
-        out_shape=jax.ShapeDtypeStruct((cols, 2 * width + 16, tile_rows), bf16),
-        scratch_shapes=[pltpu.VMEM((half_cols, tile_rows, tile_cols), f32)],
+        out_shape=(
+            jax.ShapeDtypeStruct((width + 8, tile_rows), f32),
+            jax.ShapeDtypeStruct((width + 16, tile_rows), bf16),
+        ),
+        in_specs=[in_hbm, in_hbm, in_vmem, in_vmem, in_hbm],
+        scratch_shapes=[
+            pltpu.VMEM((half_cols, tile_rows, tile_cols), f32),
+            pltpu.VMEM(query.shape, f32),
+            pltpu.VMEM(query.shape, f32),
+            pltpu.VMEM(near.shape, bf16),
+            pltpu.SemaphoreType.DMA((3,)),
+        ],
         compiler_params=params(),
         name="attend",
-    )(query, query_other, bias_heads, near, far)
-    mixed_all = lax.all_to_all(mixed, "cols", 0, 0, tiled=True)
+    )(pinned(query), pinned(query_other), bias_heads, near, pinned(far))
+    received = sent(partial, "cols", lambda c: c ^ half_cols)
+    mixed = pl.pallas_call(
+        join_kernel,
+        out_shape=jax.ShapeDtypeStruct((cols, width, tile_rows), bf16),
+        compiler_params=params(),
+        name="join",
+    )(kept, received)
+    mixed_all = lax.all_to_all(mixed, "cols", 0, 0, tiled=True).reshape(single_width, tile_rows)
 
     single_out, factors = pl.pallas_call(
         factor_kernel,
@@ -381,7 +410,6 @@
         ),
         in_specs=[whole(mixed_all.shape), whole(w_out.shape), in_hbm, in_hbm],
         scratch_shapes=[
-            pltpu.VMEM((single_width, tile_rows), bf16),
             pltpu.VMEM(single.shape, bf16),
             pltpu.VMEM(w_factors.shape, bf16),
             pltpu.SemaphoreType.DMA((2,)),
@@ -390,34 +418,28 @@
         name="factor",
     )(mixed_all, w_out, pinned(single), pinned(w_factors))
 
-    swapped = [(a * cols + b, b * cols + a) for a in range(rows) for b in range(cols)]
-    right_factors = lax.ppermute(factors, ("rows", "cols"), swapped)
+    right_factors = sent(factors, both_axes, lambda r, c: (c, r))
 
     block_rows = 32
+    pair_block = pl.BlockSpec((block_rows, tile_cols, pair_width), lambda i: (i, 0, 0))
     updated = pl.pallas_call(
         update_kernel,
         grid=(tile_rows // block_rows,),
-        in_specs=[
-            pl.BlockSpec((block_rows, tile_cols, pair_width), lambda i: (i, 0, 0)),
-            pl.BlockSpec((block_rows, factors.shape[1]), lambda i: (i, 0)),
-            whole(right_factors.shape),
-            in_place,
-            in_place,
-            in_place,
-        ],
-        out_specs=pl.BlockSpec((block_rows, tile_cols, pair_width), lambda i: (i, 0, 0)),
+        in_specs=[pair_block] + [whole(factors.shape)] * 2 + [in_place] * 3,
+        out_specs=pair_block,
         out_shape=jax.ShapeDtypeStruct(pair.shape, bf16),
         scratch_shapes=[
             pltpu.VMEM(w_pairout.shape, bf16),
             pltpu.VMEM(w_up.shape, bf16),
             pltpu.VMEM(w_down.shape, bf16),
-            pltpu.VMEM((block_rows, 1, pair_width), bf16),
-            pltpu.VMEM((block_rows, 1, pair_width), bf16),
+            pltpu.VMEM((tile_rows, 1, pair_width), bf16),
+            pltpu.VMEM((tile_rows, 1, pair_width), bf16),
+            pltpu.VMEM((tile_cols, pair_width), bf16),
             pltpu.SemaphoreType.DMA((3,)),
         ],
         compiler_params=params(20),
         name="update",
-    )(pair, factors, right_factors, pinned(w_pairout), pinned(w_up), pinned(w_down))
+    )(pair, factors, right_factors, w_pairout, w_up, w_down)
     return (single_out, updated)
 
 

time: 96.1 us -> 88.8 us (0.924)
  blocking collectives: 25.3 us -> 13.7 us
  waiting for transfers between devices: 22.1 us -> 25.4 us
  starting transfers between devices: 18.6 us -> 20.8 us
  local copies, waits for them, and re-layouts: 1.66 us -> 0.03 us
    all_to_all x1, blocking collectives: 25.3 us -> 13.7 us  [per_device(): lax.all_to_all(mixed, 'cols', 0, 0, tiled=True)]
    ppermute x7 -> x9, waiting for transfers between devices: 10.9 us -> 22.2 us  [sent(): return lax.ppermute(value, axes, routes)]
    ppermute x1 -> x0, waiting for transfers between devices: 11.2 us -> none  [per_device(): right_factors = lax.ppermute(factors, ('rows', 'cols'), swapped)]
    ppermute x7 -> x9, starting transfers between devices: 11.6 us -> 16 us  [sent(): return lax.ppermute(value, axes, routes)]
    all_to_all x1, waiting for transfers between devices: 0.01 us -> 3.16 us  [per_device(): lax.all_to_all(bias_local, 'cols', 0, 0, axis_index_groups=groups, tiled=...]
    ppermute x1 -> x0, starting transfers between devices: 2.1 us -> none  [per_device(): right_factors = lax.ppermute(factors, ('rows', 'cols'), swapped)]
    unnamed x8 -> x14, local copies, waits for them, and re-layouts: 1.66 us -> 0.03 us
    pallas_call x1 -> x2, Pallas kernels: 1.68 us -> 2.88 us  [the longest x1 2.84 us: per_device(): pl.pallas_call(attend_kernel, out_shape=(jax.ShapeDtypeStruct((width + 8,...]
  transfers between devices with their start and end apart: 9 -> 10, of which waited for: 4 -> 6; matrix products, arithmetic and copies ran while one was open for 0% -> 0% of each run, Pallas kernels for 7% -> 8%
where the time goes in v6:
time: 88.8 us; the launch traced here: 88.6 us
  Pallas kernels  27.6 us (31%)
  waiting for transfers between devices  25.4 us (29%)
  starting transfers between devices  20.8 us (23%)
  blocking collectives  13.7 us (15%)
  between operations  0.96 us (1%)
    ppermute x9, waiting for transfers between devices, sent(): return lax.ppermute(value, axes, routes)  22.2 us
    ppermute x9, starting transfers between devices, sent(): return lax.ppermute(value, axes, routes)  16 us
    pallas_call x1, Pallas kernels, per_device(): pl.pallas_call(update_kernel, grid=(tile_rows // block_rows,), in_specs=[...  14.2 us
    all_to_all x1, blocking collectives, per_device(): lax.all_to_all(mixed, 'cols', 0, 0, tiled=True)  13.7 us
    pallas_call x1, Pallas kernels, per_device(): pl.pallas_call(bias_kernel, out_shape=jax.ShapeDtypeStruct(sent_shape, bf...  6.76 us
    all_to_all x1, starting transfers between devices, per_device(): lax.all_to_all(bias_local, 'cols', 0, 0, axis_index_groups=groups, tiled=...  4.77 us
    all_to_all x1, waiting for transfers between devices, per_device(): lax.all_to_all(bias_local, 'cols', 0, 0, axis_index_groups=groups, tiled=...  3.16 us
    pallas_call x1, Pallas kernels, per_device(): pl.pallas_call(attend_kernel, out_shape=(jax.ShapeDtypeStruct((width + 8,...  2.84 us
  transfers between devices with their start and end apart: 10, of which 6 were waited for; matrix products, arithmetic and copies ran while one was open for 0% of the time, Pallas kernels for 8%

profile of v6, /device:TPU:88, one launch (start us, length us, event | category | flops | bytes accessed | tf_op | source)
XLA Modules:
  0.0 88.6 jit_solution(10870777654628702731)
XLA Ops:
  0.6 1.5 %project.1 = (f32[128,128]{1,0:T(8,128)S(1)}, bf16[128,128]{1,0:T(8,128)(2,1)S(1)}) custom-call(bf16[128,1024]{1,0:T(8,128)(2,1)} %single_hbm.3, bf16[256,1024]{1,0:T(8,128)(2,1)} %bitcast.14), custom_call_target="tpu_custom_call" | custom-call | tf_op jit(solution)/shard_map/project/pallas_call | solution.py:325
  2.2 0.0 copy-start.4
  2.2 0.1 collective-permute-start.2
  2.3 2.9 %collective-permute-start.1 = (bf16[128,128]{1,0:T(8,128)(2,1)S(1)}, bf16[128,128]{1,0:T(8,128)(2,1)S(1)}, u32[]{:S(2)}, u32[]{:S(2)}) collective-permute-start(bf16[128,128]{1,0:T(8,128)(2,1)S(1)} %get-tuple-element.14), channel_id=1, source_target_pairs={{0,128},{1,129},{2,130},{3,131},{4,132},{5,133},{6,134},{7,135},{8... | collective-permute-start | bytes 98312 | tf_op jit(solution)/shard_map/ppermute | solution.py:315
  5.2 6.4 %collective-permute-start = (bf16[128,128]{1,0:T(8,128)(2,1)S(1)}, bf16[128,128]{1,0:T(8,128)(2,1)S(1)}, u32[]{:S(2)}, u32[]{:S(2)}) collective-permute-start(bf16[128,128]{1,0:T(8,128)(2,1)S(1)} %get-tuple-element.14), channel_id=1, source_target_pairs={{0,0},{1,1},{2,2},{3,3},{4,4},{5,5},{6,6},{7,7},{8,128},{9,129},{1... | collective-permute-start | bytes 98312 | tf_op jit(solution)/shard_map/ppermute | solution.py:315
  11.6 0.0 copy-start.1
  11.6 6.8 %bias.1 = bf16[8,4,128,128]{3,2,1,0:T(8,128)(2,1)} custom-call(bf16[128,128,128]{2,1,0:T(8,128)(2,1)} %pair_ref.1, bf16[32,128]{1,0:T(8,128)(2,1)} %bitcast.20, s32[16,1,128]{2,1,0:T(1,128)} %bitcast.21), custom_call_target="tpu_custom_call" | custom-call | tf_op jit(solution)/shard_map/bias/pallas_call | solution.py:347
  18.3 0.0 copy-start.2
  18.4 0.0 collective-permute-done.1
  18.4 0.0 collective-permute-done
  18.4 0.0 collective-permute-done.2.other_hbm
  18.4 0.0 copy-start.6
  18.4 4.8 %all-to-all-start = ((bf16[8,4,128,128]{3,2,1,0:T(8,128)(2,1)}), bf16[8,4,128,128]{3,2,1,0:T(8,128)(2,1)S(1)}, u32[]{:S(2)}, u32[]{:S(2)}) async-start(bf16[8,4,128,128]{3,2,1,0:T(8,128)(2,1)} %bias.1), calls=%async_computation | async-start | bytes 2097152 | tf_op jit(solution)/shard_map/all_to_all | solution.py:369
  23.2 0.0 copy-done.6
  23.2 1.3 %collective-permute-start.4 = (bf16[2,128,128]{2,1,0:T(8,128)(2,1)S(1)}, bf16[2,128,128]{2,1,0:T(8,128)(2,1)S(1)}, u32[]{:S(2)}, u32[]{:S(2)}) collective-permute-start(bf16[2,128,128]{2,1,0:T(8,128)(2,1)S(1)} %get-tuple-element.25), channel_id=1, source_target_pairs={{0,64},{16,80},{32,96},{48,112},{64,0},{80,16},{96,32},{112,48},{1... | collective-permute-start | bytes 196616 | tf_op jit(solution)/shard_map/ppermute | solution.py:315
  24.5 2.2 %collective-permute-start.3 = (bf16[2,128,128]{2,1,0:T(8,128)(2,1)S(1)}, bf16[2,128,128]{2,1,0:T(8,128)(2,1)S(1)}, u32[]{:S(2)}, u32[]{:S(2)}) collective-permute-start(bf16[2,128,128]{2,1,0:T(8,128)(2,1)S(1)} %get-tuple-element.25), channel_id=1, source_target_pairs={{0,32},{16,48},{32,64},{48,80},{64,96},{80,112},{96,0},{112,16},{1... | collective-permute-start | bytes 196616 | tf_op jit(solution)/shard_map/ppermute | solution.py:315
  26.7 0.0 collective-permute-start.5
  26.7 2.4 %collective-permute-done.4 = bf16[2,128,128]{2,1,0:T(8,128)(2,1)S(1)} collective-permute-done((bf16[2,128,128]{2,1,0:T(8,128)(2,1)S(1)}, bf16[2,128,128]{2,1,0:T(8,128)(2,1)S(1)}, u32[]{:S(2)}, u32[]{:S(2)}) %collective-permute-start.4) | collective-permute-done | bytes 65568 | tf_op jit(solution)/shard_map/ppermute | solution.py:315
  29.1 0.0 collective-permute-done.3
  29.1 3.1 %collective-permute-done.5 = bf16[2,128,128]{2,1,0:T(8,128)(2,1)S(1)} collective-permute-done((bf16[2,128,128]{2,1,0:T(8,128)(2,1)S(1)}, bf16[2,128,128]{2,1,0:T(8,128)(2,1)S(1)}, u32[]{:S(2)}, u32[]{:S(2)}) %collective-permute-start.5) | collective-permute-done | bytes 65568 | tf_op jit(solution)/shard_map/ppermute | solution.py:315
  32.2 0.0 copy-done.4
  32.2 0.1 collective-permute-start.6
  32.3 1.7 %collective-permute-done.6.far_hbm = bf16[4,2,128,128]{3,2,1,0:T(8,128)(2,1)} collective-permute-done((bf16[4,2,128,128]{3,2,1,0:T(8,128)(2,1)S(1)}, bf16[4,2,128,128]{3,2,1,0:T(8,128)(2,1)}, u32[]{:S(2)}, u32[]{:S(2)}) %collective-permute-start.6) | collective-permute-done | bytes 262176 | tf_op jit(solution)/shard_map/ppermute | solution.py:315
  34.0 3.2 %all-to-all-done.bias_ref = bf16[8,4,128,128]{3,2,1,0:T(8,128)(2,1)S(1)} async-done(((bf16[8,4,128,128]{3,2,1,0:T(8,128)(2,1)}), bf16[8,4,128,128]{3,2,1,0:T(8,128)(2,1)S(1)}, u32[]{:S(2)}, u32[]{:S(2)}) %all-to-all-start) | async-done | bytes 1048608 | tf_op jit(solution)/shard_map/all_to_all | solution.py:369
  37.1 0.0 copy-start
  37.1 0.0 copy-start.3
  37.1 0.0 copy-start.5
  37.1 2.8 %attend.1 = (f32[72,128]{1,0:T(8,128)S(1)}, bf16[80,128]{1,0:T(8,128)(2,1)S(1)}) custom-call(f32[128,128]{1,0:T(8,128)} %copy-done.4, f32[128,128]{1,0:T(8,128)} %copy-done.6, bf16[8,4,128,128]{3,2,1,0:T(8,128)(2,1)S(1)} %all-to-all-done.bias_ref, bf16[4,2,128,128]{3,2,1,0:T(8,128)(2,1)S(1)} %pad_maximum_fusion.near_ref, ...), custom_call_target="tpu_custom_call" | custom-call | tf_op jit(solution)/shard_map/attend/pallas_call | solution.py:379
  40.0 0.1 collective-permute-start.7
  40.1 4.7 %collective-permute-done.7.received_ref = bf16[80,128]{1,0:T(8,128)(2,1)S(1)} collective-permute-done((bf16[80,128]{1,0:T(8,128)(2,1)S(1)}, bf16[80,128]{1,0:T(8,128)(2,1)S(1)}, u32[]{:S(2)}, u32[]{:S(2)}) %collective-permute-start.7) | collective-permute-done | bytes 20512 | tf_op jit(solution)/shard_map/ppermute | solution.py:315
  44.8 13.7 %all_to_all.10 = bf16[16,64,128]{2,1,0:T(8,128)(2,1)S(1)} all-to-all(bf16[16,64,128]{2,1,0:T(8,128)(2,1)S(1)} %join.1), channel_id=1, replica_groups=mesh['rows'=16,'cols'=16] {'cols'}, dimensions={0} | all-to-all | bytes 524288 | tf_op jit(solution)/shard_map/all_to_all | solution.py:403
  58.6 0.0 copy-done.1
  58.6 2.3 %factor.1 = (bf16[128,1024]{1,0:T(8,128)(2,1)}, bf16[128,128]{1,0:T(8,128)(2,1)S(1)}) custom-call(bf16[1024,128]{1,0:T(8,128)(2,1)S(1)} %bitcast.13, bf16[1024,1024]{1,0:T(8,128)(2,1)S(1)} %copy-done.1, bf16[128,1024]{1,0:T(8,128)(2,1)} %single_hbm.3, bf16[1024,128]{1,0:T(8,128)(2,1)} %w_factors_hbm.1), custom_call_target="tpu_custom_call" | custom-call | tf_op jit(solution)/shard_map/factor/pallas_call | solution.py:405
  60.8 2.9 %collective-permute-start.8 = (bf16[128,128]{1,0:T(8,128)(2,1)S(1)}, bf16[128,128]{1,0:T(8,128)(2,1)S(1)}, u32[]{:S(2)}, u32[]{:S(2)}) collective-permute-start(bf16[128,128]{1,0:T(8,128)(2,1)S(1)} %get-tuple-element.23.left_ref), channel_id=1, source_target_pairs={{0,0},{1,16},{2,32},{3,48},{4,64},{5,80},{6,96},{7,112},{8,128},{9... | collective-permute-start | bytes 98312 | tf_op jit(solution)/shard_map/ppermute | solution.py:315
  63.8 10.4 %collective-permute-done.8.right_factors_ref = bf16[128,128]{1,0:T(8,128)(2,1)S(1)} collective-permute-done((bf16[128,128]{1,0:T(8,128)(2,1)S(1)}, bf16[128,128]{1,0:T(8,128)(2,1)S(1)}, u32[]{:S(2)}, u32[]{:S(2)}) %collective-permute-start.8) | collective-permute-done | bytes 32800 | tf_op jit(solution)/shard_map/ppermute | solution.py:315
  74.2 0.0 copy-done.2
  74.2 0.0 copy-done
  74.2 0.0 copy-done.3
  74.2 0.0 copy-done.5
  74.2 14.2 %update.1 = bf16[128,128,128]{2,1,0:T(8,128)(2,1)} custom-call(bf16[128,128,128]{2,1,0:T(8,128)(2,1)S(1)} %copy-done, bf16[128,128]{1,0:T(8,128)(2,1)S(1)} %get-tuple-element.23.left_ref, bf16[128,128]{1,0:T(8,128)(2,1)S(1)} %collective-permute-done.8.right_factors_ref, bf16[128,128]{1,0:T(8,128)(2,1)S(1)} %copy-done.5, bf16[128,512]{1,0:T(8,128)(2,1)S(1)} %copy-done.2, ...), custom_call_target="tpu_custom_call" | custom-call | tf_op jit(solution)/shard_map/update/pallas_call | solution.py:425
  (3 shorter events, 0.1 us)
Async XLA Ops:
  2.2 30.0 %copy-start.4 = (f32[128,128]{1,0:T(8,128)}, f32[128,128]{1,0:T(8,128)S(1)}, u32[]{:S(2)}) copy-start(f32[128,128]{1,0:T(8,128)S(1)} %get-tuple-element.13.own_hbm) | copy-start | bytes 196612
  2.2 16.2 %collective-permute-start.2 = (f32[128,128]{1,0:T(8,128)S(1)}, f32[128,128]{1,0:T(8,128)S(1)}, u32[]{:S(2)}, u32[]{:S(2)}) collective-permute-start(f32[128,128]{1,0:T(8,128)S(1)} %get-tuple-element.13.own_hbm), channel_id=1, source_target_pairs={{0,8},{1,9},{2,10},{3,11},{4,12},{5,13},{6,14},{7,15},{8,0},{9,1},... | collective-permute-start | bytes 196616 | tf_op jit(solution)/shard_map/ppermute | solution.py:315
  2.3 16.1 %collective-permute-start.1 = (bf16[128,128]{1,0:T(8,128)(2,1)S(1)}, bf16[128,128]{1,0:T(8,128)(2,1)S(1)}, u32[]{:S(2)}, u32[]{:S(2)}) collective-permute-start(bf16[128,128]{1,0:T(8,128)(2,1)S(1)} %get-tuple-element.14), channel_id=1, source_target_pairs={{0,128},{1,129},{2,130},{3,131},{4,132},{5,133},{6,134},{7,135},{8... | collective-permute-start | bytes 98312 | tf_op jit(solution)/shard_map/ppermute | solution.py:315
  5.2 13.2 %collective-permute-start = (bf16[128,128]{1,0:T(8,128)(2,1)S(1)}, bf16[128,128]{1,0:T(8,128)(2,1)S(1)}, u32[]{:S(2)}, u32[]{:S(2)}) collective-permute-start(bf16[128,128]{1,0:T(8,128)(2,1)S(1)} %get-tuple-element.14), channel_id=1, source_target_pairs={{0,0},{1,1},{2,2},{3,3},{4,4},{5,5},{6,6},{7,7},{8,128},{9,129},{1... | collective-permute-start | bytes 98312 | tf_op jit(solution)/shard_map/ppermute | solution.py:315
  11.6 47.0 %copy-start.1 = (bf16[1024,1024]{1,0:T(8,128)(2,1)S(1)}, bf16[1024,1024]{1,0:T(8,128)(2,1)}, u32[]{:S(2)}) copy-start(bf16[1024,1024]{1,0:T(8,128)(2,1)} %w_out_ref.1) | copy-start | bytes 6291460
  18.3 55.8 %copy-start.2 = (bf16[128,512]{1,0:T(8,128)(2,1)S(1)}, bf16[128,512]{1,0:T(8,128)(2,1)}, u32[]{:S(2)}) copy-start(bf16[128,512]{1,0:T(8,128)(2,1)} %w_up_hbm.1) | copy-start | bytes 393220
  18.4 4.8 %copy-start.6 = (f32[128,128]{1,0:T(8,128)}, f32[128,128]{1,0:T(8,128)S(1)}, u32[]{:S(2)}) copy-start(f32[128,128]{1,0:T(8,128)S(1)} %collective-permute-done.2.other_hbm) | copy-start | bytes 196612
  18.4 18.7 %all-to-all-start = ((bf16[8,4,128,128]{3,2,1,0:T(8,128)(2,1)}), bf16[8,4,128,128]{3,2,1,0:T(8,128)(2,1)S(1)}, u32[]{:S(2)}, u32[]{:S(2)}) async-start(bf16[8,4,128,128]{3,2,1,0:T(8,128)(2,1)} %bias.1), calls=%async_computation | async-start | bytes 2097152 | tf_op jit(solution)/shard_map/all_to_all | solution.py:369
  23.2 5.9 %collective-permute-start.4 = (bf16[2,128,128]{2,1,0:T(8,128)(2,1)S(1)}, bf16[2,128,128]{2,1,0:T(8,128)(2,1)S(1)}, u32[]{:S(2)}, u32[]{:S(2)}) collective-permute-start(bf16[2,128,128]{2,1,0:T(8,128)(2,1)S(1)} %get-tuple-element.25), channel_id=1, source_target_pairs={{0,64},{16,80},{32,96},{48,112},{64,0},{80,16},{96,32},{112,48},{1... | collective-permute-start | bytes 196616 | tf_op jit(solution)/shard_map/ppermute | solution.py:315
  24.5 4.6 %collective-permute-start.3 = (bf16[2,128,128]{2,1,0:T(8,128)(2,1)S(1)}, bf16[2,128,128]{2,1,0:T(8,128)(2,1)S(1)}, u32[]{:S(2)}, u32[]{:S(2)}) collective-permute-start(bf16[2,128,128]{2,1,0:T(8,128)(2,1)S(1)} %get-tuple-element.25), channel_id=1, source_target_pairs={{0,32},{16,48},{32,64},{48,80},{64,96},{80,112},{96,0},{112,16},{1... | collective-permute-start | bytes 196616 | tf_op jit(solution)/shard_map/ppermute | solution.py:315
  26.7 5.5 %collective-permute-start.5 = (bf16[2,128,128]{2,1,0:T(8,128)(2,1)S(1)}, bf16[2,128,128]{2,1,0:T(8,128)(2,1)S(1)}, u32[]{:S(2)}, u32[]{:S(2)}) collective-permute-start(bf16[2,128,128]{2,1,0:T(8,128)(2,1)S(1)} %get-tuple-element.25), channel_id=1, source_target_pairs={{0,96},{16,112},{32,0},{48,16},{64,32},{80,48},{96,64},{112,80},{1... | collective-permute-start | bytes 196616 | tf_op jit(solution)/shard_map/ppermute | solution.py:315
  32.2 1.8 %collective-permute-start.6 = (bf16[4,2,128,128]{3,2,1,0:T(8,128)(2,1)S(1)}, bf16[4,2,128,128]{3,2,1,0:T(8,128)(2,1)}, u32[]{:S(2)}, u32[]{:S(2)}) collective-permute-start(bf16[4,2,128,128]{3,2,1,0:T(8,128)(2,1)S(1)} %pad_maximum_fusion.near_ref), channel_id=1, source_target_pairs={{0,16},{16,0},{32,48},{48,32},{64,80},{80,64},{96,112},{112,96},{1... | collective-permute-start | bytes 786440 | tf_op jit(solution)/shard_map/ppermute | solution.py:315
  37.1 37.0 %copy-start = (bf16[128,128,128]{2,1,0:T(8,128)(2,1)S(1)}, bf16[128,128,128]{2,1,0:T(8,128)(2,1)}, u32[]{:S(2)}) copy-start(bf16[128,128,128]{2,1,0:T(8,128)(2,1)} %pair_ref.1) | copy-start | bytes 12582916
  37.1 37.0 %copy-start.3 = (bf16[512,128]{1,0:T(8,128)(2,1)S(1)}, bf16[512,128]{1,0:T(8,128)(2,1)}, u32[]{:S(2)}) copy-start(bf16[512,128]{1,0:T(8,128)(2,1)} %w_down_hbm.1) | copy-start | bytes 393220
  37.1 37.0 %copy-start.5 = (bf16[128,128]{1,0:T(8,128)(2,1)S(1)}, bf16[128,128]{1,0:T(8,128)(2,1)}, u32[]{:S(2)}) copy-start(bf16[128,128]{1,0:T(8,128)(2,1)} %w_pairout_hbm.1) | copy-start | bytes 98308
  40.0 4.8 %collective-permute-start.7 = (bf16[80,128]{1,0:T(8,128)(2,1)S(1)}, bf16[80,128]{1,0:T(8,128)(2,1)S(1)}, u32[]{:S(2)}, u32[]{:S(2)}) collective-permute-start(bf16[80,128]{1,0:T(8,128)(2,1)S(1)} %get-tuple-element.21), channel_id=1, source_target_pairs={{0,8},{1,9},{2,10},{3,11},{4,12},{5,13},{6,14},{7,15},{8,0},{9,1},... | collective-permute-start | bytes 61448 | tf_op jit(solution)/shard_map/ppermute | solution.py:315
  60.8 13.3 %collective-permute-start.8 = (bf16[128,128]{1,0:T(8,128)(2,1)S(1)}, bf16[128,128]{1,0:T(8,128)(2,1)S(1)}, u32[]{:S(2)}, u32[]{:S(2)}) collective-permute-start(bf16[128,128]{1,0:T(8,128)(2,1)S(1)} %get-tuple-element.23.left_ref), channel_id=1, source_target_pairs={{0,0},{1,16},{2,32},{3,48},{4,64},{5,80},{6,96},{7,112},{8,128},{9... | collective-permute-start | bytes 98312 | tf_op jit(solution)/shard_map/ppermute | solution.py:315

commit v7 on v6

--- a/solution.py
+++ b/solution.py
@@ -70,7 +70,7 @@
     tile_rows, tile_cols, width = pair_ref.shape
     targets, heads_there = staged_ref.shape[:2]
     pairs = heads_there // 2
-    ends = [tile_rows // 4, 3 * tile_rows // 4, tile_rows]
+    ends = [tile_rows // 4, tile_rows]
     parts = [(weight_hbm, weight_ref), (mask_hbm.at[lax.axis_index("cols")], mask_ref)]
     at = 0
     for end in ends:
@@ -112,8 +112,12 @@
     bias_ref,
     near_ref,
     far_hbm,
+    single_hbm,
+    w_factors_hbm,
     kept_ref,
     sent_ref,
+    single_ref,
+    w_factors_ref,
     score_ref,
     own_ref,
     other_ref,
@@ -121,7 +125,14 @@
     sems,
 ):
     copies = start_copies(
-        ((own_hbm, own_ref), (other_hbm, other_ref), (far_hbm, far_ref)), sems
+        (
+            (own_hbm, own_ref),
+            (other_hbm, other_ref),
+            (far_hbm, far_ref),
+            (single_hbm, single_ref),
+            (w_factors_hbm, w_factors_ref),
+        ),
+        sems,
     )
     blocks, heads_there, tile_rows, tile_cols = bias_ref.shape
     width = own_ref.shape[0] // 2
@@ -138,7 +149,7 @@
         near, far = near_ref[sent, half ^ z, part, :], far_ref[sent, half ^ z, part, :]
         return jnp.where(core == b % 2, near, far)
 
-    for copy in copies:
+    for copy in copies[:3]:
         copy.wait()
     lane = lax.broadcasted_iota(jnp.int32, (tile_rows, 128), 1)
     for slot, query_ref in enumerate((own_ref, other_ref)):
@@ -178,6 +189,8 @@
         out_ref = sent_ref if slot else kept_ref
         out_ref[:width] = gated.astype(out_ref.dtype)
         out_ref[width:] = jnp.transpose(coded)[: out_ref.shape[0] - width].astype(out_ref.dtype)
+    for copy in copies[3:]:
+        copy.wait()
 
 
 def join_kernel(kept_ref, received_ref, out_ref):
@@ -202,40 +215,42 @@
 def factor_kernel(
     mixed_ref,
     w_out_ref,
-    single_hbm,
-    w_factors_hbm,
+    single_ref,
+    w_factors_ref,
+    w_pairout_hbm,
+    w_up_hbm,
+    w_down_hbm,
     out_ref,
     factors_ref,
-    single_ref,
-    w_factors_ref,
+    w_pairout_ref,
+    w_up_ref,
+    w_down_ref,
     sems,
 ):
-    copies = start_copies(((single_hbm, single_ref), (w_factors_hbm, w_factors_ref)), sems)
+    copies = start_copies(
+        ((w_pairout_hbm, w_pairout_ref), (w_up_hbm, w_up_ref), (w_down_hbm, w_down_ref)), sems
+    )
     mixed = jnp.transpose(mixed_ref[...].astype(f32)).astype(bf16)
     head_total = jnp.dot(mixed, w_out_ref[...], preferred_element_type=f32)
-    copies[0].wait()
     single_out = (single_ref[...].astype(f32) + head_total).astype(bf16)
     out_ref[...] = single_out
     normed = normalize(single_out.astype(f32)).astype(bf16)
-    copies[1].wait()
     factors_ref[...] = jnp.dot(normed, w_factors_ref[...], preferred_element_type=f32).astype(bf16)
+    for copy in copies:
+        copy.wait()
 
 
 def update_kernel(
     pair_ref,
     left_ref,
     right_factors_ref,
-    w_pairout_hbm,
-    w_up_hbm,
-    w_down_hbm,
-    out_ref,
     w_pairout_ref,
     w_up_ref,
     w_down_ref,
+    out_ref,
     scale_ref,
     shift_ref,
     right_ref,
-    sems,
 ):
     block_rows, tile_cols, width = pair_ref.shape
     factor_width = width // 2
@@ -243,14 +258,6 @@
 
     @pl.when(at == 0)
     def _():
-        copies = start_copies(
-            (
-                (w_pairout_hbm, w_pairout_ref),
-                (w_up_hbm, w_up_ref),
-                (w_down_hbm, w_down_ref),
-            ),
-            sems,
-        )
         right = right_factors_ref[:, factor_width:]
         right_ref[...] = jnp.concatenate([right, right], axis=1)
         left = left_ref[:, :factor_width].astype(f32)
@@ -258,8 +265,6 @@
         low = lax.broadcasted_iota(jnp.int32, (1, width), 1) < factor_width
         scale_ref[...] = jnp.where(low, left, -1.0).astype(bf16)[:, None, :]
         shift_ref[...] = jnp.where(low, 0.0, left).astype(bf16)[:, None, :]
-        for copy in copies:
-            copy.wait()
 
     rows_here = block_rows * tile_cols
     here = pl.ds(at * block_rows, block_rows)
@@ -271,6 +276,30 @@
     hidden = jnp.maximum(hidden, 0)
     down = jnp.dot(hidden, w_down_ref[...], preferred_element_type=f32)
     out_ref[...] = (pair_mid.astype(f32) + down).astype(bf16).reshape(pair_ref.shape)
+
+
+def nearest_rows(row, count):
+    def ring(a, b, length):
+        apart = abs(a - b) % length
+        return min(apart, length - apart)
+
+    def cost(col, target):
+        z = (row // 8) * 4 + col // 4, (target // 8) * 4 + row // 4
+        y = (row // 2) % 4, (target // 2) % 4
+        apart = ring(*z, 8) + ring(*y, 4) + ring(col % 4, row % 4, 4) + 0.3 * (row % 2 != target % 2)
+        return apart**4
+
+    chosen = list(range(count))
+    better = True
+    while better:
+        better = False
+        for a in range(count):
+            for b in range(a):
+                now = cost(a, chosen[a]) + cost(b, chosen[b])
+                if cost(a, chosen[b]) + cost(b, chosen[a]) < now - 1e-9:
+                    chosen[a], chosen[b] = chosen[b], chosen[a]
+                    better = True
+    return chosen
 
 
 def whole(shape):
@@ -353,18 +382,16 @@
             pltpu.VMEM(pair.shape, bf16),
             pltpu.VMEM((heads, pair_width), bf16),
             pltpu.VMEM((1, tile_cols), jnp.int32),
-            pltpu.VMEM((heads, tile_rows // 2, tile_cols), f32),
+            pltpu.VMEM((heads, 3 * tile_rows // 4, tile_cols), f32),
             pltpu.VMEM(sent_shape, bf16),
-            pltpu.SemaphoreType.DMA((5,)),
-            pltpu.SemaphoreType.DMA((3,)),
+            pltpu.SemaphoreType.DMA((4,)),
+            pltpu.SemaphoreType.DMA((2,)),
         ],
         compiler_params=params(28),
         name="bias",
     )(pinned(pair), pinned(jnp.transpose(w_bias)), pinned(residue_mask.reshape(cols, 1, tile_cols)))
     query_other = sent(query, "cols", lambda c: c ^ half_cols)
-    bias_local, kv_first, kv_last, query_other = lax.optimization_barrier(
-        (bias_local, kv_first, kv_last, query_other)
-    )
+    bias_local, kv_first, kv_last = lax.optimization_barrier((bias_local, kv_first, kv_last))
     groups = [list(range(half_cols)), list(range(half_cols, cols))]
     bias_heads = lax.all_to_all(bias_local, "cols", 0, 0, axis_index_groups=groups, tiled=True)
 
@@ -373,26 +400,37 @@
     for s in range(1, shifts):
         around = lambda r: (r & half_rows) | ((r + 2 * s) & (half_rows - 1))
         near.append(sent(both, "rows", around))
+    near[-1], query_other = lax.optimization_barrier((near[-1], query_other))
     near = jnp.stack(near)
     far = sent(near, "rows", lambda r: r ^ 1)
 
-    kept, partial = pl.pallas_call(
+    kept, partial, single_near, w_factors_near = pl.pallas_call(
         attend_kernel,
         out_shape=(
             jax.ShapeDtypeStruct((width + 8, tile_rows), f32),
             jax.ShapeDtypeStruct((width + 16, tile_rows), bf16),
+            jax.ShapeDtypeStruct(single.shape, bf16),
+            jax.ShapeDtypeStruct(w_factors.shape, bf16),
         ),
-        in_specs=[in_hbm, in_hbm, in_vmem, in_vmem, in_hbm],
+        in_specs=[in_hbm, in_hbm, in_vmem, in_vmem, in_hbm, in_hbm, in_hbm],
         scratch_shapes=[
             pltpu.VMEM((half_cols, tile_rows, tile_cols), f32),
             pltpu.VMEM(query.shape, f32),
             pltpu.VMEM(query.shape, f32),
             pltpu.VMEM(near.shape, bf16),
-            pltpu.SemaphoreType.DMA((3,)),
+            pltpu.SemaphoreType.DMA((5,)),
         ],
         compiler_params=params(),
         name="attend",
-    )(pinned(query), pinned(query_other), bias_heads, near, pinned(far))
+    )(
+        pinned(query),
+        pinned(query_other),
+        bias_heads,
+        near,
+        pinned(far),
+        pinned(single),
+        pinned(w_factors),
+    )
     received = sent(partial, "cols", lambda c: c ^ half_cols)
     mixed = pl.pallas_call(
         join_kernel,
@@ -402,44 +440,40 @@
     )(kept, received)
     mixed_all = lax.all_to_all(mixed, "cols", 0, 0, tiled=True).reshape(single_width, tile_rows)
 
-    single_out, factors = pl.pallas_call(
+    single_out, factors, pairout_near, up_near, down_near = pl.pallas_call(
         factor_kernel,
         out_shape=(
             jax.ShapeDtypeStruct(single.shape, bf16),
             jax.ShapeDtypeStruct((tile_rows, w_factors.shape[1]), bf16),
+            jax.ShapeDtypeStruct(w_pairout.shape, bf16),
+            jax.ShapeDtypeStruct(w_up.shape, bf16),
+            jax.ShapeDtypeStruct(w_down.shape, bf16),
         ),
-        in_specs=[whole(mixed_all.shape), whole(w_out.shape), in_hbm, in_hbm],
-        scratch_shapes=[
-            pltpu.VMEM(single.shape, bf16),
-            pltpu.VMEM(w_factors.shape, bf16),
-            pltpu.SemaphoreType.DMA((2,)),
-        ],
+        in_specs=[in_vmem] * 4 + [in_hbm] * 3,
+        scratch_shapes=[pltpu.SemaphoreType.DMA((3,))],
         compiler_params=params(),
         name="factor",
-    )(mixed_all, w_out, pinned(single), pinned(w_factors))
-
-    right_factors = sent(factors, both_axes, lambda r, c: (c, r))
+    )(mixed_all, w_out, single_near, w_factors_near, pinned(w_pairout), pinned(w_up), pinned(w_down))
+
+    targets = [nearest_rows(row, rows) for row in range(rows)]
+    right_factors = sent(factors, both_axes, lambda r, c: (targets[r][c], r))
 
     block_rows = 32
     pair_block = pl.BlockSpec((block_rows, tile_cols, pair_width), lambda i: (i, 0, 0))
     updated = pl.pallas_call(
         update_kernel,
         grid=(tile_rows // block_rows,),
-        in_specs=[pair_block] + [whole(factors.shape)] * 2 + [in_place] * 3,
+        in_specs=[pair_block] + [whole(factors.shape)] * 2 + [in_vmem] * 3,
         out_specs=pair_block,
         out_shape=jax.ShapeDtypeStruct(pair.shape, bf16),
         scratch_shapes=[
-            pltpu.VMEM(w_pairout.shape, bf16),
-            pltpu.VMEM(w_up.shape, bf16),
-            pltpu.VMEM(w_down.shape, bf16),
             pltpu.VMEM((tile_rows, 1, pair_width), bf16),
             pltpu.VMEM((tile_rows, 1, pair_width), bf16),
             pltpu.VMEM((tile_cols, pair_width), bf16),
-            pltpu.SemaphoreType.DMA((3,)),
         ],
         compiler_params=params(20),
         name="update",
-    )(pair, factors, right_factors, w_pairout, w_up, w_down)
+    )(pair, factors, right_factors, pairout_near, up_near, down_near)
     return (single_out, updated)
 
 

time: 88.8 us -> 87 us (0.980)
  starting transfers between devices: 20.8 us -> 17.4 us
  blocking collectives: 13.7 us -> 16.3 us
    ppermute x9, starting transfers between devices: 16 us -> 12.5 us  [sent(): return lax.ppermute(value, axes, routes)]
    ppermute x9, waiting for transfers between devices: 22.2 us -> 25.4 us  [sent(): return lax.ppermute(value, axes, routes)]
    all_to_all x1, waiting for transfers between devices: 3.16 us -> 0.01 us  [per_device(): lax.all_to_all(bias_local, 'cols', 0, 0, axis_index_groups=groups, tiled=...]
    all_to_all x1, blocking collectives: 13.7 us -> 16.3 us  [per_device(): lax.all_to_all(mixed, 'cols', 0, 0, tiled=True)]
  transfers between devices with their start and end apart: 10 -> 10, of which waited for: 6 -> 4; matrix products, arithmetic and copies ran while one was open for 0% -> 0% of each run, Pallas kernels for 8% -> 7%
where the time goes in v7:
time: 87 us; the launch traced here: 86.7 us
  Pallas kernels  26.8 us (31%)
  waiting for transfers between devices  25.4 us (29%)
  starting transfers between devices  17.4 us (20%)
  blocking collectives  16.3 us (19%)
    ppermute x9, waiting for transfers between devices, sent(): return lax.ppermute(value, axes, routes)  25.4 us
    all_to_all x1, blocking collectives, per_device(): lax.all_to_all(mixed, 'cols', 0, 0, tiled=True)  16.3 us
    pallas_call x1, Pallas kernels, per_device(): pl.pallas_call(update_kernel, grid=(tile_rows // block_rows,), in_specs=[...  13.7 us
    ppermute x9, starting transfers between devices, sent(): return lax.ppermute(value, axes, routes)  12.5 us
    pallas_call x1, Pallas kernels, per_device(): pl.pallas_call(bias_kernel, out_shape=jax.ShapeDtypeStruct(sent_shape, bf...  6.48 us
    all_to_all x1, starting transfers between devices, per_device(): lax.all_to_all(bias_local, 'cols', 0, 0, axis_index_groups=groups, tiled=...  4.9 us
    pallas_call x1, Pallas kernels, per_device(): pl.pallas_call(attend_kernel, out_shape=(jax.ShapeDtypeStruct((width + 8,...  2.86 us
    pallas_call x1, Pallas kernels, per_device(): pl.pallas_call(factor_kernel, out_shape=(jax.ShapeDtypeStruct(single.shap...  2.16 us
  transfers between devices with their start and end apart: 10, of which 4 were waited for; matrix products, arithmetic and copies ran while one was open for 0% of the time, Pallas kernels for 7%

profile of v7, /device:TPU:88, one launch (start us, length us, event | category | flops | bytes accessed | tf_op | source)
XLA Modules:
  0.0 86.7 jit_solution(9681390230757119544)
XLA Ops:
  0.6 1.5 %project.1 = (f32[128,128]{1,0:T(8,128)S(1)}, bf16[128,128]{1,0:T(8,128)(2,1)S(1)}) custom-call(bf16[128,1024]{1,0:T(8,128)(2,1)} %single_hbm.3, bf16[256,1024]{1,0:T(8,128)(2,1)} %bitcast.14), custom_call_target="tpu_custom_call" | custom-call | tf_op jit(solution)/shard_map/project/pallas_call | solution.py:354
  2.2 0.0 copy-start.2
  2.2 0.1 collective-permute-start.1
  2.3 7.8 %collective-permute-start = (bf16[128,128]{1,0:T(8,128)(2,1)S(1)}, bf16[128,128]{1,0:T(8,128)(2,1)S(1)}, u32[]{:S(2)}, u32[]{:S(2)}) collective-permute-start(bf16[128,128]{1,0:T(8,128)(2,1)S(1)} %get-tuple-element.20), channel_id=1, source_target_pairs={{0,0},{1,1},{2,2},{3,3},{4,4},{5,5},{6,6},{7,7},{8,128},{9,129},{1... | collective-permute-start | bytes 98312 | tf_op jit(solution)/shard_map/ppermute | solution.py:344
  10.1 6.5 %bias.1 = bf16[8,4,128,128]{3,2,1,0:T(8,128)(2,1)} custom-call(bf16[128,128,128]{2,1,0:T(8,128)(2,1)} %pair_ref.1, bf16[32,128]{1,0:T(8,128)(2,1)} %bitcast.20, s32[16,1,128]{2,1,0:T(1,128)} %bitcast.21), custom_call_target="tpu_custom_call" | custom-call | tf_op jit(solution)/shard_map/bias/pallas_call | solution.py:376
  16.6 0.0 copy-start.1
  16.6 0.0 collective-permute-done.1
  16.6 0.0 collective-permute-done
  16.6 4.9 %all-to-all-start = ((bf16[8,4,128,128]{3,2,1,0:T(8,128)(2,1)}), bf16[8,4,128,128]{3,2,1,0:T(8,128)(2,1)S(1)}, u32[]{:S(2)}, u32[]{:S(2)}) async-start(bf16[8,4,128,128]{3,2,1,0:T(8,128)(2,1)} %bias.1), calls=%async_computation | async-start | bytes 2097152 | tf_op jit(solution)/shard_map/all_to_all | solution.py:396
  21.5 0.0 collective-permute-start.3
  21.6 0.8 collective-permute-start.2
  22.4 2.5 %collective-permute-start.4 = (bf16[2,128,128]{2,1,0:T(8,128)(2,1)S(1)}, bf16[2,128,128]{2,1,0:T(8,128)(2,1)S(1)}, u32[]{:S(2)}, u32[]{:S(2)}) collective-permute-start(bf16[2,128,128]{2,1,0:T(8,128)(2,1)S(1)} %get-tuple-element.37), channel_id=1, source_target_pairs={{0,32},{16,48},{32,64},{48,80},{64,96},{80,112},{96,0},{112,16},{1... | collective-permute-start | bytes 196616 | tf_op jit(solution)/shard_map/ppermute | solution.py:344
  24.9 0.0 collective-permute-start.5
  24.9 9.2 %collective-permute-done.3.other_hbm = f32[128,128]{1,0:T(8,128)S(1)} collective-permute-done((f32[128,128]{1,0:T(8,128)S(1)}, f32[128,128]{1,0:T(8,128)S(1)}, u32[]{:S(2)}, u32[]{:S(2)}) %collective-permute-start.3) | collective-permute-done | bytes 65568 | tf_op jit(solution)/shard_map/ppermute | solution.py:344
  34.1 0.0 copy-start.3
  34.1 0.0 collective-permute-done.2
  34.1 0.0 collective-permute-done.4
  34.1 0.0 collective-permute-done.5
  34.2 0.1 collective-permute-start.6
  34.3 1.7 %collective-permute-done.6.far_hbm = bf16[4,2,128,128]{3,2,1,0:T(8,128)(2,1)} collective-permute-done((bf16[4,2,128,128]{3,2,1,0:T(8,128)(2,1)S(1)}, bf16[4,2,128,128]{3,2,1,0:T(8,128)(2,1)}, u32[]{:S(2)}, u32[]{:S(2)}) %collective-permute-start.6) | collective-permute-done | bytes 262176 | tf_op jit(solution)/shard_map/ppermute | solution.py:344
  36.0 0.0 all-to-all-done.bias_ref
  36.0 0.0 copy-done.2
  36.0 0.0 copy-done.3
  36.0 0.0 copy-start
  36.0 2.9 %attend.1 = (f32[72,128]{1,0:T(8,128)S(1)}, bf16[80,128]{1,0:T(8,128)(2,1)S(1)}, bf16[128,1024]{1,0:T(8,128)(2,1)S(1)}, bf16[1024,128]{1,0:T(8,128)(2,1)S(1)}) custom-call(f32[128,128]{1,0:T(8,128)} %copy-done.2, f32[128,128]{1,0:T(8,128)} %copy-done.3, bf16[8,4,128,128]{3,2,1,0:T(8,128)(2,1)S(1)} %all-to-all-done.bias_ref, ...), custom_call_target="tpu_custom_call" | custom-call | tf_op jit(solution)/shard_map/attend/pallas_call | solution.py:407
  38.8 0.8 collective-permute-start.7
  39.7 4.0 %collective-permute-done.7.received_ref = bf16[80,128]{1,0:T(8,128)(2,1)S(1)} collective-permute-done((bf16[80,128]{1,0:T(8,128)(2,1)S(1)}, bf16[80,128]{1,0:T(8,128)(2,1)S(1)}, u32[]{:S(2)}, u32[]{:S(2)}) %collective-permute-start.7) | collective-permute-done | bytes 20512 | tf_op jit(solution)/shard_map/ppermute | solution.py:344
  43.7 16.3 %all_to_all.10 = bf16[16,64,128]{2,1,0:T(8,128)(2,1)S(1)} all-to-all(bf16[16,64,128]{2,1,0:T(8,128)(2,1)S(1)} %join.1), channel_id=1, replica_groups=mesh['rows'=16,'cols'=16] {'cols'}, dimensions={0} | all-to-all | bytes 524288 | tf_op jit(solution)/shard_map/all_to_all | solution.py:441
  60.0 0.0 copy-done.1
  60.0 2.2 %factor.1 = (bf16[128,1024]{1,0:T(8,128)(2,1)}, bf16[128,128]{1,0:T(8,128)(2,1)S(1)}, bf16[128,128]{1,0:T(8,128)(2,1)S(1)}, bf16[128,512]{1,0:T(8,128)(2,1)S(1)}, bf16[512,128]{1,0:T(8,128)(2,1)S(1)}) custom-call(bf16[1024,128]{1,0:T(8,128)(2,1)S(1)} %bitcast.13, bf16[1024,1024]{1,0:T(8,128)(2,1)S(1)} %copy-done.1, ...), custom_call_target="tpu_custom_call" | custom-call | tf_op jit(solution)/shard_map/factor/pallas_call | solution.py:443
  62.2 0.3 collective-permute-start.8
  62.5 10.5 %collective-permute-done.8.right_factors_ref = bf16[128,128]{1,0:T(8,128)(2,1)S(1)} collective-permute-done((bf16[128,128]{1,0:T(8,128)(2,1)S(1)}, bf16[128,128]{1,0:T(8,128)(2,1)S(1)}, u32[]{:S(2)}, u32[]{:S(2)}) %collective-permute-start.8) | collective-permute-done | bytes 32800 | tf_op jit(solution)/shard_map/ppermute | solution.py:344
  73.0 0.0 copy-done
  73.0 13.7 %update.1 = bf16[128,128,128]{2,1,0:T(8,128)(2,1)} custom-call(bf16[128,128,128]{2,1,0:T(8,128)(2,1)S(1)} %copy-done, bf16[128,128]{1,0:T(8,128)(2,1)S(1)} %get-tuple-element.32.left_ref, bf16[128,128]{1,0:T(8,128)(2,1)S(1)} %collective-permute-done.8.right_factors_ref, bf16[128,128]{1,0:T(8,128)(2,1)S(1)} %get-tuple-element.33.w_pairout_ref, ...), custom_call_target="tpu_custom_call" | custom-call | tf_op jit(solution)/shard_map/update/pallas_call | solution.py:463
  (3 shorter events, 0.1 us)
Async XLA Ops:
  2.2 33.8 %copy-start.2 = (f32[128,128]{1,0:T(8,128)}, f32[128,128]{1,0:T(8,128)S(1)}, u32[]{:S(2)}) copy-start(f32[128,128]{1,0:T(8,128)S(1)} %get-tuple-element.19.own_hbm) | copy-start | bytes 196612
  2.2 14.4 %collective-permute-start.1 = (bf16[128,128]{1,0:T(8,128)(2,1)S(1)}, bf16[128,128]{1,0:T(8,128)(2,1)S(1)}, u32[]{:S(2)}, u32[]{:S(2)}) collective-permute-start(bf16[128,128]{1,0:T(8,128)(2,1)S(1)} %get-tuple-element.20), channel_id=1, source_target_pairs={{0,128},{1,129},{2,130},{3,131},{4,132},{5,133},{6,134},{7,135},{8... | collective-permute-start | bytes 98312 | tf_op jit(solution)/shard_map/ppermute | solution.py:344
  2.3 14.4 %collective-permute-start = (bf16[128,128]{1,0:T(8,128)(2,1)S(1)}, bf16[128,128]{1,0:T(8,128)(2,1)S(1)}, u32[]{:S(2)}, u32[]{:S(2)}) collective-permute-start(bf16[128,128]{1,0:T(8,128)(2,1)S(1)} %get-tuple-element.20), channel_id=1, source_target_pairs={{0,0},{1,1},{2,2},{3,3},{4,4},{5,5},{6,6},{7,7},{8,128},{9,129},{1... | collective-permute-start | bytes 98312 | tf_op jit(solution)/shard_map/ppermute | solution.py:344
  16.6 43.4 %copy-start.1 = (bf16[1024,1024]{1,0:T(8,128)(2,1)S(1)}, bf16[1024,1024]{1,0:T(8,128)(2,1)}, u32[]{:S(2)}) copy-start(bf16[1024,1024]{1,0:T(8,128)(2,1)} %w_out_ref.1) | copy-start | bytes 6291460
  16.6 19.3 %all-to-all-start = ((bf16[8,4,128,128]{3,2,1,0:T(8,128)(2,1)}), bf16[8,4,128,128]{3,2,1,0:T(8,128)(2,1)S(1)}, u32[]{:S(2)}, u32[]{:S(2)}) async-start(bf16[8,4,128,128]{3,2,1,0:T(8,128)(2,1)} %bias.1), calls=%async_computation | async-start | bytes 2097152 | tf_op jit(solution)/shard_map/all_to_all | solution.py:396
  21.5 12.6 %collective-permute-start.3 = (f32[128,128]{1,0:T(8,128)S(1)}, f32[128,128]{1,0:T(8,128)S(1)}, u32[]{:S(2)}, u32[]{:S(2)}) collective-permute-start(f32[128,128]{1,0:T(8,128)S(1)} %get-tuple-element.19.own_hbm), channel_id=1, source_target_pairs={{0,8},{1,9},{2,10},{3,11},{4,12},{5,13},{6,14},{7,15},{8,0},{9,1},... | collective-permute-start | bytes 196616 | tf_op jit(solution)/shard_map/ppermute | solution.py:344
  21.6 12.6 %collective-permute-start.2 = (bf16[2,128,128]{2,1,0:T(8,128)(2,1)S(1)}, bf16[2,128,128]{2,1,0:T(8,128)(2,1)S(1)}, u32[]{:S(2)}, u32[]{:S(2)}) collective-permute-start(bf16[2,128,128]{2,1,0:T(8,128)(2,1)S(1)} %get-tuple-element.37), channel_id=1, source_target_pairs={{0,96},{16,112},{32,0},{48,16},{64,32},{80,48},{96,64},{112,80},{1... | collective-permute-start | bytes 196616 | tf_op jit(solution)/shard_map/ppermute | solution.py:344
  22.4 11.8 %collective-permute-start.4 = (bf16[2,128,128]{2,1,0:T(8,128)(2,1)S(1)}, bf16[2,128,128]{2,1,0:T(8,128)(2,1)S(1)}, u32[]{:S(2)}, u32[]{:S(2)}) collective-permute-start(bf16[2,128,128]{2,1,0:T(8,128)(2,1)S(1)} %get-tuple-element.37), channel_id=1, source_target_pairs={{0,32},{16,48},{32,64},{48,80},{64,96},{80,112},{96,0},{112,16},{1... | collective-permute-start | bytes 196616 | tf_op jit(solution)/shard_map/ppermute | solution.py:344
  24.9 9.3 %collective-permute-start.5 = (bf16[2,128,128]{2,1,0:T(8,128)(2,1)S(1)}, bf16[2,128,128]{2,1,0:T(8,128)(2,1)S(1)}, u32[]{:S(2)}, u32[]{:S(2)}) collective-permute-start(bf16[2,128,128]{2,1,0:T(8,128)(2,1)S(1)} %get-tuple-element.37), channel_id=1, source_target_pairs={{0,64},{16,80},{32,96},{48,112},{64,0},{80,16},{96,32},{112,48},{1... | collective-permute-start | bytes 196616 | tf_op jit(solution)/shard_map/ppermute | solution.py:344
  34.1 1.8 %copy-start.3 = (f32[128,128]{1,0:T(8,128)}, f32[128,128]{1,0:T(8,128)S(1)}, u32[]{:S(2)}) copy-start(f32[128,128]{1,0:T(8,128)S(1)} %collective-permute-done.3.other_hbm) | copy-start | bytes 196612
  34.2 1.8 %collective-permute-start.6 = (bf16[4,2,128,128]{3,2,1,0:T(8,128)(2,1)S(1)}, bf16[4,2,128,128]{3,2,1,0:T(8,128)(2,1)}, u32[]{:S(2)}, u32[]{:S(2)}) collective-permute-start(bf16[4,2,128,128]{3,2,1,0:T(8,128)(2,1)S(1)} %pad_maximum_fusion.near_ref), channel_id=1, source_target_pairs={{0,16},{16,0},{32,48},{48,32},{64,80},{80,64},{96,112},{112,96},{1... | collective-permute-start | bytes 786440 | tf_op jit(solution)/shard_map/ppermute | solution.py:344
  36.0 37.0 %copy-start = (bf16[128,128,128]{2,1,0:T(8,128)(2,1)S(1)}, bf16[128,128,128]{2,1,0:T(8,128)(2,1)}, u32[]{:S(2)}) copy-start(bf16[128,128,128]{2,1,0:T(8,128)(2,1)} %pair_ref.1) | copy-start | bytes 12582916
  38.8 4.8 %collective-permute-start.7 = (bf16[80,128]{1,0:T(8,128)(2,1)S(1)}, bf16[80,128]{1,0:T(8,128)(2,1)S(1)}, u32[]{:S(2)}, u32[]{:S(2)}) collective-permute-start(bf16[80,128]{1,0:T(8,128)(2,1)S(1)} %get-tuple-element.28), channel_id=1, source_target_pairs={{0,8},{1,9},{2,10},{3,11},{4,12},{5,13},{6,14},{7,15},{8,0},{9,1},... | collective-permute-start | bytes 61448 | tf_op jit(solution)/shard_map/ppermute | solution.py:344
  62.2 10.8 %collective-permute-start.8 = (bf16[128,128]{1,0:T(8,128)(2,1)S(1)}, bf16[128,128]{1,0:T(8,128)(2,1)S(1)}, u32[]{:S(2)}, u32[]{:S(2)}) collective-permute-start(bf16[128,128]{1,0:T(8,128)(2,1)S(1)} %get-tuple-element.32.left_ref), channel_id=1, source_target_pairs={{0,80},{1,64},{2,96},{3,112},{4,48},{5,16},{6,0},{7,32},{8,176},{9... | collective-permute-start | bytes 98312 | tf_op jit(solution)/shard_map/ppermute | solution.py:344

commit v8 on v7

--- a/solution.py
+++ b/solution.py
@@ -39,8 +39,8 @@
     copies[1].wait()
     projected = nt_dot(weight_ref[...], normed)
     width = query_ref.shape[0] // 2
-    query_ref[:width] = projected[:width].astype(bf16).astype(f32)
-    query_ref[width:] = jax.nn.sigmoid(projected[3 * width :])
+    query_ref[:width] = projected[:width].astype(bf16)
+    query_ref[width:] = jax.nn.sigmoid(projected[3 * width :]).astype(bf16)
     kv_ref[...] = projected[width : 3 * width].astype(bf16)
 
 
@@ -107,30 +107,35 @@
 
 
 def attend_kernel(
-    own_hbm,
-    other_hbm,
+    own_ref,
+    other_ref,
     bias_ref,
     near_ref,
     far_hbm,
     single_hbm,
     w_factors_hbm,
+    w_pairout_hbm,
+    w_up_hbm,
+    w_down_hbm,
     kept_ref,
     sent_ref,
     single_ref,
     w_factors_ref,
+    w_pairout_ref,
+    w_up_ref,
+    w_down_ref,
     score_ref,
-    own_ref,
-    other_ref,
     far_ref,
     sems,
 ):
     copies = start_copies(
         (
-            (own_hbm, own_ref),
-            (other_hbm, other_ref),
             (far_hbm, far_ref),
             (single_hbm, single_ref),
             (w_factors_hbm, w_factors_ref),
+            (w_pairout_hbm, w_pairout_ref),
+            (w_up_hbm, w_up_ref),
+            (w_down_hbm, w_down_ref),
         ),
         sems,
     )
@@ -149,12 +154,11 @@
         near, far = near_ref[sent, half ^ z, part, :], far_ref[sent, half ^ z, part, :]
         return jnp.where(core == b % 2, near, far)
 
-    for copy in copies[:3]:
-        copy.wait()
+    copies[0].wait()
     lane = lax.broadcasted_iota(jnp.int32, (tile_rows, 128), 1)
     for slot, query_ref in enumerate((own_ref, other_ref)):
         z = second ^ slot
-        query = jnp.transpose(query_ref[:width]).astype(bf16)
+        query = jnp.transpose(query_ref[:width].astype(f32)).astype(bf16)
         attended, sums = [], []
         for h in range(pairs):
             query_head = query[:, h * head_width : (h + 1) * head_width]
@@ -176,7 +180,7 @@
             total = jnp.sum(total, axis=-1, keepdims=True)
             attended.append(mixed / total)
             sums.append(top + jnp.log(total))
-        gated = jnp.transpose(jnp.concatenate(attended, axis=1)) * query_ref[width:]
+        gated = jnp.transpose(jnp.concatenate(attended, axis=1)) * query_ref[width:].astype(f32)
         coded = jnp.zeros((tile_rows, 128), f32)
         for h, value in enumerate(sums):
             if slot == 0:
@@ -189,7 +193,7 @@
         out_ref = sent_ref if slot else kept_ref
         out_ref[:width] = gated.astype(out_ref.dtype)
         out_ref[width:] = jnp.transpose(coded)[: out_ref.shape[0] - width].astype(out_ref.dtype)
-    for copy in copies[3:]:
+    for copy in copies[1:]:
         copy.wait()
 
 
@@ -212,32 +216,13 @@
             out_ref[d, here] = joined.astype(bf16)
 
 
-def factor_kernel(
-    mixed_ref,
-    w_out_ref,
-    single_ref,
-    w_factors_ref,
-    w_pairout_hbm,
-    w_up_hbm,
-    w_down_hbm,
-    out_ref,
-    factors_ref,
-    w_pairout_ref,
-    w_up_ref,
-    w_down_ref,
-    sems,
-):
-    copies = start_copies(
-        ((w_pairout_hbm, w_pairout_ref), (w_up_hbm, w_up_ref), (w_down_hbm, w_down_ref)), sems
-    )
+def factor_kernel(mixed_ref, w_out_ref, single_ref, w_factors_ref, out_ref, factors_ref):
     mixed = jnp.transpose(mixed_ref[...].astype(f32)).astype(bf16)
     head_total = jnp.dot(mixed, w_out_ref[...], preferred_element_type=f32)
     single_out = (single_ref[...].astype(f32) + head_total).astype(bf16)
     out_ref[...] = single_out
     normed = normalize(single_out.astype(f32)).astype(bf16)
     factors_ref[...] = jnp.dot(normed, w_factors_ref[...], preferred_element_type=f32).astype(bf16)
-    for copy in copies:
-        copy.wait()
 
 
 def update_kernel(
@@ -354,7 +339,7 @@
     query, kv = pl.pallas_call(
         project_kernel,
         out_shape=(
-            jax.ShapeDtypeStruct((2 * width, tile_rows), f32),
+            jax.ShapeDtypeStruct((2 * width, tile_rows), bf16),
             jax.ShapeDtypeStruct((2 * width, tile_rows), bf16),
         ),
         in_specs=[in_hbm, in_hbm],
@@ -391,7 +376,9 @@
         name="bias",
     )(pinned(pair), pinned(jnp.transpose(w_bias)), pinned(residue_mask.reshape(cols, 1, tile_cols)))
     query_other = sent(query, "cols", lambda c: c ^ half_cols)
-    bias_local, kv_first, kv_last = lax.optimization_barrier((bias_local, kv_first, kv_last))
+    bias_local, kv_first, kv_last, query_other = lax.optimization_barrier(
+        (bias_local, kv_first, kv_last, query_other)
+    )
     groups = [list(range(half_cols)), list(range(half_cols, cols))]
     bias_heads = lax.all_to_all(bias_local, "cols", 0, 0, axis_index_groups=groups, tiled=True)
 
@@ -400,36 +387,39 @@
     for s in range(1, shifts):
         around = lambda r: (r & half_rows) | ((r + 2 * s) & (half_rows - 1))
         near.append(sent(both, "rows", around))
-    near[-1], query_other = lax.optimization_barrier((near[-1], query_other))
     near = jnp.stack(near)
     far = sent(near, "rows", lambda r: r ^ 1)
 
-    kept, partial, single_near, w_factors_near = pl.pallas_call(
+    kept, partial, single_near, factors_near, pairout_near, up_near, down_near = pl.pallas_call(
         attend_kernel,
         out_shape=(
             jax.ShapeDtypeStruct((width + 8, tile_rows), f32),
             jax.ShapeDtypeStruct((width + 16, tile_rows), bf16),
             jax.ShapeDtypeStruct(single.shape, bf16),
             jax.ShapeDtypeStruct(w_factors.shape, bf16),
+            jax.ShapeDtypeStruct(w_pairout.shape, bf16),
+            jax.ShapeDtypeStruct(w_up.shape, bf16),
+            jax.ShapeDtypeStruct(w_down.shape, bf16),
         ),
-        in_specs=[in_hbm, in_hbm, in_vmem, in_vmem, in_hbm, in_hbm, in_hbm],
+        in_specs=[in_vmem] * 4 + [in_hbm] * 6,
         scratch_shapes=[
             pltpu.VMEM((half_cols, tile_rows, tile_cols), f32),
-            pltpu.VMEM(query.shape, f32),
-            pltpu.VMEM(query.shape, f32),
             pltpu.VMEM(near.shape, bf16),
-            pltpu.SemaphoreType.DMA((5,)),
+            pltpu.SemaphoreType.DMA((6,)),
         ],
         compiler_params=params(),
         name="attend",
     )(
-        pinned(query),
-        pinned(query_other),
+        query,
+        query_other,
         bias_heads,
         near,
         pinned(far),
         pinned(single),
         pinned(w_factors),
+        pinned(w_pairout),
+        pinned(w_up),
+        pinned(w_down),
     )
     received = sent(partial, "cols", lambda c: c ^ half_cols)
     mixed = pl.pallas_call(
@@ -440,20 +430,15 @@
     )(kept, received)
     mixed_all = lax.all_to_all(mixed, "cols", 0, 0, tiled=True).reshape(single_width, tile_rows)
 
-    single_out, factors, pairout_near, up_near, down_near = pl.pallas_call(
+    single_out, factors = pl.pallas_call(
         factor_kernel,
         out_shape=(
             jax.ShapeDtypeStruct(single.shape, bf16),
             jax.ShapeDtypeStruct((tile_rows, w_factors.shape[1]), bf16),
-            jax.ShapeDtypeStruct(w_pairout.shape, bf16),
-            jax.ShapeDtypeStruct(w_up.shape, bf16),
-            jax.ShapeDtypeStruct(w_down.shape, bf16),
         ),
-        in_specs=[in_vmem] * 4 + [in_hbm] * 3,
-        scratch_shapes=[pltpu.SemaphoreType.DMA((3,))],
         compiler_params=params(),
         name="factor",
-    )(mixed_all, w_out, single_near, w_factors_near, pinned(w_pairout), pinned(w_up), pinned(w_down))
+    )(mixed_all, w_out, single_near, factors_near)
 
     targets = [nearest_rows(row, rows) for row in range(rows)]
     right_factors = sent(factors, both_axes, lambda r, c: (targets[r][c], r))

time: 87 us -> 84.2 us (0.968)
  blocking collectives: 16.3 us -> 13.6 us
    all_to_all x1, waiting for transfers between devices: 0.01 us -> 3.17 us  [per_device(): lax.all_to_all(bias_local, 'cols', 0, 0, axis_index_groups=groups, tiled=...]
    ppermute x9, waiting for transfers between devices: 25.4 us -> 22.4 us  [sent(): return lax.ppermute(value, axes, routes)]
    all_to_all x1, blocking collectives: 16.3 us -> 13.6 us  [per_device(): lax.all_to_all(mixed, 'cols', 0, 0, tiled=True)]
  transfers between devices with their start and end apart: 10 -> 10, of which waited for: 4 -> 6; matrix products, arithmetic and copies ran while one was open for 0% -> 0% of each run, Pallas kernels for 7% -> 8%
where the time goes in v8:
time: 84.2 us; the launch traced here: 84 us
  Pallas kernels  26 us (31%)
  waiting for transfers between devices  25.6 us (30%)
  starting transfers between devices  18 us (21%)
  blocking collectives  13.6 us (16%)
    ppermute x9, waiting for transfers between devices, sent(): return lax.ppermute(value, axes, routes)  22.4 us
    pallas_call x1, Pallas kernels, per_device(): pl.pallas_call(update_kernel, grid=(tile_rows // block_rows,), in_specs=[...  13.7 us
    all_to_all x1, blocking collectives, per_device(): lax.all_to_all(mixed, 'cols', 0, 0, tiled=True)  13.6 us
    ppermute x9, starting transfers between devices, sent(): return lax.ppermute(value, axes, routes)  13.1 us
    pallas_call x1, Pallas kernels, per_device(): pl.pallas_call(bias_kernel, out_shape=jax.ShapeDtypeStruct(sent_shape, bf...  6.48 us
    all_to_all x1, starting transfers between devices, per_device(): lax.all_to_all(bias_local, 'cols', 0, 0, axis_index_groups=groups, tiled=...  4.9 us
    all_to_all x1, waiting for transfers between devices, per_device(): lax.all_to_all(bias_local, 'cols', 0, 0, axis_index_groups=groups, tiled=...  3.17 us
    pallas_call x1, Pallas kernels, per_device(): pl.pallas_call(attend_kernel, out_shape=(jax.ShapeDtypeStruct((width + 8,...  2.81 us
  transfers between devices with their start and end apart: 10, of which 6 were waited for; matrix products, arithmetic and copies ran while one was open for 0% of the time, Pallas kernels for 8%

profile of v8, /device:TPU:88, one launch (start us, length us, event | category | flops | bytes accessed | tf_op | source)
XLA Modules:
  0.0 84.0 jit_solution(9420297642414293931)
XLA Ops:
  0.6 1.5 %project.1 = (bf16[128,128]{1,0:T(8,128)(2,1)S(1)}, bf16[128,128]{1,0:T(8,128)(2,1)S(1)}) custom-call(bf16[128,1024]{1,0:T(8,128)(2,1)} %single_hbm.3, bf16[256,1024]{1,0:T(8,128)(2,1)} %bitcast.14), custom_call_target="tpu_custom_call" | custom-call | tf_op jit(solution)/shard_map/project/pallas_call | solution.py:339
  2.2 0.1 collective-permute-start.2
  2.3 2.9 %collective-permute-start.1 = (bf16[128,128]{1,0:T(8,128)(2,1)S(1)}, bf16[128,128]{1,0:T(8,128)(2,1)S(1)}, u32[]{:S(2)}, u32[]{:S(2)}) collective-permute-start(bf16[128,128]{1,0:T(8,128)(2,1)S(1)} %get-tuple-element.19), channel_id=1, source_target_pairs={{0,128},{1,129},{2,130},{3,131},{4,132},{5,133},{6,134},{7,135},{8... | collective-permute-start | bytes 98312 | tf_op jit(solution)/shard_map/ppermute | solution.py:329
  5.2 6.4 %collective-permute-start = (bf16[128,128]{1,0:T(8,128)(2,1)S(1)}, bf16[128,128]{1,0:T(8,128)(2,1)S(1)}, u32[]{:S(2)}, u32[]{:S(2)}) collective-permute-start(bf16[128,128]{1,0:T(8,128)(2,1)S(1)} %get-tuple-element.19), channel_id=1, source_target_pairs={{0,0},{1,1},{2,2},{3,3},{4,4},{5,5},{6,6},{7,7},{8,128},{9,129},{1... | collective-permute-start | bytes 98312 | tf_op jit(solution)/shard_map/ppermute | solution.py:329
  11.6 6.5 %bias.1 = bf16[8,4,128,128]{3,2,1,0:T(8,128)(2,1)} custom-call(bf16[128,128,128]{2,1,0:T(8,128)(2,1)} %pair_ref.1, bf16[32,128]{1,0:T(8,128)(2,1)} %bitcast.20, s32[16,1,128]{2,1,0:T(1,128)} %bitcast.21), custom_call_target="tpu_custom_call" | custom-call | tf_op jit(solution)/shard_map/bias/pallas_call | solution.py:361
  18.0 0.0 copy-start.1
  18.1 0.0 collective-permute-done.2.other_ref
  18.1 0.0 collective-permute-done.1
  18.1 0.0 collective-permute-done
  18.1 4.9 %all-to-all-start = ((bf16[8,4,128,128]{3,2,1,0:T(8,128)(2,1)}), bf16[8,4,128,128]{3,2,1,0:T(8,128)(2,1)S(1)}, u32[]{:S(2)}, u32[]{:S(2)}) async-start(bf16[8,4,128,128]{3,2,1,0:T(8,128)(2,1)} %bias.1), calls=%async_computation | async-start | bytes 2097152 | tf_op jit(solution)/shard_map/all_to_all | solution.py:383
  23.0 1.3 %collective-permute-start.4 = (bf16[2,128,128]{2,1,0:T(8,128)(2,1)S(1)}, bf16[2,128,128]{2,1,0:T(8,128)(2,1)S(1)}, u32[]{:S(2)}, u32[]{:S(2)}) collective-permute-start(bf16[2,128,128]{2,1,0:T(8,128)(2,1)S(1)} %get-tuple-element.35), channel_id=1, source_target_pairs={{0,64},{16,80},{32,96},{48,112},{64,0},{80,16},{96,32},{112,48},{1... | collective-permute-start | bytes 196616 | tf_op jit(solution)/shard_map/ppermute | solution.py:329
  24.3 2.2 %collective-permute-start.3 = (bf16[2,128,128]{2,1,0:T(8,128)(2,1)S(1)}, bf16[2,128,128]{2,1,0:T(8,128)(2,1)S(1)}, u32[]{:S(2)}, u32[]{:S(2)}) collective-permute-start(bf16[2,128,128]{2,1,0:T(8,128)(2,1)S(1)} %get-tuple-element.35), channel_id=1, source_target_pairs={{0,32},{16,48},{32,64},{48,80},{64,96},{80,112},{96,0},{112,16},{1... | collective-permute-start | bytes 196616 | tf_op jit(solution)/shard_map/ppermute | solution.py:329
  26.5 0.0 collective-permute-start.5
  26.5 2.4 %collective-permute-done.4 = bf16[2,128,128]{2,1,0:T(8,128)(2,1)S(1)} collective-permute-done((bf16[2,128,128]{2,1,0:T(8,128)(2,1)S(1)}, bf16[2,128,128]{2,1,0:T(8,128)(2,1)S(1)}, u32[]{:S(2)}, u32[]{:S(2)}) %collective-permute-start.4) | collective-permute-done | bytes 65568 | tf_op jit(solution)/shard_map/ppermute | solution.py:329
  28.9 0.0 collective-permute-done.3
  28.9 3.1 %collective-permute-done.5 = bf16[2,128,128]{2,1,0:T(8,128)(2,1)S(1)} collective-permute-done((bf16[2,128,128]{2,1,0:T(8,128)(2,1)S(1)}, bf16[2,128,128]{2,1,0:T(8,128)(2,1)S(1)}, u32[]{:S(2)}, u32[]{:S(2)}) %collective-permute-start.5) | collective-permute-done | bytes 65568 | tf_op jit(solution)/shard_map/ppermute | solution.py:329
  32.0 0.1 collective-permute-start.6
  32.1 1.7 %collective-permute-done.6.far_hbm = bf16[4,2,128,128]{3,2,1,0:T(8,128)(2,1)} collective-permute-done((bf16[4,2,128,128]{3,2,1,0:T(8,128)(2,1)S(1)}, bf16[4,2,128,128]{3,2,1,0:T(8,128)(2,1)}, u32[]{:S(2)}, u32[]{:S(2)}) %collective-permute-start.6) | collective-permute-done | bytes 262176 | tf_op jit(solution)/shard_map/ppermute | solution.py:329
  33.8 3.2 %all-to-all-done.bias_ref = bf16[8,4,128,128]{3,2,1,0:T(8,128)(2,1)S(1)} async-done(((bf16[8,4,128,128]{3,2,1,0:T(8,128)(2,1)}), bf16[8,4,128,128]{3,2,1,0:T(8,128)(2,1)S(1)}, u32[]{:S(2)}, u32[]{:S(2)}) %all-to-all-start) | async-done | bytes 1048608 | tf_op jit(solution)/shard_map/all_to_all | solution.py:383
  36.9 0.0 copy-start
  36.9 2.8 %attend.1 = (f32[72,128]{1,0:T(8,128)S(1)}, bf16[80,128]{1,0:T(8,128)(2,1)S(1)}, bf16[128,1024]{1,0:T(8,128)(2,1)S(1)}, bf16[1024,128]{1,0:T(8,128)(2,1)S(1)}, b...) custom-call(bf16[128,128]{1,0:T(8,128)(2,1)S(1)} %get-tuple-element.18.own_ref, ...), custom_call_target="tpu_custom_call" | custom-call | tf_op jit(solution)/shard_map/attend/pallas_call | solution.py:393
  39.8 0.1 collective-permute-start.7
  39.9 4.8 %collective-permute-done.7.received_ref = bf16[80,128]{1,0:T(8,128)(2,1)S(1)} collective-permute-done((bf16[80,128]{1,0:T(8,128)(2,1)S(1)}, bf16[80,128]{1,0:T(8,128)(2,1)S(1)}, u32[]{:S(2)}, u32[]{:S(2)}) %collective-permute-start.7) | collective-permute-done | bytes 20512 | tf_op jit(solution)/shard_map/ppermute | solution.py:329
  44.7 13.6 %all_to_all.10 = bf16[16,64,128]{2,1,0:T(8,128)(2,1)S(1)} all-to-all(bf16[16,64,128]{2,1,0:T(8,128)(2,1)S(1)} %join.1), channel_id=1, replica_groups=mesh['rows'=16,'cols'=16] {'cols'}, dimensions={0} | all-to-all | bytes 524288 | tf_op jit(solution)/shard_map/all_to_all | solution.py:431
  58.3 0.0 copy-done.1
  58.3 1.4 %factor.1 = (bf16[128,1024]{1,0:T(8,128)(2,1)}, bf16[128,128]{1,0:T(8,128)(2,1)S(1)}) custom-call(bf16[1024,128]{1,0:T(8,128)(2,1)S(1)} %bitcast.13, bf16[1024,1024]{1,0:T(8,128)(2,1)S(1)} %copy-done.1, bf16[128,1024]{1,0:T(8,128)(2,1)S(1)} %get-tuple-element.27.single_ref, bf16[1024,128]{1,0:T(8,128)(2,1)S(1)} %get-tuple-element.28.w_factors_ref), custom_call_target="tpu_custom_call" | custom-call | tf_op jit(solution)/shard_map/factor/pallas_call | solution.py:433
  59.7 0.0 collective-permute-start.8
  59.7 10.5 %collective-permute-done.8.right_factors_ref = bf16[128,128]{1,0:T(8,128)(2,1)S(1)} collective-permute-done((bf16[128,128]{1,0:T(8,128)(2,1)S(1)}, bf16[128,128]{1,0:T(8,128)(2,1)S(1)}, u32[]{:S(2)}, u32[]{:S(2)}) %collective-permute-start.8) | collective-permute-done | bytes 32800 | tf_op jit(solution)/shard_map/ppermute | solution.py:329
  70.3 0.0 copy-done
  70.3 13.7 %update.1 = bf16[128,128,128]{2,1,0:T(8,128)(2,1)} custom-call(bf16[128,128,128]{2,1,0:T(8,128)(2,1)S(1)} %copy-done, bf16[128,128]{1,0:T(8,128)(2,1)S(1)} %get-tuple-element.30.left_ref, bf16[128,128]{1,0:T(8,128)(2,1)S(1)} %collective-permute-done.8.right_factors_ref, bf16[128,128]{1,0:T(8,128)(2,1)S(1)} %get-tuple-element.31.w_pairout_ref, ...), custom_call_target="tpu_custom_call" | custom-call | tf_op jit(solution)/shard_map/update/pallas_call | solution.py:448
  (3 shorter events, 0.1 us)
Async XLA Ops:
  2.2 15.9 %collective-permute-start.2 = (bf16[128,128]{1,0:T(8,128)(2,1)S(1)}, bf16[128,128]{1,0:T(8,128)(2,1)S(1)}, u32[]{:S(2)}, u32[]{:S(2)}) collective-permute-start(bf16[128,128]{1,0:T(8,128)(2,1)S(1)} %get-tuple-element.18.own_ref), channel_id=1, source_target_pairs={{0,8},{1,9},{2,10},{3,11},{4,12},{5,13},{6,14},{7,15},{8,0},{9,1},... | collective-permute-start | bytes 98312 | tf_op jit(solution)/shard_map/ppermute | solution.py:329
  2.3 15.8 %collective-permute-start.1 = (bf16[128,128]{1,0:T(8,128)(2,1)S(1)}, bf16[128,128]{1,0:T(8,128)(2,1)S(1)}, u32[]{:S(2)}, u32[]{:S(2)}) collective-permute-start(bf16[128,128]{1,0:T(8,128)(2,1)S(1)} %get-tuple-element.19), channel_id=1, source_target_pairs={{0,128},{1,129},{2,130},{3,131},{4,132},{5,133},{6,134},{7,135},{8... | collective-permute-start | bytes 98312 | tf_op jit(solution)/shard_map/ppermute | solution.py:329
  5.2 12.9 %collective-permute-start = (bf16[128,128]{1,0:T(8,128)(2,1)S(1)}, bf16[128,128]{1,0:T(8,128)(2,1)S(1)}, u32[]{:S(2)}, u32[]{:S(2)}) collective-permute-start(bf16[128,128]{1,0:T(8,128)(2,1)S(1)} %get-tuple-element.19), channel_id=1, source_target_pairs={{0,0},{1,1},{2,2},{3,3},{4,4},{5,5},{6,6},{7,7},{8,128},{9,129},{1... | collective-permute-start | bytes 98312 | tf_op jit(solution)/shard_map/ppermute | solution.py:329
  18.0 40.3 %copy-start.1 = (bf16[1024,1024]{1,0:T(8,128)(2,1)S(1)}, bf16[1024,1024]{1,0:T(8,128)(2,1)}, u32[]{:S(2)}) copy-start(bf16[1024,1024]{1,0:T(8,128)(2,1)} %w_out_ref.1) | copy-start | bytes 6291460
  18.1 18.9 %all-to-all-start = ((bf16[8,4,128,128]{3,2,1,0:T(8,128)(2,1)}), bf16[8,4,128,128]{3,2,1,0:T(8,128)(2,1)S(1)}, u32[]{:S(2)}, u32[]{:S(2)}) async-start(bf16[8,4,128,128]{3,2,1,0:T(8,128)(2,1)} %bias.1), calls=%async_computation | async-start | bytes 2097152 | tf_op jit(solution)/shard_map/all_to_all | solution.py:383
  23.0 5.9 %collective-permute-start.4 = (bf16[2,128,128]{2,1,0:T(8,128)(2,1)S(1)}, bf16[2,128,128]{2,1,0:T(8,128)(2,1)S(1)}, u32[]{:S(2)}, u32[]{:S(2)}) collective-permute-start(bf16[2,128,128]{2,1,0:T(8,128)(2,1)S(1)} %get-tuple-element.35), channel_id=1, source_target_pairs={{0,64},{16,80},{32,96},{48,112},{64,0},{80,16},{96,32},{112,48},{1... | collective-permute-start | bytes 196616 | tf_op jit(solution)/shard_map/ppermute | solution.py:329
  24.3 4.6 %collective-permute-start.3 = (bf16[2,128,128]{2,1,0:T(8,128)(2,1)S(1)}, bf16[2,128,128]{2,1,0:T(8,128)(2,1)S(1)}, u32[]{:S(2)}, u32[]{:S(2)}) collective-permute-start(bf16[2,128,128]{2,1,0:T(8,128)(2,1)S(1)} %get-tuple-element.35), channel_id=1, source_target_pairs={{0,32},{16,48},{32,64},{48,80},{64,96},{80,112},{96,0},{112,16},{1... | collective-permute-start | bytes 196616 | tf_op jit(solution)/shard_map/ppermute | solution.py:329
  26.5 5.5 %collective-permute-start.5 = (bf16[2,128,128]{2,1,0:T(8,128)(2,1)S(1)}, bf16[2,128,128]{2,1,0:T(8,128)(2,1)S(1)}, u32[]{:S(2)}, u32[]{:S(2)}) collective-permute-start(bf16[2,128,128]{2,1,0:T(8,128)(2,1)S(1)} %get-tuple-element.35), channel_id=1, source_target_pairs={{0,96},{16,112},{32,0},{48,16},{64,32},{80,48},{96,64},{112,80},{1... | collective-permute-start | bytes 196616 | tf_op jit(solution)/shard_map/ppermute | solution.py:329
  32.0 1.8 %collective-permute-start.6 = (bf16[4,2,128,128]{3,2,1,0:T(8,128)(2,1)S(1)}, bf16[4,2,128,128]{3,2,1,0:T(8,128)(2,1)}, u32[]{:S(2)}, u32[]{:S(2)}) collective-permute-start(bf16[4,2,128,128]{3,2,1,0:T(8,128)(2,1)S(1)} %pad_maximum_fusion.near_ref), channel_id=1, source_target_pairs={{0,16},{16,0},{32,48},{48,32},{64,80},{80,64},{96,112},{112,96},{1... | collective-permute-start | bytes 786440 | tf_op jit(solution)/shard_map/ppermute | solution.py:329
  36.9 33.3 %copy-start = (bf16[128,128,128]{2,1,0:T(8,128)(2,1)S(1)}, bf16[128,128,128]{2,1,0:T(8,128)(2,1)}, u32[]{:S(2)}) copy-start(bf16[128,128,128]{2,1,0:T(8,128)(2,1)} %pair_ref.1) | copy-start | bytes 12582916
  39.8 4.9 %collective-permute-start.7 = (bf16[80,128]{1,0:T(8,128)(2,1)S(1)}, bf16[80,128]{1,0:T(8,128)(2,1)S(1)}, u32[]{:S(2)}, u32[]{:S(2)}) collective-permute-start(bf16[80,128]{1,0:T(8,128)(2,1)S(1)} %get-tuple-element.26), channel_id=1, source_target_pairs={{0,8},{1,9},{2,10},{3,11},{4,12},{5,13},{6,14},{7,15},{8,0},{9,1},... | collective-permute-start | bytes 61448 | tf_op jit(solution)/shard_map/ppermute | solution.py:329
  59.7 10.5 %collective-permute-start.8 = (bf16[128,128]{1,0:T(8,128)(2,1)S(1)}, bf16[128,128]{1,0:T(8,128)(2,1)S(1)}, u32[]{:S(2)}, u32[]{:S(2)}) collective-permute-start(bf16[128,128]{1,0:T(8,128)(2,1)S(1)} %get-tuple-element.30.left_ref), channel_id=1, source_target_pairs={{0,80},{1,64},{2,96},{3,112},{4,48},{5,16},{6,0},{7,32},{8,176},{9... | collective-permute-start | bytes 98312 | tf_op jit(solution)/shard_map/ppermute | solution.py:329

commit v9 on v8

--- a/solution.py
+++ b/solution.py
@@ -52,6 +52,18 @@
     )
     square = jnp.mean(centred * centred, -1, keepdims=True)
     return (centred * lax.rsqrt(square + epsilon)).astype(bf16)
+
+
+def normalize_mixed(rounded, groups=8, across=4):
+    size = rounded.shape[0] // groups
+    parts = []
+    for g in range(groups):
+        rows_here = rounded[g * size : (g + 1) * size]
+        if g % across == across - 1:
+            parts.append(normalize(rows_here.astype(f32)).astype(bf16))
+        else:
+            parts.append(normalize_rows(rows_here))
+    return jnp.concatenate(parts, axis=0)
 
 
 def bias_kernel(
@@ -154,11 +166,13 @@
         near, far = near_ref[sent, half ^ z, part, :], far_ref[sent, half ^ z, part, :]
         return jnp.where(core == b % 2, near, far)
 
+    queries = jnp.concatenate([own_ref[:width], other_ref[:width]], axis=0)
+    queries = jnp.transpose(queries.astype(f32)).astype(bf16)
     copies[0].wait()
-    lane = lax.broadcasted_iota(jnp.int32, (tile_rows, 128), 1)
+    lane = lax.broadcasted_iota(jnp.int32, (tile_rows, 128 - width), 1)
     for slot, query_ref in enumerate((own_ref, other_ref)):
         z = second ^ slot
-        query = jnp.transpose(query_ref[:width].astype(f32)).astype(bf16)
+        query = queries[:, slot * width : (slot + 1) * width]
         attended, sums = [], []
         for h in range(pairs):
             query_head = query[:, h * head_width : (h + 1) * head_width]
@@ -180,8 +194,7 @@
             total = jnp.sum(total, axis=-1, keepdims=True)
             attended.append(mixed / total)
             sums.append(top + jnp.log(total))
-        gated = jnp.transpose(jnp.concatenate(attended, axis=1)) * query_ref[width:].astype(f32)
-        coded = jnp.zeros((tile_rows, 128), f32)
+        coded = jnp.zeros((tile_rows, 128 - width), f32)
         for h, value in enumerate(sums):
             if slot == 0:
                 coded = jnp.where(lane == h, value, coded)
@@ -190,9 +203,10 @@
                 part = value.astype(bf16).astype(f32)
                 value = value - part
                 coded = jnp.where(lane == p * pairs + h, part, coded)
+        turned = jnp.transpose(jnp.concatenate(attended + [coded], axis=1))
         out_ref = sent_ref if slot else kept_ref
-        out_ref[:width] = gated.astype(out_ref.dtype)
-        out_ref[width:] = jnp.transpose(coded)[: out_ref.shape[0] - width].astype(out_ref.dtype)
+        out_ref[:width] = (turned[:width] * query_ref[width:].astype(f32)).astype(out_ref.dtype)
+        out_ref[width:] = turned[width : out_ref.shape[0]].astype(out_ref.dtype)
     for copy in copies[1:]:
         copy.wait()
 
@@ -237,7 +251,7 @@
     shift_ref,
     right_ref,
 ):
-    block_rows, tile_cols, width = pair_ref.shape
+    block_rows, tile_cols, width = out_ref.shape
     factor_width = width // 2
     at = pl.program_id(0)
 
@@ -255,12 +269,12 @@
     here = pl.ds(at * block_rows, block_rows)
     paired = (right_ref[...][None] * scale_ref[here] + shift_ref[here]).reshape(rows_here, width)
     moved = jnp.dot(paired, w_pairout_ref[...], preferred_element_type=f32)
-    pair_mid = (pair_ref[...].reshape(rows_here, width).astype(f32) + moved).astype(bf16)
-    normed = normalize_rows(pair_mid)
+    pair_mid = (pair_ref[here].reshape(rows_here, width).astype(f32) + moved).astype(bf16)
+    normed = normalize_mixed(pair_mid)
     hidden = jnp.dot(normed, w_up_ref[...], preferred_element_type=f32).astype(bf16)
     hidden = jnp.maximum(hidden, 0)
     down = jnp.dot(hidden, w_down_ref[...], preferred_element_type=f32)
-    out_ref[...] = (pair_mid.astype(f32) + down).astype(bf16).reshape(pair_ref.shape)
+    out_ref[...] = (pair_mid.astype(f32) + down).astype(bf16).reshape(out_ref.shape)
 
 
 def nearest_rows(row, count):
@@ -448,7 +462,7 @@
     updated = pl.pallas_call(
         update_kernel,
         grid=(tile_rows // block_rows,),
-        in_specs=[pair_block] + [whole(factors.shape)] * 2 + [in_vmem] * 3,
+        in_specs=[in_vmem] * 6,
         out_specs=pair_block,
         out_shape=jax.ShapeDtypeStruct(pair.shape, bf16),
         scratch_shapes=[

time: 84.2 us -> 83.6 us (level)
  no operation moved by 1% of the time
where the time goes in v9:
time: 83.6 us; the launch traced here: 83.4 us
  waiting for transfers between devices  25.5 us (31%)
  Pallas kernels  25.4 us (30%)
  starting transfers between devices  18 us (22%)
  blocking collectives  13.7 us (16%)
    ppermute x9, waiting for transfers between devices, sent(): return lax.ppermute(value, axes, routes)  22.4 us
    all_to_all x1, blocking collectives, per_device(): lax.all_to_all(mixed, 'cols', 0, 0, tiled=True)  13.7 us
    pallas_call x1, Pallas kernels, per_device(): pl.pallas_call(update_kernel, grid=(tile_rows // block_rows,), in_specs=[...  13.3 us
    ppermute x9, starting transfers between devices, sent(): return lax.ppermute(value, axes, routes)  13.1 us
    pallas_call x1, Pallas kernels, per_device(): pl.pallas_call(bias_kernel, out_shape=jax.ShapeDtypeStruct(sent_shape, bf...  6.48 us
    all_to_all x1, starting transfers between devices, per_device(): lax.all_to_all(bias_local, 'cols', 0, 0, axis_index_groups=groups, tiled=...  4.9 us
    all_to_all x1, waiting for transfers between devices, per_device(): lax.all_to_all(bias_local, 'cols', 0, 0, axis_index_groups=groups, tiled=...  3.17 us
    pallas_call x1, Pallas kernels, per_device(): pl.pallas_call(attend_kernel, out_shape=(jax.ShapeDtypeStruct((width + 8,...  2.7 us
  transfers between devices with their start and end apart: 10, of which 6 were waited for; matrix products, arithmetic and copies ran while one was open for 0% of the time, Pallas kernels for 8%

profile of v9, /device:TPU:88, one launch (start us, length us, event | category | flops | bytes accessed | tf_op | source)
XLA Modules:
  0.0 83.4 jit_solution(7273165883890389407)
XLA Ops:
  0.6 1.5 %project.1 = (bf16[128,128]{1,0:T(8,128)(2,1)S(1)}, bf16[128,128]{1,0:T(8,128)(2,1)S(1)}) custom-call(bf16[128,1024]{1,0:T(8,128)(2,1)} %single_hbm.3, bf16[256,1024]{1,0:T(8,128)(2,1)} %bitcast.14), custom_call_target="tpu_custom_call" | custom-call | tf_op jit(solution)/shard_map/project/pallas_call | solution.py:353
  2.2 0.1 collective-permute-start.2
  2.3 2.9 %collective-permute-start.1 = (bf16[128,128]{1,0:T(8,128)(2,1)S(1)}, bf16[128,128]{1,0:T(8,128)(2,1)S(1)}, u32[]{:S(2)}, u32[]{:S(2)}) collective-permute-start(bf16[128,128]{1,0:T(8,128)(2,1)S(1)} %get-tuple-element.19), channel_id=1, source_target_pairs={{0,128},{1,129},{2,130},{3,131},{4,132},{5,133},{6,134},{7,135},{8... | collective-permute-start | bytes 98312 | tf_op jit(solution)/shard_map/ppermute | solution.py:343
  5.2 6.4 %collective-permute-start = (bf16[128,128]{1,0:T(8,128)(2,1)S(1)}, bf16[128,128]{1,0:T(8,128)(2,1)S(1)}, u32[]{:S(2)}, u32[]{:S(2)}) collective-permute-start(bf16[128,128]{1,0:T(8,128)(2,1)S(1)} %get-tuple-element.19), channel_id=1, source_target_pairs={{0,0},{1,1},{2,2},{3,3},{4,4},{5,5},{6,6},{7,7},{8,128},{9,129},{1... | collective-permute-start | bytes 98312 | tf_op jit(solution)/shard_map/ppermute | solution.py:343
  11.6 6.5 %bias.1 = bf16[8,4,128,128]{3,2,1,0:T(8,128)(2,1)} custom-call(bf16[128,128,128]{2,1,0:T(8,128)(2,1)} %pair_ref.1, bf16[32,128]{1,0:T(8,128)(2,1)} %bitcast.20, s32[16,1,128]{2,1,0:T(1,128)} %bitcast.21), custom_call_target="tpu_custom_call" | custom-call | tf_op jit(solution)/shard_map/bias/pallas_call | solution.py:375
  18.0 0.0 copy-start.1
  18.1 0.0 collective-permute-done.2.other_ref
  18.1 0.0 collective-permute-done.1
  18.1 0.0 collective-permute-done
  18.1 4.9 %all-to-all-start = ((bf16[8,4,128,128]{3,2,1,0:T(8,128)(2,1)}), bf16[8,4,128,128]{3,2,1,0:T(8,128)(2,1)S(1)}, u32[]{:S(2)}, u32[]{:S(2)}) async-start(bf16[8,4,128,128]{3,2,1,0:T(8,128)(2,1)} %bias.1), calls=%async_computation | async-start | bytes 2097152 | tf_op jit(solution)/shard_map/all_to_all | solution.py:397
  23.0 1.3 %collective-permute-start.4 = (bf16[2,128,128]{2,1,0:T(8,128)(2,1)S(1)}, bf16[2,128,128]{2,1,0:T(8,128)(2,1)S(1)}, u32[]{:S(2)}, u32[]{:S(2)}) collective-permute-start(bf16[2,128,128]{2,1,0:T(8,128)(2,1)S(1)} %get-tuple-element.35), channel_id=1, source_target_pairs={{0,64},{16,80},{32,96},{48,112},{64,0},{80,16},{96,32},{112,48},{1... | collective-permute-start | bytes 196616 | tf_op jit(solution)/shard_map/ppermute | solution.py:343
  24.3 2.2 %collective-permute-start.3 = (bf16[2,128,128]{2,1,0:T(8,128)(2,1)S(1)}, bf16[2,128,128]{2,1,0:T(8,128)(2,1)S(1)}, u32[]{:S(2)}, u32[]{:S(2)}) collective-permute-start(bf16[2,128,128]{2,1,0:T(8,128)(2,1)S(1)} %get-tuple-element.35), channel_id=1, source_target_pairs={{0,32},{16,48},{32,64},{48,80},{64,96},{80,112},{96,0},{112,16},{1... | collective-permute-start | bytes 196616 | tf_op jit(solution)/shard_map/ppermute | solution.py:343
  26.5 0.0 collective-permute-start.5
  26.5 2.4 %collective-permute-done.4 = bf16[2,128,128]{2,1,0:T(8,128)(2,1)S(1)} collective-permute-done((bf16[2,128,128]{2,1,0:T(8,128)(2,1)S(1)}, bf16[2,128,128]{2,1,0:T(8,128)(2,1)S(1)}, u32[]{:S(2)}, u32[]{:S(2)}) %collective-permute-start.4) | collective-permute-done | bytes 65568 | tf_op jit(solution)/shard_map/ppermute | solution.py:343
  28.9 0.0 collective-permute-done.3
  28.9 3.1 %collective-permute-done.5 = bf16[2,128,128]{2,1,0:T(8,128)(2,1)S(1)} collective-permute-done((bf16[2,128,128]{2,1,0:T(8,128)(2,1)S(1)}, bf16[2,128,128]{2,1,0:T(8,128)(2,1)S(1)}, u32[]{:S(2)}, u32[]{:S(2)}) %collective-permute-start.5) | collective-permute-done | bytes 65568 | tf_op jit(solution)/shard_map/ppermute | solution.py:343
  32.0 0.1 collective-permute-start.6
  32.1 1.7 %collective-permute-done.6.far_hbm = bf16[4,2,128,128]{3,2,1,0:T(8,128)(2,1)} collective-permute-done((bf16[4,2,128,128]{3,2,1,0:T(8,128)(2,1)S(1)}, bf16[4,2,128,128]{3,2,1,0:T(8,128)(2,1)}, u32[]{:S(2)}, u32[]{:S(2)}) %collective-permute-start.6) | collective-permute-done | bytes 262176 | tf_op jit(solution)/shard_map/ppermute | solution.py:343
  33.8 3.2 %all-to-all-done.bias_ref = bf16[8,4,128,128]{3,2,1,0:T(8,128)(2,1)S(1)} async-done(((bf16[8,4,128,128]{3,2,1,0:T(8,128)(2,1)}), bf16[8,4,128,128]{3,2,1,0:T(8,128)(2,1)S(1)}, u32[]{:S(2)}, u32[]{:S(2)}) %all-to-all-start) | async-done | bytes 1048608 | tf_op jit(solution)/shard_map/all_to_all | solution.py:397
  36.9 0.0 copy-start
  36.9 2.7 %attend.1 = (f32[72,128]{1,0:T(8,128)S(1)}, bf16[80,128]{1,0:T(8,128)(2,1)S(1)}, bf16[128,1024]{1,0:T(8,128)(2,1)S(1)}, bf16[1024,128]{1,0:T(8,128)(2,1)S(1)}, b...) custom-call(bf16[128,128]{1,0:T(8,128)(2,1)S(1)} %get-tuple-element.18.own_ref, ...), custom_call_target="tpu_custom_call" | custom-call | tf_op jit(solution)/shard_map/attend/pallas_call | solution.py:407
  39.7 0.1 collective-permute-start.7
  39.8 4.7 %collective-permute-done.7.received_ref = bf16[80,128]{1,0:T(8,128)(2,1)S(1)} collective-permute-done((bf16[80,128]{1,0:T(8,128)(2,1)S(1)}, bf16[80,128]{1,0:T(8,128)(2,1)S(1)}, u32[]{:S(2)}, u32[]{:S(2)}) %collective-permute-start.7) | collective-permute-done | bytes 20512 | tf_op jit(solution)/shard_map/ppermute | solution.py:343
  44.5 13.7 %all_to_all.10 = bf16[16,64,128]{2,1,0:T(8,128)(2,1)S(1)} all-to-all(bf16[16,64,128]{2,1,0:T(8,128)(2,1)S(1)} %join.1), channel_id=1, replica_groups=mesh['rows'=16,'cols'=16] {'cols'}, dimensions={0} | all-to-all | bytes 524288 | tf_op jit(solution)/shard_map/all_to_all | solution.py:445
  58.2 0.0 copy-done.1
  58.2 1.4 %factor.1 = (bf16[128,1024]{1,0:T(8,128)(2,1)}, bf16[128,128]{1,0:T(8,128)(2,1)S(1)}) custom-call(bf16[1024,128]{1,0:T(8,128)(2,1)S(1)} %bitcast.13, bf16[1024,1024]{1,0:T(8,128)(2,1)S(1)} %copy-done.1, bf16[128,1024]{1,0:T(8,128)(2,1)S(1)} %get-tuple-element.27.single_ref, bf16[1024,128]{1,0:T(8,128)(2,1)S(1)} %get-tuple-element.28.w_factors_ref), custom_call_target="tpu_custom_call" | custom-call | tf_op jit(solution)/shard_map/factor/pallas_call | solution.py:447
  59.6 0.0 collective-permute-start.8
  59.6 10.5 %collective-permute-done.8.right_factors_ref = bf16[128,128]{1,0:T(8,128)(2,1)S(1)} collective-permute-done((bf16[128,128]{1,0:T(8,128)(2,1)S(1)}, bf16[128,128]{1,0:T(8,128)(2,1)S(1)}, u32[]{:S(2)}, u32[]{:S(2)}) %collective-permute-start.8) | collective-permute-done | bytes 32800 | tf_op jit(solution)/shard_map/ppermute | solution.py:343
  70.1 0.0 copy-done
  70.1 13.3 %update.1 = bf16[128,128,128]{2,1,0:T(8,128)(2,1)} custom-call(bf16[128,128,128]{2,1,0:T(8,128)(2,1)S(1)} %copy-done, bf16[128,128]{1,0:T(8,128)(2,1)S(1)} %get-tuple-element.30.left_ref, bf16[128,128]{1,0:T(8,128)(2,1)S(1)} %collective-permute-done.8.right_factors_ref, bf16[128,128]{1,0:T(8,128)(2,1)S(1)} %get-tuple-element.31.w_pairout_ref, ...), custom_call_target="tpu_custom_call" | custom-call | tf_op jit(solution)/shard_map/update/pallas_call | solution.py:462
  (3 shorter events, 0.1 us)
Async XLA Ops:
  2.2 15.9 %collective-permute-start.2 = (bf16[128,128]{1,0:T(8,128)(2,1)S(1)}, bf16[128,128]{1,0:T(8,128)(2,1)S(1)}, u32[]{:S(2)}, u32[]{:S(2)}) collective-permute-start(bf16[128,128]{1,0:T(8,128)(2,1)S(1)} %get-tuple-element.18.own_ref), channel_id=1, source_target_pairs={{0,8},{1,9},{2,10},{3,11},{4,12},{5,13},{6,14},{7,15},{8,0},{9,1},... | collective-permute-start | bytes 98312 | tf_op jit(solution)/shard_map/ppermute | solution.py:343
  2.3 15.8 %collective-permute-start.1 = (bf16[128,128]{1,0:T(8,128)(2,1)S(1)}, bf16[128,128]{1,0:T(8,128)(2,1)S(1)}, u32[]{:S(2)}, u32[]{:S(2)}) collective-permute-start(bf16[128,128]{1,0:T(8,128)(2,1)S(1)} %get-tuple-element.19), channel_id=1, source_target_pairs={{0,128},{1,129},{2,130},{3,131},{4,132},{5,133},{6,134},{7,135},{8... | collective-permute-start | bytes 98312 | tf_op jit(solution)/shard_map/ppermute | solution.py:343
  5.2 12.9 %collective-permute-start = (bf16[128,128]{1,0:T(8,128)(2,1)S(1)}, bf16[128,128]{1,0:T(8,128)(2,1)S(1)}, u32[]{:S(2)}, u32[]{:S(2)}) collective-permute-start(bf16[128,128]{1,0:T(8,128)(2,1)S(1)} %get-tuple-element.19), channel_id=1, source_target_pairs={{0,0},{1,1},{2,2},{3,3},{4,4},{5,5},{6,6},{7,7},{8,128},{9,129},{1... | collective-permute-start | bytes 98312 | tf_op jit(solution)/shard_map/ppermute | solution.py:343
  18.0 40.2 %copy-start.1 = (bf16[1024,1024]{1,0:T(8,128)(2,1)S(1)}, bf16[1024,1024]{1,0:T(8,128)(2,1)}, u32[]{:S(2)}) copy-start(bf16[1024,1024]{1,0:T(8,128)(2,1)} %w_out_ref.1) | copy-start | bytes 6291460
  18.1 18.9 %all-to-all-start = ((bf16[8,4,128,128]{3,2,1,0:T(8,128)(2,1)}), bf16[8,4,128,128]{3,2,1,0:T(8,128)(2,1)S(1)}, u32[]{:S(2)}, u32[]{:S(2)}) async-start(bf16[8,4,128,128]{3,2,1,0:T(8,128)(2,1)} %bias.1), calls=%async_computation | async-start | bytes 2097152 | tf_op jit(solution)/shard_map/all_to_all | solution.py:397
  23.0 5.9 %collective-permute-start.4 = (bf16[2,128,128]{2,1,0:T(8,128)(2,1)S(1)}, bf16[2,128,128]{2,1,0:T(8,128)(2,1)S(1)}, u32[]{:S(2)}, u32[]{:S(2)}) collective-permute-start(bf16[2,128,128]{2,1,0:T(8,128)(2,1)S(1)} %get-tuple-element.35), channel_id=1, source_target_pairs={{0,64},{16,80},{32,96},{48,112},{64,0},{80,16},{96,32},{112,48},{1... | collective-permute-start | bytes 196616 | tf_op jit(solution)/shard_map/ppermute | solution.py:343
  24.3 4.6 %collective-permute-start.3 = (bf16[2,128,128]{2,1,0:T(8,128)(2,1)S(1)}, bf16[2,128,128]{2,1,0:T(8,128)(2,1)S(1)}, u32[]{:S(2)}, u32[]{:S(2)}) collective-permute-start(bf16[2,128,128]{2,1,0:T(8,128)(2,1)S(1)} %get-tuple-element.35), channel_id=1, source_target_pairs={{0,32},{16,48},{32,64},{48,80},{64,96},{80,112},{96,0},{112,16},{1... | collective-permute-start | bytes 196616 | tf_op jit(solution)/shard_map/ppermute | solution.py:343
  26.5 5.5 %collective-permute-start.5 = (bf16[2,128,128]{2,1,0:T(8,128)(2,1)S(1)}, bf16[2,128,128]{2,1,0:T(8,128)(2,1)S(1)}, u32[]{:S(2)}, u32[]{:S(2)}) collective-permute-start(bf16[2,128,128]{2,1,0:T(8,128)(2,1)S(1)} %get-tuple-element.35), channel_id=1, source_target_pairs={{0,96},{16,112},{32,0},{48,16},{64,32},{80,48},{96,64},{112,80},{1... | collective-permute-start | bytes 196616 | tf_op jit(solution)/shard_map/ppermute | solution.py:343
  32.0 1.8 %collective-permute-start.6 = (bf16[4,2,128,128]{3,2,1,0:T(8,128)(2,1)S(1)}, bf16[4,2,128,128]{3,2,1,0:T(8,128)(2,1)}, u32[]{:S(2)}, u32[]{:S(2)}) collective-permute-start(bf16[4,2,128,128]{3,2,1,0:T(8,128)(2,1)S(1)} %pad_maximum_fusion.near_ref), channel_id=1, source_target_pairs={{0,16},{16,0},{32,48},{48,32},{64,80},{80,64},{96,112},{112,96},{1... | collective-permute-start | bytes 786440 | tf_op jit(solution)/shard_map/ppermute | solution.py:343
  36.9 33.2 %copy-start = (bf16[128,128,128]{2,1,0:T(8,128)(2,1)S(1)}, bf16[128,128,128]{2,1,0:T(8,128)(2,1)}, u32[]{:S(2)}) copy-start(bf16[128,128,128]{2,1,0:T(8,128)(2,1)} %pair_ref.1) | copy-start | bytes 12582916
  39.7 4.8 %collective-permute-start.7 = (bf16[80,128]{1,0:T(8,128)(2,1)S(1)}, bf16[80,128]{1,0:T(8,128)(2,1)S(1)}, u32[]{:S(2)}, u32[]{:S(2)}) collective-permute-start(bf16[80,128]{1,0:T(8,128)(2,1)S(1)} %get-tuple-element.26), channel_id=1, source_target_pairs={{0,8},{1,9},{2,10},{3,11},{4,12},{5,13},{6,14},{7,15},{8,0},{9,1},... | collective-permute-start | bytes 61448 | tf_op jit(solution)/shard_map/ppermute | solution.py:343
  59.6 10.5 %collective-permute-start.8 = (bf16[128,128]{1,0:T(8,128)(2,1)S(1)}, bf16[128,128]{1,0:T(8,128)(2,1)S(1)}, u32[]{:S(2)}, u32[]{:S(2)}) collective-permute-start(bf16[128,128]{1,0:T(8,128)(2,1)S(1)} %get-tuple-element.30.left_ref), channel_id=1, source_target_pairs={{0,80},{1,64},{2,96},{3,112},{4,48},{5,16},{6,0},{7,32},{8,176},{9... | collective-permute-start | bytes 98312 | tf_op jit(solution)/shard_map/ppermute | solution.py:343

commit v10 on v9

--- a/solution.py
+++ b/solution.py
@@ -31,9 +31,16 @@
 
 
 def project_kernel(
-    single_hbm, weight_hbm, query_ref, kv_ref, single_ref, weight_ref, sems
+    single_hbm, weight_hbm, pair_hbm, query_ref, kv_ref, pair_ref, single_ref, weight_ref, sems
 ):
-    copies = start_copies(((single_hbm, single_ref), (weight_hbm, weight_ref)), sems)
+    copies = start_copies(
+        (
+            (single_hbm, single_ref),
+            (weight_hbm, weight_ref),
+            (pair_hbm.at[pl.ds(0, pair_ref.shape[0])], pair_ref),
+        ),
+        sems,
+    )
     copies[0].wait()
     normed = normalize(single_ref[...].astype(f32)).astype(bf16)
     copies[1].wait()
@@ -42,6 +49,7 @@
     query_ref[:width] = projected[:width].astype(bf16)
     query_ref[width:] = jax.nn.sigmoid(projected[3 * width :]).astype(bf16)
     kv_ref[...] = projected[width : 3 * width].astype(bf16)
+    copies[2].wait()
 
 
 def normalize_rows(rounded):
@@ -67,11 +75,12 @@
 
 
 def bias_kernel(
+    head_ref,
     pair_hbm,
     weight_hbm,
     mask_hbm,
     out_hbm,
-    pair_ref,
+    tail_ref,
     weight_ref,
     mask_ref,
     held_ref,
@@ -79,26 +88,28 @@
     sems,
     out_sems,
 ):
-    tile_rows, tile_cols, width = pair_ref.shape
+    head_rows, tile_cols, width = head_ref.shape
+    tail_rows = tail_ref.shape[0]
     targets, heads_there = staged_ref.shape[:2]
     pairs = heads_there // 2
-    ends = [tile_rows // 4, tile_rows]
-    parts = [(weight_hbm, weight_ref), (mask_hbm.at[lax.axis_index("cols")], mask_ref)]
-    at = 0
-    for end in ends:
-        rows_here = pl.ds(at, end - at)
-        parts.append((pair_hbm.at[rows_here], pair_ref.at[rows_here]))
-        at = end
-    copies = start_copies(parts, sems)
-    copies[0].wait()
-    copies[1].wait()
-    included = mask_ref[...] > 0
-    at = 0
+    copies = start_copies(
+        (
+            (weight_hbm, weight_ref),
+            (mask_hbm.at[lax.axis_index("cols")], mask_ref),
+            (pair_hbm.at[pl.ds(head_rows, tail_rows)], tail_ref),
+        ),
+        sems,
+    )
     outs = []
-    for chunk, end in enumerate(ends):
-        copies[2 + chunk].wait()
-        step = end - at
-        normed = normalize_rows(pair_ref[at:end].reshape(step * tile_cols, width))
+    for chunk, (pair_ref, at) in enumerate(((head_ref, 0), (tail_ref, head_rows))):
+        step = pair_ref.shape[0]
+        if chunk:
+            copies[2].wait()
+        normed = normalize_rows(pair_ref[...].reshape(step * tile_cols, width))
+        if not chunk:
+            copies[0].wait()
+            copies[1].wait()
+            included = mask_ref[...] > 0
         both = nt_dot(weight_ref[...], normed)
         for i in range(step):
             held_ref[:, i, :] = both[:, i * tile_cols : (i + 1) * tile_cols]
@@ -106,14 +117,15 @@
         for d in range(targets):
             for p in range(heads_there // pairs):
                 first = p * targets * pairs + d * pairs
-                staged_ref[d, p * pairs : (p + 1) * pairs, at:end] = held[first : first + pairs]
+                staged_ref[d, p * pairs : (p + 1) * pairs, at : at + step] = held[
+                    first : first + pairs
+                ]
         rows_here = pl.ds(at, step)
         out = pltpu.make_async_copy(
             staged_ref.at[:, :, rows_here], out_hbm.at[:, :, rows_here], out_sems.at[chunk]
         )
         out.start()
         outs.append(out)
-        at = end
     for out in outs:
         out.wait()
 
@@ -350,21 +362,23 @@
         return target
 
     weight = jnp.transpose(w_project, (0, 2, 1)).reshape(4 * width, single_width)
-    query, kv = pl.pallas_call(
+    head_rows = tile_rows // 4
+    query, kv, pair_head = pl.pallas_call(
         project_kernel,
         out_shape=(
             jax.ShapeDtypeStruct((2 * width, tile_rows), bf16),
             jax.ShapeDtypeStruct((2 * width, tile_rows), bf16),
-        ),
-        in_specs=[in_hbm, in_hbm],
+            jax.ShapeDtypeStruct((head_rows, tile_cols, pair_width), bf16),
+        ),
+        in_specs=[in_hbm, in_hbm, in_hbm],
         scratch_shapes=[
             pltpu.VMEM(single.shape, bf16),
             pltpu.VMEM(weight.shape, bf16),
-            pltpu.SemaphoreType.DMA((2,)),
+            pltpu.SemaphoreType.DMA((3,)),
         ],
         compiler_params=params(),
         name="project",
-    )(pinned(single), pinned(weight))
+    )(pinned(single), pinned(weight), pinned(pair))
 
     kv_first = sent(kv, both_axes, rerouted(0))
     kv_last = sent(kv, both_axes, rerouted(1))
@@ -375,20 +389,25 @@
     bias_local = pl.pallas_call(
         bias_kernel,
         out_shape=jax.ShapeDtypeStruct(sent_shape, bf16),
-        in_specs=[in_hbm, in_hbm, in_hbm],
+        in_specs=[in_vmem, in_hbm, in_hbm, in_hbm],
         out_specs=in_place,
         scratch_shapes=[
-            pltpu.VMEM(pair.shape, bf16),
+            pltpu.VMEM((tile_rows - head_rows, tile_cols, pair_width), bf16),
             pltpu.VMEM((heads, pair_width), bf16),
             pltpu.VMEM((1, tile_cols), jnp.int32),
-            pltpu.VMEM((heads, 3 * tile_rows // 4, tile_cols), f32),
+            pltpu.VMEM((heads, tile_rows - head_rows, tile_cols), f32),
             pltpu.VMEM(sent_shape, bf16),
-            pltpu.SemaphoreType.DMA((4,)),
+            pltpu.SemaphoreType.DMA((3,)),
             pltpu.SemaphoreType.DMA((2,)),
         ],
         compiler_params=params(28),
         name="bias",
-    )(pinned(pair), pinned(jnp.transpose(w_bias)), pinned(residue_mask.reshape(cols, 1, tile_cols)))
+    )(
+        pair_head,
+        pinned(pair),
+        pinned(jnp.transpose(w_bias)),
+        pinned(residue_mask.reshape(cols, 1, tile_cols)),
+    )
     query_other = sent(query, "cols", lambda c: c ^ half_cols)
     bias_local, kv_first, kv_last, query_other = lax.optimization_barrier(
         (bias_local, kv_first, kv_last, query_other)

time: 83.6 us -> 83.9 us (level)
  no operation moved by 1% of the time
where the time goes in v10:
time: 83.9 us; the launch traced here: 83.6 us
  Pallas kernels  25.6 us (31%)
  waiting for transfers between devices  25.5 us (30%)
  starting transfers between devices  18 us (21%)
  blocking collectives  13.7 us (16%)
    ppermute x9, waiting for transfers between devices, sent(): return lax.ppermute(value, axes, routes)  22.4 us
    all_to_all x1, blocking collectives, per_device(): lax.all_to_all(mixed, 'cols', 0, 0, tiled=True)  13.7 us
    pallas_call x1, Pallas kernels, per_device(): pl.pallas_call(update_kernel, grid=(tile_rows // block_rows,), in_specs=[...  13.3 us
    ppermute x9, starting transfers between devices, sent(): return lax.ppermute(value, axes, routes)  13.1 us
    pallas_call x1, Pallas kernels, per_device(): pl.pallas_call(bias_kernel, out_shape=jax.ShapeDtypeStruct(sent_shape, bf...  6.65 us
    all_to_all x1, starting transfers between devices, per_device(): lax.all_to_all(bias_local, 'cols', 0, 0, axis_index_groups=groups, tiled=...  4.89 us
    all_to_all x1, waiting for transfers between devices, per_device(): lax.all_to_all(bias_local, 'cols', 0, 0, axis_index_groups=groups, tiled=...  3.17 us
    pallas_call x1, Pallas kernels, per_device(): pl.pallas_call(attend_kernel, out_shape=(jax.ShapeDtypeStruct((width + 8,...  2.7 us
  transfers between devices with their start and end apart: 10, of which 6 were waited for; matrix products, arithmetic and copies ran while one was open for 0% of the time, Pallas kernels for 8%

profile of v10, /device:TPU:88, one launch (start us, length us, event | category | flops | bytes accessed | tf_op | source)
XLA Modules:
  0.0 83.6 jit_solution(4411444876509157310)
XLA Ops:
  0.6 1.5 %project.1 = (bf16[128,128]{1,0:T(8,128)(2,1)S(1)}, bf16[128,128]{1,0:T(8,128)(2,1)S(1)}, bf16[32,128,128]{2,1,0:T(8,128)(2,1)S(1)}) custom-call(bf16[128,1024]{1,0:T(8,128)(2,1)} %single_hbm.3, bf16[256,1024]{1,0:T(8,128)(2,1)} %bitcast.14, bf16[128,128,128]{2,1,0:T(8,128)(2,1)} %pair_ref.1), custom_call_target="tpu_custom_call" | custom-call | tf_op jit(solution)/shard_map/project/pallas_call | solution.py:366
  2.2 0.1 collective-permute-start.2
  2.3 2.9 %collective-permute-start.1 = (bf16[128,128]{1,0:T(8,128)(2,1)S(1)}, bf16[128,128]{1,0:T(8,128)(2,1)S(1)}, u32[]{:S(2)}, u32[]{:S(2)}) collective-permute-start(bf16[128,128]{1,0:T(8,128)(2,1)S(1)} %get-tuple-element.21), channel_id=1, source_target_pairs={{0,128},{1,129},{2,130},{3,131},{4,132},{5,133},{6,134},{7,135},{8... | collective-permute-start | bytes 98312 | tf_op jit(solution)/shard_map/ppermute | solution.py:355
  5.2 6.4 %collective-permute-start = (bf16[128,128]{1,0:T(8,128)(2,1)S(1)}, bf16[128,128]{1,0:T(8,128)(2,1)S(1)}, u32[]{:S(2)}, u32[]{:S(2)}) collective-permute-start(bf16[128,128]{1,0:T(8,128)(2,1)S(1)} %get-tuple-element.21), channel_id=1, source_target_pairs={{0,0},{1,1},{2,2},{3,3},{4,4},{5,5},{6,6},{7,7},{8,128},{9,129},{1... | collective-permute-start | bytes 98312 | tf_op jit(solution)/shard_map/ppermute | solution.py:355
  11.6 6.6 %bias.1 = bf16[8,4,128,128]{3,2,1,0:T(8,128)(2,1)} custom-call(bf16[32,128,128]{2,1,0:T(8,128)(2,1)S(1)} %get-tuple-element.20.head_ref, bf16[128,128,128]{2,1,0:T(8,128)(2,1)} %pair_ref.1, bf16[32,128]{1,0:T(8,128)(2,1)} %bitcast.20, s32[16,1,128]{2,1,0:T(1,128)} %bitcast.21), custom_call_target="tpu_custom_call" | custom-call | tf_op jit(solution)/shard_map/bias/pallas_call | solution.py:389
  18.2 0.0 copy-start.1
  18.2 0.0 collective-permute-done.2.other_ref
  18.2 0.0 collective-permute-done.1
  18.3 0.0 collective-permute-done
  18.3 4.9 %all-to-all-start = ((bf16[8,4,128,128]{3,2,1,0:T(8,128)(2,1)}), bf16[8,4,128,128]{3,2,1,0:T(8,128)(2,1)S(1)}, u32[]{:S(2)}, u32[]{:S(2)}) async-start(bf16[8,4,128,128]{3,2,1,0:T(8,128)(2,1)} %bias.1), calls=%async_computation | async-start | bytes 2097152 | tf_op jit(solution)/shard_map/all_to_all | solution.py:416
  23.2 1.3 %collective-permute-start.4 = (bf16[2,128,128]{2,1,0:T(8,128)(2,1)S(1)}, bf16[2,128,128]{2,1,0:T(8,128)(2,1)S(1)}, u32[]{:S(2)}, u32[]{:S(2)}) collective-permute-start(bf16[2,128,128]{2,1,0:T(8,128)(2,1)S(1)} %get-tuple-element.37), channel_id=1, source_target_pairs={{0,64},{16,80},{32,96},{48,112},{64,0},{80,16},{96,32},{112,48},{1... | collective-permute-start | bytes 196616 | tf_op jit(solution)/shard_map/ppermute | solution.py:355
  24.5 2.2 %collective-permute-start.3 = (bf16[2,128,128]{2,1,0:T(8,128)(2,1)S(1)}, bf16[2,128,128]{2,1,0:T(8,128)(2,1)S(1)}, u32[]{:S(2)}, u32[]{:S(2)}) collective-permute-start(bf16[2,128,128]{2,1,0:T(8,128)(2,1)S(1)} %get-tuple-element.37), channel_id=1, source_target_pairs={{0,32},{16,48},{32,64},{48,80},{64,96},{80,112},{96,0},{112,16},{1... | collective-permute-start | bytes 196616 | tf_op jit(solution)/shard_map/ppermute | solution.py:355
  26.7 0.0 collective-permute-start.5
  26.7 2.4 %collective-permute-done.4 = bf16[2,128,128]{2,1,0:T(8,128)(2,1)S(1)} collective-permute-done((bf16[2,128,128]{2,1,0:T(8,128)(2,1)S(1)}, bf16[2,128,128]{2,1,0:T(8,128)(2,1)S(1)}, u32[]{:S(2)}, u32[]{:S(2)}) %collective-permute-start.4) | collective-permute-done | bytes 65568 | tf_op jit(solution)/shard_map/ppermute | solution.py:355
  29.1 0.0 collective-permute-done.3
  29.1 3.1 %collective-permute-done.5 = bf16[2,128,128]{2,1,0:T(8,128)(2,1)S(1)} collective-permute-done((bf16[2,128,128]{2,1,0:T(8,128)(2,1)S(1)}, bf16[2,128,128]{2,1,0:T(8,128)(2,1)S(1)}, u32[]{:S(2)}, u32[]{:S(2)}) %collective-permute-start.5) | collective-permute-done | bytes 65568 | tf_op jit(solution)/shard_map/ppermute | solution.py:355
  32.2 0.1 collective-permute-start.6
  32.3 1.7 %collective-permute-done.6.far_hbm = bf16[4,2,128,128]{3,2,1,0:T(8,128)(2,1)} collective-permute-done((bf16[4,2,128,128]{3,2,1,0:T(8,128)(2,1)S(1)}, bf16[4,2,128,128]{3,2,1,0:T(8,128)(2,1)}, u32[]{:S(2)}, u32[]{:S(2)}) %collective-permute-start.6) | collective-permute-done | bytes 262176 | tf_op jit(solution)/shard_map/ppermute | solution.py:355
  33.9 3.2 %all-to-all-done.bias_ref = bf16[8,4,128,128]{3,2,1,0:T(8,128)(2,1)S(1)} async-done(((bf16[8,4,128,128]{3,2,1,0:T(8,128)(2,1)}), bf16[8,4,128,128]{3,2,1,0:T(8,128)(2,1)S(1)}, u32[]{:S(2)}, u32[]{:S(2)}) %all-to-all-start) | async-done | bytes 1048608 | tf_op jit(solution)/shard_map/all_to_all | solution.py:416
  37.1 0.0 copy-start
  37.1 2.7 %attend.1 = (f32[72,128]{1,0:T(8,128)S(1)}, bf16[80,128]{1,0:T(8,128)(2,1)S(1)}, bf16[128,1024]{1,0:T(8,128)(2,1)S(1)}, bf16[1024,128]{1,0:T(8,128)(2,1)S(1)}, b...) custom-call(bf16[128,128]{1,0:T(8,128)(2,1)S(1)} %get-tuple-element.19.own_ref, ...), custom_call_target="tpu_custom_call" | custom-call | tf_op jit(solution)/shard_map/attend/pallas_call | solution.py:426
  39.8 0.1 collective-permute-start.7
  39.9 4.7 %collective-permute-done.7.received_ref = bf16[80,128]{1,0:T(8,128)(2,1)S(1)} collective-permute-done((bf16[80,128]{1,0:T(8,128)(2,1)S(1)}, bf16[80,128]{1,0:T(8,128)(2,1)S(1)}, u32[]{:S(2)}, u32[]{:S(2)}) %collective-permute-start.7) | collective-permute-done | bytes 20512 | tf_op jit(solution)/shard_map/ppermute | solution.py:355
  44.7 13.7 %all_to_all.10 = bf16[16,64,128]{2,1,0:T(8,128)(2,1)S(1)} all-to-all(bf16[16,64,128]{2,1,0:T(8,128)(2,1)S(1)} %join.1), channel_id=1, replica_groups=mesh['rows'=16,'cols'=16] {'cols'}, dimensions={0} | all-to-all | bytes 524288 | tf_op jit(solution)/shard_map/all_to_all | solution.py:464
  58.4 0.0 copy-done.1
  58.4 1.4 %factor.1 = (bf16[128,1024]{1,0:T(8,128)(2,1)}, bf16[128,128]{1,0:T(8,128)(2,1)S(1)}) custom-call(bf16[1024,128]{1,0:T(8,128)(2,1)S(1)} %bitcast.13, bf16[1024,1024]{1,0:T(8,128)(2,1)S(1)} %copy-done.1, bf16[128,1024]{1,0:T(8,128)(2,1)S(1)} %get-tuple-element.29.single_ref, bf16[1024,128]{1,0:T(8,128)(2,1)S(1)} %get-tuple-element.30.w_factors_ref), custom_call_target="tpu_custom_call" | custom-call | tf_op jit(solution)/shard_map/factor/pallas_call | solution.py:466
  59.8 0.0 collective-permute-start.8
  59.8 10.5 %collective-permute-done.8.right_factors_ref = bf16[128,128]{1,0:T(8,128)(2,1)S(1)} collective-permute-done((bf16[128,128]{1,0:T(8,128)(2,1)S(1)}, bf16[128,128]{1,0:T(8,128)(2,1)S(1)}, u32[]{:S(2)}, u32[]{:S(2)}) %collective-permute-start.8) | collective-permute-done | bytes 32800 | tf_op jit(solution)/shard_map/ppermute | solution.py:355
  70.3 0.0 copy-done
  70.3 13.3 %update.1 = bf16[128,128,128]{2,1,0:T(8,128)(2,1)} custom-call(bf16[128,128,128]{2,1,0:T(8,128)(2,1)S(1)} %copy-done, bf16[128,128]{1,0:T(8,128)(2,1)S(1)} %get-tuple-element.32.left_ref, bf16[128,128]{1,0:T(8,128)(2,1)S(1)} %collective-permute-done.8.right_factors_ref, bf16[128,128]{1,0:T(8,128)(2,1)S(1)} %get-tuple-element.33.w_pairout_ref, ...), custom_call_target="tpu_custom_call" | custom-call | tf_op jit(solution)/shard_map/update/pallas_call | solution.py:481
  (3 shorter events, 0.1 us)
Async XLA Ops:
  2.2 16.1 %collective-permute-start.2 = (bf16[128,128]{1,0:T(8,128)(2,1)S(1)}, bf16[128,128]{1,0:T(8,128)(2,1)S(1)}, u32[]{:S(2)}, u32[]{:S(2)}) collective-permute-start(bf16[128,128]{1,0:T(8,128)(2,1)S(1)} %get-tuple-element.19.own_ref), channel_id=1, source_target_pairs={{0,8},{1,9},{2,10},{3,11},{4,12},{5,13},{6,14},{7,15},{8,0},{9,1},... | collective-permute-start | bytes 98312 | tf_op jit(solution)/shard_map/ppermute | solution.py:355
  2.3 16.0 %collective-permute-start.1 = (bf16[128,128]{1,0:T(8,128)(2,1)S(1)}, bf16[128,128]{1,0:T(8,128)(2,1)S(1)}, u32[]{:S(2)}, u32[]{:S(2)}) collective-permute-start(bf16[128,128]{1,0:T(8,128)(2,1)S(1)} %get-tuple-element.21), channel_id=1, source_target_pairs={{0,128},{1,129},{2,130},{3,131},{4,132},{5,133},{6,134},{7,135},{8... | collective-permute-start | bytes 98312 | tf_op jit(solution)/shard_map/ppermute | solution.py:355
  5.2 13.1 %collective-permute-start = (bf16[128,128]{1,0:T(8,128)(2,1)S(1)}, bf16[128,128]{1,0:T(8,128)(2,1)S(1)}, u32[]{:S(2)}, u32[]{:S(2)}) collective-permute-start(bf16[128,128]{1,0:T(8,128)(2,1)S(1)} %get-tuple-element.21), channel_id=1, source_target_pairs={{0,0},{1,1},{2,2},{3,3},{4,4},{5,5},{6,6},{7,7},{8,128},{9,129},{1... | collective-permute-start | bytes 98312 | tf_op jit(solution)/shard_map/ppermute | solution.py:355
  18.2 40.2 %copy-start.1 = (bf16[1024,1024]{1,0:T(8,128)(2,1)S(1)}, bf16[1024,1024]{1,0:T(8,128)(2,1)}, u32[]{:S(2)}) copy-start(bf16[1024,1024]{1,0:T(8,128)(2,1)} %w_out_ref.1) | copy-start | bytes 6291460
  18.3 18.8 %all-to-all-start = ((bf16[8,4,128,128]{3,2,1,0:T(8,128)(2,1)}), bf16[8,4,128,128]{3,2,1,0:T(8,128)(2,1)S(1)}, u32[]{:S(2)}, u32[]{:S(2)}) async-start(bf16[8,4,128,128]{3,2,1,0:T(8,128)(2,1)} %bias.1), calls=%async_computation | async-start | bytes 2097152 | tf_op jit(solution)/shard_map/all_to_all | solution.py:416
  23.2 5.9 %collective-permute-start.4 = (bf16[2,128,128]{2,1,0:T(8,128)(2,1)S(1)}, bf16[2,128,128]{2,1,0:T(8,128)(2,1)S(1)}, u32[]{:S(2)}, u32[]{:S(2)}) collective-permute-start(bf16[2,128,128]{2,1,0:T(8,128)(2,1)S(1)} %get-tuple-element.37), channel_id=1, source_target_pairs={{0,64},{16,80},{32,96},{48,112},{64,0},{80,16},{96,32},{112,48},{1... | collective-permute-start | bytes 196616 | tf_op jit(solution)/shard_map/ppermute | solution.py:355
  24.5 4.6 %collective-permute-start.3 = (bf16[2,128,128]{2,1,0:T(8,128)(2,1)S(1)}, bf16[2,128,128]{2,1,0:T(8,128)(2,1)S(1)}, u32[]{:S(2)}, u32[]{:S(2)}) collective-permute-start(bf16[2,128,128]{2,1,0:T(8,128)(2,1)S(1)} %get-tuple-element.37), channel_id=1, source_target_pairs={{0,32},{16,48},{32,64},{48,80},{64,96},{80,112},{96,0},{112,16},{1... | collective-permute-start | bytes 196616 | tf_op jit(solution)/shard_map/ppermute | solution.py:355
  26.7 5.5 %collective-permute-start.5 = (bf16[2,128,128]{2,1,0:T(8,128)(2,1)S(1)}, bf16[2,128,128]{2,1,0:T(8,128)(2,1)S(1)}, u32[]{:S(2)}, u32[]{:S(2)}) collective-permute-start(bf16[2,128,128]{2,1,0:T(8,128)(2,1)S(1)} %get-tuple-element.37), channel_id=1, source_target_pairs={{0,96},{16,112},{32,0},{48,16},{64,32},{80,48},{96,64},{112,80},{1... | collective-permute-start | bytes 196616 | tf_op jit(solution)/shard_map/ppermute | solution.py:355
  32.2 1.8 %collective-permute-start.6 = (bf16[4,2,128,128]{3,2,1,0:T(8,128)(2,1)S(1)}, bf16[4,2,128,128]{3,2,1,0:T(8,128)(2,1)}, u32[]{:S(2)}, u32[]{:S(2)}) collective-permute-start(bf16[4,2,128,128]{3,2,1,0:T(8,128)(2,1)S(1)} %pad_maximum_fusion.near_ref), channel_id=1, source_target_pairs={{0,16},{16,0},{32,48},{48,32},{64,80},{80,64},{96,112},{112,96},{1... | collective-permute-start | bytes 786440 | tf_op jit(solution)/shard_map/ppermute | solution.py:355
  37.1 33.2 %copy-start = (bf16[128,128,128]{2,1,0:T(8,128)(2,1)S(1)}, bf16[128,128,128]{2,1,0:T(8,128)(2,1)}, u32[]{:S(2)}) copy-start(bf16[128,128,128]{2,1,0:T(8,128)(2,1)} %pair_ref.1) | copy-start | bytes 12582916
  39.8 4.8 %collective-permute-start.7 = (bf16[80,128]{1,0:T(8,128)(2,1)S(1)}, bf16[80,128]{1,0:T(8,128)(2,1)S(1)}, u32[]{:S(2)}, u32[]{:S(2)}) collective-permute-start(bf16[80,128]{1,0:T(8,128)(2,1)S(1)} %get-tuple-element.28), channel_id=1, source_target_pairs={{0,8},{1,9},{2,10},{3,11},{4,12},{5,13},{6,14},{7,15},{8,0},{9,1},... | collective-permute-start | bytes 61448 | tf_op jit(solution)/shard_map/ppermute | solution.py:355
  59.8 10.5 %collective-permute-start.8 = (bf16[128,128]{1,0:T(8,128)(2,1)S(1)}, bf16[128,128]{1,0:T(8,128)(2,1)S(1)}, u32[]{:S(2)}, u32[]{:S(2)}) collective-permute-start(bf16[128,128]{1,0:T(8,128)(2,1)S(1)} %get-tuple-element.32.left_ref), channel_id=1, source_target_pairs={{0,80},{1,64},{2,96},{3,112},{4,48},{5,16},{6,0},{7,32},{8,176},{9... | collective-permute-start | bytes 98312 | tf_op jit(solution)/shard_map/ppermute | solution.py:355

commit v11 on v9

--- a/solution.py
+++ b/solution.py
@@ -122,13 +122,13 @@
     own_ref,
     other_ref,
     bias_ref,
-    near_ref,
-    far_hbm,
+    kv_ref,
     single_hbm,
     w_factors_hbm,
     w_pairout_hbm,
     w_up_hbm,
     w_down_hbm,
+    w_out_hbm,
     kept_ref,
     sent_ref,
     single_ref,
@@ -136,15 +136,15 @@
     w_pairout_ref,
     w_up_ref,
     w_down_ref,
+    w_out_ref,
     score_ref,
-    far_ref,
     sems,
 ):
     copies = start_copies(
         (
-            (far_hbm, far_ref),
             (single_hbm, single_ref),
             (w_factors_hbm, w_factors_ref),
+            (w_out_hbm, w_out_ref),
             (w_pairout_hbm, w_pairout_ref),
             (w_up_hbm, w_up_ref),
             (w_down_hbm, w_down_ref),
@@ -156,19 +156,17 @@
     pairs = heads_there // 2
     head_width = width // pairs
     score_scale = 1.0 / math.sqrt(head_width)
-    shifts = near_ref.shape[0]
+    shifts = kv_ref.shape[1]
     row, col = lax.axis_index("rows"), lax.axis_index("cols")
     half, turn, core = row // (2 * shifts), (row // 2) % shifts, row % 2
     second = col // blocks
 
     def block(b, z, part):
         sent = (turn + shifts - b // 2) % shifts
-        near, far = near_ref[sent, half ^ z, part, :], far_ref[sent, half ^ z, part, :]
-        return jnp.where(core == b % 2, near, far)
+        return kv_ref[(b % 2) ^ core, sent, half ^ z, part, :]
 
     queries = jnp.concatenate([own_ref[:width], other_ref[:width]], axis=0)
     queries = jnp.transpose(queries.astype(f32)).astype(bf16)
-    copies[0].wait()
     lane = lax.broadcasted_iota(jnp.int32, (tile_rows, 128 - width), 1)
     for slot, query_ref in enumerate((own_ref, other_ref)):
         z = second ^ slot
@@ -207,7 +205,7 @@
         out_ref = sent_ref if slot else kept_ref
         out_ref[:width] = (turned[:width] * query_ref[width:].astype(f32)).astype(out_ref.dtype)
         out_ref[width:] = turned[width : out_ref.shape[0]].astype(out_ref.dtype)
-    for copy in copies[1:]:
+    for copy in copies:
         copy.wait()
 
 
@@ -402,9 +400,9 @@
         around = lambda r: (r & half_rows) | ((r + 2 * s) & (half_rows - 1))
         near.append(sent(both, "rows", around))
     near = jnp.stack(near)
-    far = sent(near, "rows", lambda r: r ^ 1)
-
-    kept, partial, single_near, factors_near, pairout_near, up_near, down_near = pl.pallas_call(
+    kv_all = jnp.stack([near, sent(near, "rows", lambda r: r ^ 1)])
+
+    kept, partial, single_near, factors_near, pairout_near, up_near, down_near, out_near = pl.pallas_call(
         attend_kernel,
         out_shape=(
             jax.ShapeDtypeStruct((width + 8, tile_rows), f32),
@@ -414,11 +412,11 @@
             jax.ShapeDtypeStruct(w_pairout.shape, bf16),
             jax.ShapeDtypeStruct(w_up.shape, bf16),
             jax.ShapeDtypeStruct(w_down.shape, bf16),
+            jax.ShapeDtypeStruct(w_out.shape, bf16),
         ),
         in_specs=[in_vmem] * 4 + [in_hbm] * 6,
         scratch_shapes=[
             pltpu.VMEM((half_cols, tile_rows, tile_cols), f32),
-            pltpu.VMEM(near.shape, bf16),
             pltpu.SemaphoreType.DMA((6,)),
         ],
         compiler_params=params(),
@@ -427,13 +425,13 @@
         query,
         query_other,
         bias_heads,
-        near,
-        pinned(far),
+        kv_all,
         pinned(single),
         pinned(w_factors),
         pinned(w_pairout),
         pinned(w_up),
         pinned(w_down),
+        pinned(w_out),
     )
     received = sent(partial, "cols", lambda c: c ^ half_cols)
     mixed = pl.pallas_call(
@@ -452,7 +450,7 @@
         ),
         compiler_params=params(),
         name="factor",
-    )(mixed_all, w_out, single_near, factors_near)
+    )(mixed_all, out_near, single_near, factors_near)
 
     targets = [nearest_rows(row, rows) for row in range(rows)]
     right_factors = sent(factors, both_axes, lambda r, c: (targets[r][c], r))

time: 83.6 us -> 84.1 us (level)
  no operation moved by 1% of the time
where the time goes in v11:
time: 84.1 us; the launch traced here: 83.9 us
  Pallas kernels  26 us (31%)
  waiting for transfers between devices  25.5 us (30%)
  starting transfers between devices  17.8 us (21%)
  blocking collectives  13.7 us (16%)
    ppermute x9, waiting for transfers between devices, sent(): return lax.ppermute(value, axes, routes)  22.2 us
    all_to_all x1, blocking collectives, per_device(): lax.all_to_all(mixed, 'cols', 0, 0, tiled=True)  13.7 us
    pallas_call x1, Pallas kernels, per_device(): pl.pallas_call(update_kernel, grid=(tile_rows // block_rows,), in_specs=[...  13.3 us
    ppermute x9, starting transfers between devices, sent(): return lax.ppermute(value, axes, routes)  13.1 us
    pallas_call x1, Pallas kernels, per_device(): pl.pallas_call(bias_kernel, out_shape=jax.ShapeDtypeStruct(sent_shape, bf...  6.48 us
    all_to_all x1, starting transfers between devices, per_device(): lax.all_to_all(bias_local, 'cols', 0, 0, axis_index_groups=groups, tiled=...  4.77 us
    pallas_call x1, Pallas kernels, per_device(): pl.pallas_call(attend_kernel, out_shape=(jax.ShapeDtypeStruct((width + 8,...  3.28 us
    all_to_all x1, waiting for transfers between devices, per_device(): lax.all_to_all(bias_local, 'cols', 0, 0, axis_index_groups=groups, tiled=...  3.24 us
  transfers between devices with their start and end apart: 10, of which 6 were waited for; matrix products, arithmetic and copies ran while one was open for 0% of the time, Pallas kernels for 8%

profile of v11, /device:TPU:88, one launch (start us, length us, event | category | flops | bytes accessed | tf_op | source)
XLA Modules:
  0.0 83.9 jit_solution(4955439021452991570)
XLA Ops:
  0.6 1.5 %project.1 = (bf16[128,128]{1,0:T(8,128)(2,1)S(1)}, bf16[128,128]{1,0:T(8,128)(2,1)S(1)}) custom-call(bf16[128,1024]{1,0:T(8,128)(2,1)} %single_hbm.3, bf16[256,1024]{1,0:T(8,128)(2,1)} %bitcast.17), custom_call_target="tpu_custom_call" | custom-call | tf_op jit(solution)/shard_map/project/pallas_call | solution.py:351
  2.2 0.1 collective-permute-start.2
  2.3 2.9 %collective-permute-start.1 = (bf16[128,128]{1,0:T(8,128)(2,1)S(1)}, bf16[128,128]{1,0:T(8,128)(2,1)S(1)}, u32[]{:S(2)}, u32[]{:S(2)}) collective-permute-start(bf16[128,128]{1,0:T(8,128)(2,1)S(1)} %get-tuple-element.20), channel_id=1, source_target_pairs={{0,128},{1,129},{2,130},{3,131},{4,132},{5,133},{6,134},{7,135},{8... | collective-permute-start | bytes 98312 | tf_op jit(solution)/shard_map/ppermute | solution.py:341
  5.2 6.4 %collective-permute-start = (bf16[128,128]{1,0:T(8,128)(2,1)S(1)}, bf16[128,128]{1,0:T(8,128)(2,1)S(1)}, u32[]{:S(2)}, u32[]{:S(2)}) collective-permute-start(bf16[128,128]{1,0:T(8,128)(2,1)S(1)} %get-tuple-element.20), channel_id=1, source_target_pairs={{0,0},{1,1},{2,2},{3,3},{4,4},{5,5},{6,6},{7,7},{8,128},{9,129},{1... | collective-permute-start | bytes 98312 | tf_op jit(solution)/shard_map/ppermute | solution.py:341
  11.6 6.5 %bias.1 = bf16[8,4,128,128]{3,2,1,0:T(8,128)(2,1)} custom-call(bf16[128,128,128]{2,1,0:T(8,128)(2,1)} %pair_ref.1, bf16[32,128]{1,0:T(8,128)(2,1)} %bitcast.24, s32[16,1,128]{2,1,0:T(1,128)} %bitcast.25), custom_call_target="tpu_custom_call" | custom-call | tf_op jit(solution)/shard_map/bias/pallas_call | solution.py:373
  18.0 0.0 collective-permute-done.2.other_ref
  18.1 0.0 collective-permute-done.1
  18.1 0.0 collective-permute-done
  18.1 4.8 %all-to-all-start = ((bf16[8,4,128,128]{3,2,1,0:T(8,128)(2,1)}), bf16[8,4,128,128]{3,2,1,0:T(8,128)(2,1)S(1)}, u32[]{:S(2)}, u32[]{:S(2)}) async-start(bf16[8,4,128,128]{3,2,1,0:T(8,128)(2,1)} %bias.1), calls=%async_computation | async-start | bytes 2097152 | tf_op jit(solution)/shard_map/all_to_all | solution.py:395
  22.9 1.3 %collective-permute-start.4 = (bf16[2,128,128]{2,1,0:T(8,128)(2,1)S(1)}, bf16[2,128,128]{2,1,0:T(8,128)(2,1)S(1)}, u32[]{:S(2)}, u32[]{:S(2)}) collective-permute-start(bf16[2,128,128]{2,1,0:T(8,128)(2,1)S(1)} %get-tuple-element.39), channel_id=1, source_target_pairs={{0,64},{16,80},{32,96},{48,112},{64,0},{80,16},{96,32},{112,48},{1... | collective-permute-start | bytes 196616 | tf_op jit(solution)/shard_map/ppermute | solution.py:341
  24.2 2.2 %collective-permute-start.3 = (bf16[2,128,128]{2,1,0:T(8,128)(2,1)S(1)}, bf16[2,128,128]{2,1,0:T(8,128)(2,1)S(1)}, u32[]{:S(2)}, u32[]{:S(2)}) collective-permute-start(bf16[2,128,128]{2,1,0:T(8,128)(2,1)S(1)} %get-tuple-element.39), channel_id=1, source_target_pairs={{0,32},{16,48},{32,64},{48,80},{64,96},{80,112},{96,0},{112,16},{1... | collective-permute-start | bytes 196616 | tf_op jit(solution)/shard_map/ppermute | solution.py:341
  26.4 0.0 collective-permute-start.5
  26.4 2.4 %collective-permute-done.4 = bf16[2,128,128]{2,1,0:T(8,128)(2,1)S(1)} collective-permute-done((bf16[2,128,128]{2,1,0:T(8,128)(2,1)S(1)}, bf16[2,128,128]{2,1,0:T(8,128)(2,1)S(1)}, u32[]{:S(2)}, u32[]{:S(2)}) %collective-permute-start.4) | collective-permute-done | bytes 65568 | tf_op jit(solution)/shard_map/ppermute | solution.py:341
  28.8 0.0 collective-permute-done.3
  28.8 3.1 %collective-permute-done.5 = bf16[2,128,128]{2,1,0:T(8,128)(2,1)S(1)} collective-permute-done((bf16[2,128,128]{2,1,0:T(8,128)(2,1)S(1)}, bf16[2,128,128]{2,1,0:T(8,128)(2,1)S(1)}, u32[]{:S(2)}, u32[]{:S(2)}) %collective-permute-start.5) | collective-permute-done | bytes 65568 | tf_op jit(solution)/shard_map/ppermute | solution.py:341
  31.9 0.1 collective-permute-start.6
  32.0 1.5 %collective-permute-done.6 = bf16[4,2,128,128]{3,2,1,0:T(8,128)(2,1)S(1)} collective-permute-done((bf16[4,2,128,128]{3,2,1,0:T(8,128)(2,1)S(1)}, bf16[4,2,128,128]{3,2,1,0:T(8,128)(2,1)S(1)}, u32[]{:S(2)}, u32[]{:S(2)}) %collective-permute-start.6) | collective-permute-done | bytes 262176 | tf_op jit(solution)/shard_map/ppermute | solution.py:341
  33.5 0.1 pad_maximum_fusion.kv_ref
  33.6 3.2 %all-to-all-done.bias_ref = bf16[8,4,128,128]{3,2,1,0:T(8,128)(2,1)S(1)} async-done(((bf16[8,4,128,128]{3,2,1,0:T(8,128)(2,1)}), bf16[8,4,128,128]{3,2,1,0:T(8,128)(2,1)S(1)}, u32[]{:S(2)}, u32[]{:S(2)}) %all-to-all-start) | async-done | bytes 1048608 | tf_op jit(solution)/shard_map/all_to_all | solution.py:395
  36.8 0.0 copy-start
  36.8 3.3 %attend.1 = (f32[72,128]{1,0:T(8,128)S(1)}, bf16[80,128]{1,0:T(8,128)(2,1)S(1)}, bf16[128,1024]{1,0:T(8,128)(2,1)S(1)}, bf16[1024,128]{1,0:T(8,128)(2,1)S(1)}, b...) custom-call(bf16[128,128]{1,0:T(8,128)(2,1)S(1)} %get-tuple-element., ...), custom_call_target="tpu_custom_call" | custom-call | tf_op jit(solution)/shard_map/attend/pallas_call | solution.py:405
  40.1 0.1 collective-permute-start.7
  40.2 4.7 %collective-permute-done.7.received_ref = bf16[80,128]{1,0:T(8,128)(2,1)S(1)} collective-permute-done((bf16[80,128]{1,0:T(8,128)(2,1)S(1)}, bf16[80,128]{1,0:T(8,128)(2,1)S(1)}, u32[]{:S(2)}, u32[]{:S(2)}) %collective-permute-start.7) | collective-permute-done | bytes 20512 | tf_op jit(solution)/shard_map/ppermute | solution.py:341
  44.9 13.7 %all_to_all.10 = bf16[16,64,128]{2,1,0:T(8,128)(2,1)S(1)} all-to-all(bf16[16,64,128]{2,1,0:T(8,128)(2,1)S(1)} %join.1), channel_id=1, replica_groups=mesh['rows'=16,'cols'=16] {'cols'}, dimensions={0} | all-to-all | bytes 524288 | tf_op jit(solution)/shard_map/all_to_all | solution.py:443
  58.7 1.4 %factor.1 = (bf16[128,1024]{1,0:T(8,128)(2,1)}, bf16[128,128]{1,0:T(8,128)(2,1)S(1)}) custom-call(bf16[1024,128]{1,0:T(8,128)(2,1)S(1)} %bitcast.16, bf16[1024,1024]{1,0:T(8,128)(2,1)S(1)} %get-tuple-element.28.w_out_ref, bf16[128,1024]{1,0:T(8,128)(2,1)S(1)} %get-tuple-element.29.single_ref, bf16[1024,128]{1,0:T(8,128)(2,1)S(1)} %get-tuple-element.30.w_factors_ref), custom_call_target="tpu_custom_call" | custom-call | tf_op jit(solution)/shard_map/factor/pallas_call | solution.py:445
  60.0 0.0 collective-permute-start.8
  60.0 10.5 %collective-permute-done.8.right_factors_ref = bf16[128,128]{1,0:T(8,128)(2,1)S(1)} collective-permute-done((bf16[128,128]{1,0:T(8,128)(2,1)S(1)}, bf16[128,128]{1,0:T(8,128)(2,1)S(1)}, u32[]{:S(2)}, u32[]{:S(2)}) %collective-permute-start.8) | collective-permute-done | bytes 32800 | tf_op jit(solution)/shard_map/ppermute | solution.py:341
  70.6 0.0 copy-done
  70.6 13.3 %update.1 = bf16[128,128,128]{2,1,0:T(8,128)(2,1)} custom-call(bf16[128,128,128]{2,1,0:T(8,128)(2,1)S(1)} %copy-done, bf16[128,128]{1,0:T(8,128)(2,1)S(1)} %get-tuple-element.32.left_ref, bf16[128,128]{1,0:T(8,128)(2,1)S(1)} %collective-permute-done.8.right_factors_ref, bf16[128,128]{1,0:T(8,128)(2,1)S(1)} %get-tuple-element.33.w_pairout_ref, ...), custom_call_target="tpu_custom_call" | custom-call | tf_op jit(solution)/shard_map/update/pallas_call | solution.py:460
  (3 shorter events, 0.1 us)
Async XLA Ops:
  2.2 15.9 %collective-permute-start.2 = (bf16[128,128]{1,0:T(8,128)(2,1)S(1)}, bf16[128,128]{1,0:T(8,128)(2,1)S(1)}, u32[]{:S(2)}, u32[]{:S(2)}) collective-permute-start(bf16[128,128]{1,0:T(8,128)(2,1)S(1)} %get-tuple-element.19.own_ref), channel_id=1, source_target_pairs={{0,8},{1,9},{2,10},{3,11},{4,12},{5,13},{6,14},{7,15},{8,0},{9,1},... | collective-permute-start | bytes 98312 | tf_op jit(solution)/shard_map/ppermute | solution.py:341
  2.3 15.8 %collective-permute-start.1 = (bf16[128,128]{1,0:T(8,128)(2,1)S(1)}, bf16[128,128]{1,0:T(8,128)(2,1)S(1)}, u32[]{:S(2)}, u32[]{:S(2)}) collective-permute-start(bf16[128,128]{1,0:T(8,128)(2,1)S(1)} %get-tuple-element.20), channel_id=1, source_target_pairs={{0,128},{1,129},{2,130},{3,131},{4,132},{5,133},{6,134},{7,135},{8... | collective-permute-start | bytes 98312 | tf_op jit(solution)/shard_map/ppermute | solution.py:341
  5.2 12.9 %collective-permute-start = (bf16[128,128]{1,0:T(8,128)(2,1)S(1)}, bf16[128,128]{1,0:T(8,128)(2,1)S(1)}, u32[]{:S(2)}, u32[]{:S(2)}) collective-permute-start(bf16[128,128]{1,0:T(8,128)(2,1)S(1)} %get-tuple-element.20), channel_id=1, source_target_pairs={{0,0},{1,1},{2,2},{3,3},{4,4},{5,5},{6,6},{7,7},{8,128},{9,129},{1... | collective-permute-start | bytes 98312 | tf_op jit(solution)/shard_map/ppermute | solution.py:341
  18.1 18.7 %all-to-all-start = ((bf16[8,4,128,128]{3,2,1,0:T(8,128)(2,1)}), bf16[8,4,128,128]{3,2,1,0:T(8,128)(2,1)S(1)}, u32[]{:S(2)}, u32[]{:S(2)}) async-start(bf16[8,4,128,128]{3,2,1,0:T(8,128)(2,1)} %bias.1), calls=%async_computation | async-start | bytes 2097152 | tf_op jit(solution)/shard_map/all_to_all | solution.py:395
  22.9 5.9 %collective-permute-start.4 = (bf16[2,128,128]{2,1,0:T(8,128)(2,1)S(1)}, bf16[2,128,128]{2,1,0:T(8,128)(2,1)S(1)}, u32[]{:S(2)}, u32[]{:S(2)}) collective-permute-start(bf16[2,128,128]{2,1,0:T(8,128)(2,1)S(1)} %get-tuple-element.39), channel_id=1, source_target_pairs={{0,64},{16,80},{32,96},{48,112},{64,0},{80,16},{96,32},{112,48},{1... | collective-permute-start | bytes 196616 | tf_op jit(solution)/shard_map/ppermute | solution.py:341
  24.2 4.6 %collective-permute-start.3 = (bf16[2,128,128]{2,1,0:T(8,128)(2,1)S(1)}, bf16[2,128,128]{2,1,0:T(8,128)(2,1)S(1)}, u32[]{:S(2)}, u32[]{:S(2)}) collective-permute-start(bf16[2,128,128]{2,1,0:T(8,128)(2,1)S(1)} %get-tuple-element.39), channel_id=1, source_target_pairs={{0,32},{16,48},{32,64},{48,80},{64,96},{80,112},{96,0},{112,16},{1... | collective-permute-start | bytes 196616 | tf_op jit(solution)/shard_map/ppermute | solution.py:341
  26.4 5.5 %collective-permute-start.5 = (bf16[2,128,128]{2,1,0:T(8,128)(2,1)S(1)}, bf16[2,128,128]{2,1,0:T(8,128)(2,1)S(1)}, u32[]{:S(2)}, u32[]{:S(2)}) collective-permute-start(bf16[2,128,128]{2,1,0:T(8,128)(2,1)S(1)} %get-tuple-element.39), channel_id=1, source_target_pairs={{0,96},{16,112},{32,0},{48,16},{64,32},{80,48},{96,64},{112,80},{1... | collective-permute-start | bytes 196616 | tf_op jit(solution)/shard_map/ppermute | solution.py:341
  31.9 1.6 %collective-permute-start.6 = (bf16[4,2,128,128]{3,2,1,0:T(8,128)(2,1)S(1)}, bf16[4,2,128,128]{3,2,1,0:T(8,128)(2,1)S(1)}, u32[]{:S(2)}, u32[]{:S(2)}) collective-permute-start(bf16[4,2,128,128]{3,2,1,0:T(8,128)(2,1)S(1)} %get-tuple-element.37), channel_id=1, source_target_pairs={{0,16},{16,0},{32,48},{48,32},{64,80},{80,64},{96,112},{112,96},{1... | collective-permute-start | bytes 786440 | tf_op jit(solution)/shard_map/ppermute | solution.py:341
  36.8 33.8 %copy-start = (bf16[128,128,128]{2,1,0:T(8,128)(2,1)S(1)}, bf16[128,128,128]{2,1,0:T(8,128)(2,1)}, u32[]{:S(2)}) copy-start(bf16[128,128,128]{2,1,0:T(8,128)(2,1)} %pair_ref.1) | copy-start | bytes 12582916
  40.1 4.8 %collective-permute-start.7 = (bf16[80,128]{1,0:T(8,128)(2,1)S(1)}, bf16[80,128]{1,0:T(8,128)(2,1)S(1)}, u32[]{:S(2)}, u32[]{:S(2)}) collective-permute-start(bf16[80,128]{1,0:T(8,128)(2,1)S(1)} %get-tuple-element.27), channel_id=1, source_target_pairs={{0,8},{1,9},{2,10},{3,11},{4,12},{5,13},{6,14},{7,15},{8,0},{9,1},... | collective-permute-start | bytes 61448 | tf_op jit(solution)/shard_map/ppermute | solution.py:341
  60.0 10.5 %collective-permute-start.8 = (bf16[128,128]{1,0:T(8,128)(2,1)S(1)}, bf16[128,128]{1,0:T(8,128)(2,1)S(1)}, u32[]{:S(2)}, u32[]{:S(2)}) collective-permute-start(bf16[128,128]{1,0:T(8,128)(2,1)S(1)} %get-tuple-element.32.left_ref), channel_id=1, source_target_pairs={{0,80},{1,64},{2,96},{3,112},{4,48},{5,16},{6,0},{7,32},{8,176},{9... | collective-permute-start | bytes 98312 | tf_op jit(solution)/shard_map/ppermute | solution.py:341
